TPU v7x, 256 devices: a whole 4x4x8 slice. The times are simulated.
256 devices in a mesh: seq: 32 (over x, z_lo, core), dp: 8 (over z_hi, y).
Axes of the slice: x: 4, y: 4, z: 8 (z_hi: 2, z_lo: 4; z = z_hi * 4 + z_lo), core: 2. Of those that a mesh axis runs over, the one named last changes fastest.
Arguments:
- tokens: bfloat16 [8, 16384, 1536], P('dp', 'seq'), may hold values from -6 to 6
- cotangent: bfloat16 [8, 16384, 1536], P('dp', 'seq'), may hold values from -6 to 6
- conv_weight: float32 [3, 1536], replicated, may hold values from -3.5 to 3.5
- gate_weight: bfloat16 [1536, 1536], P('seq'), may hold values from -0.15625 to 0.15625
- leading_block_factor: bfloat16 [128, 128, 128], P('seq'), may hold values from -0.5 to 0.5
- trailing_block_factor: bfloat16 [128, 128, 128], P('seq'), may hold values from -0.5 to 0.5
Outputs:
- mixed: bfloat16 [8, 16384, 1536], P('dp', 'seq')
- grad_tokens: bfloat16 [8, 16384, 1536], P('dp', 'seq')
- grad_conv: float32 [3, 1536], replicated
- grad_gate: float32 [1536, 1536], P('seq')
- grad_first: float32 [128, 128, 128], P('seq')
- trailing_factor_gradient: float32 [128, 128, 128], P('seq')
All inputs are finite; a program needn't handle non-finite values.
Results may differ from a plain program's by a relative error of at most 0.0067.
Values may be sent and summed in bfloat16 or wider, within the bound.
No kernel may reach another device: no remote copies, remote signals or barrier semaphores. Data moves between devices by JAX's collectives and lax.ppermute only.
A program may use at most 128 MiB of HBM per device.

v0:
```python
import functools

import jax
import jax.numpy as jnp
from jax import lax
from jax.experimental import pallas as pl
from jax.experimental.pallas import tpu as pltpu
from jax.sharding import Mesh, PartitionSpec as P

SEQ = ("x", "z_lo", "core")
DP = ("z_hi", "y")
F32 = jnp.float32
BF16 = jnp.bfloat16
ROOM = 48 * 1024 * 1024


def like(shape, dtype=BF16):
    return jax.ShapeDtypeStruct(shape, dtype)


def exchange(values):
    owners = lax.axis_size(SEQ)
    cut = values.reshape(owners, values.shape[0] // owners, values.shape[1])
    return lax.all_to_all(cut, SEQ, split_axis=0, concat_axis=0, tiled=True).reshape(values.shape)


def matmul(left, right, left_dim=1, right_dim=0):
    return lax.dot_general(
        left, right, (((left_dim,), (right_dim,)), ((), ())), preferred_element_type=F32
    )


def position(axis, offset=0):
    count = lax.axis_size(axis)
    return (lax.axis_index(axis) + offset % count) & (count - 1)


def on_device(kernel, operands, outputs, needs=(), scratch=(), step=0, whole=(), kept=()):
    width = max(one.shape[-1] for one in operands)

    def spec(shape, entire=False):
        zeros = (0,) * (len(shape) - 1)
        if step and shape[-1] == width and not entire:
            return pl.BlockSpec((*shape[:-1], step), lambda k: (*zeros, k))
        return pl.BlockSpec(shape, lambda k: (*zeros, 0))

    count = len(operands)

    def body(*refs):
        kernel(*refs[:count], *refs[count + len(needs) :])

    return pl.pallas_call(
        body,
        grid=(width // step if step else 1,),
        in_specs=[spec(one.shape, k in whole) for k, one in enumerate(operands)]
        + [pl.BlockSpec(memory_space=pl.ANY)] * len(needs),
        out_specs=[spec(one.shape) for one in outputs],
        out_shape=[pltpu.HBM(one.shape, one.dtype) if k in kept else one for k, one in enumerate(outputs)],
        scratch_shapes=scratch,
        cost_estimate=pl.CostEstimate(flops=1000, transcendentals=0, bytes_accessed=1000),
        compiler_params=pltpu.CompilerParams(vmem_limit_bytes=ROOM),
    )(*operands, *needs)


def setup_kernel(lead_in, trail_in, lead_ref, lead_back, trail_ref, trail_back, to_position, to_group, *, owners):
    blocks, size, _ = lead_in.shape
    per = size // owners
    rows = blocks * size
    line = lax.broadcasted_iota(jnp.int32, (rows, rows), 0)
    column = lax.broadcasted_iota(jnp.int32, (rows, rows), 1)
    owner, rest = lax.div(column, per * blocks), lax.rem(column, per * blocks)
    inner, block = lax.div(rest, blocks), lax.rem(rest, blocks)
    by_position = (line == (block * owners + owner) * per + inner).astype(F32).astype(BF16)
    by_group = (line == (inner * owners + owner) * blocks + block).astype(F32).astype(BF16)
    to_position[...] = by_position
    to_group[...] = by_group
    same = lax.div(line, size) == lax.div(column, size)

    def diagonal(ref):
        tall = ref[...].reshape(rows, size).astype(F32)
        return jnp.where(same, jnp.concatenate([tall] * blocks, axis=1), 0.0).astype(BF16)

    lead = diagonal(lead_in)
    trail = diagonal(trail_in)
    lead_ref[...] = matmul(by_position, lead, 0, 0).astype(BF16)
    lead_back[...] = matmul(lead, by_position, 0, 0).astype(BF16)
    trail_ref[...] = matmul(by_group, matmul(trail, by_group).astype(BF16), 0, 0).astype(BF16)
    trail_back[...] = matmul(by_group, matmul(trail, by_group, 0, 0).astype(BF16), 0, 0).astype(BF16)


def with_neighbours(values, before, after_row):
    count = values.shape[0]
    line = lax.broadcasted_iota(jnp.int32, values.shape, 0)
    previous = jnp.where(line == 0, before, pltpu.roll(values, 1, 0))
    following = jnp.where(line == count - 1, after_row, pltpu.roll(values, count - 1, 0))
    return previous, following


def forward_kernel(tok_ref, before_ref, after_ref, taps_ref, lead_ref, conv_ref, send_ref):
    values = tok_ref[...].astype(F32)
    previous, following = with_neighbours(values, before_ref[...].astype(F32), after_ref[...].astype(F32))
    taps = taps_ref[...]
    conv_in = (taps[0:1] * previous + taps[1:2] * values + taps[2:3] * following).astype(BF16)
    conv_ref[...] = conv_in
    send_ref[...] = matmul(lead_ref[...], conv_in).astype(BF16)


def mix_kernel(mix_ref, values_ref, out_ref):
    out_ref[...] = matmul(mix_ref[...], values_ref[...]).astype(BF16)


def half_kernel(own_ref, before_ref, after_ref, low_ref, high_ref, out_ref):
    out_ref[position("x")] = own_ref[...]
    out_ref[position("x", -1)] = before_ref[...]
    out_ref[position("x", 1)] = after_ref[...]
    part = low_ref.shape[0]
    out_ref[position("x", 2), :part] = low_ref[...]
    out_ref[position("x", 2), part:] = high_ref[...]


def project_kernel(tok_ref, mine_ref, other_ref, cotangent_ref, order_ref, weight_ref, gate_ref, send_ref):
    core = lax.axis_index("core")
    weight_ref[:, core] = mine_ref[...]
    weight_ref[:, 1 - core] = other_ref[...]
    gate = matmul(tok_ref[...], weight_ref[...].reshape(tok_ref.shape[1], gate_ref.shape[1]))
    gate_ref[...] = gate
    d_monarch = (cotangent_ref[...].astype(F32) * gate).astype(BF16)
    send_ref[...] = matmul(order_ref[...], d_monarch, 0, 0).astype(BF16)


def project_back(d_gate, weight, step=512):
    rows, width = d_gate.shape

    def body(left_ref, right_ref, out_ref):
        out_ref[...] = matmul(left_ref[...], right_ref[...], 1, 1)

    return pl.pallas_call(
        body,
        grid=(width // step,),
        in_specs=[
            pl.BlockSpec((rows, width), lambda k: (0, 0)),
            pl.BlockSpec((step, width), lambda k: (k, 0)),
        ],
        out_specs=pl.BlockSpec((rows, step), lambda k: (0, k)),
        out_shape=like((rows, width), F32),
        cost_estimate=pl.CostEstimate(flops=1000, transcendentals=0, bytes_accessed=1000),
        compiler_params=pltpu.CompilerParams(vmem_limit_bytes=ROOM),
    )(d_gate, weight)


def gate_kernel(order_ref, second_ref, gate_ref, cotangent_ref, mixed_ref, d_gate_ref):
    monarch = matmul(order_ref[...], second_ref[...])
    mixed_ref[...] = (monarch * gate_ref[...]).astype(BF16)
    d_gate_ref[...] = (cotangent_ref[...].astype(F32) * monarch).astype(BF16)


def weight_kernel(tok_ref, d_gate_ref, mine_ref, other_ref, whole, *, owners):
    core = lax.axis_index("core")
    rows = whole.shape[0] // owners
    whole[...] = matmul(tok_ref[...], d_gate_ref[...], 0, 0)
    for k in range(owners // 2):
        near = pl.multiple_of((2 * k + core) * rows, rows)
        far = pl.multiple_of((2 * k + 1 - core) * rows, rows)
        mine_ref[k * rows : (k + 1) * rows, :] = whole[pl.ds(near, rows), :].astype(BF16)
        other_ref[k * rows : (k + 1) * rows, :] = whole[pl.ds(far, rows), :].astype(BF16)


def backward_kernel(
    mix_ref, delta_ref, tok_ref, before_ref, after_ref, out_ref, first_ref, last_ref, sums_ref
):
    d_conv = matmul(mix_ref[...], delta_ref[...]).astype(BF16)
    out_ref[...] = d_conv
    first_ref[...] = d_conv[:1]
    last_ref[...] = d_conv[-1:]
    d_wide = d_conv.astype(F32)
    values = tok_ref[...].astype(F32)
    previous, following = with_neighbours(values, before_ref[...].astype(F32), after_ref[...].astype(F32))
    sums = [jnp.sum(d_wide * one, axis=0, keepdims=True) for one in (previous, values, following)]
    sums = jnp.concatenate(sums, axis=0).astype(BF16)
    sums_ref[...] = jnp.broadcast_to(sums[None], sums_ref.shape)


def add_pairs(left, right, sums):
    @pl.when(pl.program_id(0) == 0)
    def _():
        sums[...] = jnp.zeros(sums.shape, F32)

    size = sums.shape[1]
    for k in range(sums.shape[0]):
        block = slice(k * size, (k + 1) * size)
        sums[k] += matmul(left[block], right[block], 1, 1)


def second_kernel(order_ref, delta_ref, columns_ref, out_ref, sums):
    order = order_ref[...]
    left = matmul(order, delta_ref[...]).astype(BF16)
    right = matmul(order, columns_ref[...]).astype(BF16)
    add_pairs(left, right, sums)

    @pl.when(pl.program_id(0) == pl.num_programs(0) - 1)
    def _():
        out_ref[...] = sums[...].astype(BF16)


def first_kernel(order_ref, d_first_ref, conv_ref, second_ref, *refs):
    outs, sums = refs[:-1], refs[-1]
    add_pairs(matmul(order_ref[...], d_first_ref[...]).astype(BF16), conv_ref[...], sums)

    @pl.when(pl.program_id(0) == pl.num_programs(0) - 1)
    def _():
        size = sums.shape[1]
        for k, one in enumerate(outs):
            block = position("y", k)
            one[:size, :] = sums[block].astype(BF16)
            one[size:, :] = second_ref[block]


def total(refs):
    value = refs[0][...].astype(F32)
    for one in refs[1:]:
        value = value + one[...].astype(F32)
    return value


def lanes(values, size):
    count = values.shape[1] // size
    return jnp.concatenate([values[:, k * size : (k + 1) * size] for k in range(count)], axis=0)


def pack_kernel(*refs, z_count):
    gate, factors = refs[:z_count], refs[z_count:-2]
    spread_ref, out_ref = refs[-2:]
    size = out_ref.shape[1]
    taps = jnp.sum(spread_ref[...].astype(F32), axis=0)
    taps = jnp.concatenate([taps, jnp.zeros((8 - taps.shape[0], taps.shape[1]), F32)], axis=0)
    line = 0
    for one in (lanes(total(gate), size), total(factors), lanes(taps, size)):
        out_ref[line : line + one.shape[0], :] = one.astype(BF16)
        line += one.shape[0]


def finish_kernel(pieces, gate_ref, second_ref, first_ref, taps_ref):
    count = pieces.shape[0]
    size = second_ref.shape[1]
    own, width = gate_ref.shape
    share = width // count
    rows = second_ref.shape[0] // count
    gate_rows = own * share // size
    tap_rows = gate_rows + 2 * rows
    taps = None
    for k in range(count):
        for j in range(share // size):
            columns = slice(k * share + j * size, k * share + (j + 1) * size)
            gate_ref[:, columns] = pieces[k, j * own : (j + 1) * own, :].astype(F32)
        block = slice(k * rows, (k + 1) * rows)
        first_ref[block, :] = pieces[k, gate_rows : gate_rows + rows, :].astype(F32)
        second_ref[block, :] = pieces[k, gate_rows + rows : tap_rows, :].astype(F32)
        part = pieces[k, tap_rows:, :].astype(F32)
        taps = part if taps is None else taps + part
    for j in range(width // size):
        taps_ref[:, j * size : (j + 1) * size] = taps[j * 8 : j * 8 + taps_ref.shape[0], :]


def shift(values, axis, step):
    count = lax.axis_size(axis)
    return lax.ppermute(values, axis, [(i, (i + step) % count) for i in range(count)])


def spread_over(values, axis):
    copies = jnp.broadcast_to(values[None], (lax.axis_size(axis), *values.shape))
    return lax.all_to_all(copies, axis, split_axis=0, concat_axis=0, tiled=True)


def swap(values, axis):
    return lax.ppermute(values, axis, [(0, 1), (1, 0)])


def halo_rows(first, last):
    count = lax.axis_size(SEQ)
    up = [(i, i + 1) for i in range(count - 1)]
    down = [(i + 1, i) for i in range(count - 1)]
    before = lax.ppermute(last, SEQ, up)
    after = lax.ppermute(first, SEQ, down)
    return before, after


def shift_down(values, before):
    return jnp.concatenate([before, values[:-1]], axis=0)


def shift_up(values, after):
    return jnp.concatenate([values[1:], after], axis=0)


def piece(values, index, count, dim):
    sizes = list(values.shape)
    sizes[dim] = sizes[dim] // count
    starts = [jnp.uint32(0)] * values.ndim
    starts[dim] = index.astype(jnp.uint32) * jnp.uint32(sizes[dim])
    return lax.dynamic_slice(values, starts, sizes)


def cut(values, axis, dim):
    count = lax.axis_size(axis)
    return [piece(values, position(axis, k), count, dim).astype(BF16) for k in range(count)]


def send_pieces(pieces, axis):
    count = len(pieces)
    return [pieces[0]] + [
        shift(pieces[k], axis, k) for k in range(1, count)
    ]


def add_up(pieces):
    value, *others = [one.astype(F32) for one in pieces]
    for one in others:
        value = value + one
    return value


def shards(tokens, cotangent, conv_weight, gate_weight, leading, trailing):
    features = tokens[0]
    grad_out = cotangent[0]
    rows, width = features.shape
    blocks, size, _ = leading.shape
    owners = lax.axis_size(SEQ)
    per = size // owners
    wide = like((rows, width))
    square = like((rows, rows))
    own = gate_weight.shape[0]
    x_count, z_count, y_count = lax.axis_size("x"), lax.axis_size("z_lo"), lax.axis_size("y")

    tok_before, tok_after = halo_rows(features[:1], features[-1:])
    near = spread_over(gate_weight, "z_lo")
    lead, lead_back, trail, trail_back, to_position, to_group = on_device(
        functools.partial(setup_kernel, owners=owners), [leading, trailing], [square] * 6, kept=range(1, 6)
    )
    conv_in, send = on_device(
        forward_kernel,
        [features, tok_before, tok_after, conv_weight, lead],
        [wide, wide],
        needs=[near],
        step=512,
    )
    columns = exchange(send)
    before, after = shift(near, "x", 1), shift(near, "x", -1)
    low, high = shift(before[: z_count // 2], "x", 1), shift(after[z_count // 2 :], "x", -1)
    (near,) = on_device(
        half_kernel, [near, before, after, low, high], [like((x_count, *near.shape))]
    )
    far = swap(near, "core")
    (send,) = on_device(mix_kernel, [trail, columns], [wide], needs=[near], step=512)
    second_out = exchange(send)

    near, far = [one.reshape(x_count * z_count, own, width) for one in (near, far)]
    whole_gate, gate_act, send = on_device(
        project_kernel,
        [features, near, far, grad_out, to_position],
        [like((x_count * z_count, 2, own, width)), like((rows, width), F32), wide],
        needs=[send],
        step=512,
        whole=[0],
    )
    whole_gate = whole_gate.reshape(width, width)
    send, second_out = lax.optimization_barrier((send, second_out))
    delta = exchange(send)

    mixed, d_gate = on_device(
        gate_kernel, [to_position, second_out, gate_act, grad_out], [wide, wide], step=512
    )
    mine, other = on_device(
        functools.partial(weight_kernel, owners=owners),
        [features, d_gate],
        [like((width // 2, width))] * 2,
        scratch=[pltpu.VMEM((width, width), F32)],
    )
    other = swap(other, "core")
    gate_back = project_back(d_gate, whole_gate)
    pieces = [
        (
            piece(mine, position("y", k), y_count, 1).astype(F32)
            + piece(other, position("y", k), y_count, 1).astype(F32)
        ).astype(BF16)
        for k in range(y_count)
    ]
    delta, *pieces = lax.optimization_barrier((delta, *pieces))
    (send,) = on_device(mix_kernel, [trail_back, delta], [wide], needs=[gate_back], step=512)
    d_first = exchange(send)
    (grad_second,) = on_device(
        second_kernel,
        [to_group, delta, columns],
        [like((per, size, size))],
        scratch=[pltpu.VMEM((per, size, size), F32)],
        needs=[send],
        step=512,
    )
    arrived = send_pieces(pieces, "y")
    grad_second, *arrived = lax.optimization_barrier((grad_second, *arrived))
    pieces = send_pieces(cut(add_up(arrived), "x", 0), "x")

    edge = like((1, width))
    d_conv, *d_edge, spread = on_device(
        backward_kernel,
        [lead_back, d_first, features, tok_before, tok_after],
        [wide, edge, edge, like((owners, *conv_weight.shape))],
        needs=[grad_second],
        step=512,
    )
    spread = lax.all_to_all(spread, SEQ, split_axis=0, concat_axis=0, tiled=True)
    *factors, = on_device(
        first_kernel,
        [to_position, d_first, conv_in, grad_second],
        [like((2 * size, size))] * y_count,
        scratch=[pltpu.VMEM((blocks, size, size), F32)],
        needs=[d_conv],
        step=512,
    )
    factors[0], *pieces = lax.optimization_barrier((factors[0], *pieces))
    grad_before, grad_after = halo_rows(*d_edge)
    parts = [
        *send_pieces(cut(add_up(pieces), "z_lo", 0), "z_lo"),
        *send_pieces(factors, "y"),
    ]
    d_next = shift_up(d_conv, grad_after).astype(F32)
    d_prev = shift_down(d_conv, grad_before).astype(F32)
    conv_back = conv_weight[0] * d_next + conv_weight[1] * d_conv.astype(F32) + conv_weight[2] * d_prev
    grad_tokens = (conv_back + gate_back).astype(BF16)

    lines = (own * width // y_count) // size + 2 * size + 8 * (width // size)
    (packed,) = on_device(
        functools.partial(pack_kernel, z_count=z_count), [*parts, spread], [like((lines, size))]
    )
    packed = (packed.astype(F32) + swap(packed, "z_hi").astype(F32)).astype(BF16)
    grad_gate, grad_second, grad_first, grad_conv = on_device(
        finish_kernel,
        [spread_over(packed, "y")],
        [
            like((own, width), F32),
            like((rows, size), F32),
            like((rows, size), F32),
            like(conv_weight.shape, F32),
        ],
    )
    return (
        mixed[None],
        grad_tokens[None],
        grad_conv,
        grad_gate,
        grad_first.reshape(leading.shape),
        grad_second.reshape(trailing.shape),
    )


def solution(mesh):
    fine = Mesh(mesh.devices.reshape(4, 4, 2, 2, 4), ("x", "z_lo", "core", "z_hi", "y"))
    return jax.shard_map(
        shards,
        mesh=fine,
        in_specs=(
            P(DP, SEQ, None),
            P(DP, SEQ, None),
            P(),
            P(SEQ, None),
            P(SEQ, None, None),
            P(SEQ, None, None),
        ),
        out_specs=(
            P(DP, SEQ, None),
            P(DP, SEQ, None),
            P(),
            P(SEQ, None),
            P(SEQ, None, None),
            P(SEQ, None, None),
        ),
        check_vma=False,
    )
```

profile of v0, /device:TPU:6, one launch (start us, length us, event | category | flops | bytes accessed | tf_op | source)
XLA Modules:
  0.0 286.2 jit_solution(4197387825895018101)
XLA Ops:
  0.7 1.9 broadcast_in_dim.8
  2.6 5.9 %all-to-all-start = ((bf16[4,48,1536]{2,1,0:T(8,128)(2,1)}), bf16[4,48,1536]{2,1,0:T(8,128)(2,1)S(1)}, u32[]{:S(2)}, u32[]{:S(2)}) async-start(bf16[4,48,1536]{2,1,0:T(8,128)(2,1)} %broadcast_in_dim.8), calls=%async_computation | async-start | bytes 1179648 | tf_op jit(solution)/shard_map/all_to_all | solution.py:271
  8.5 1.9 collective-permute-start.5
  10.4 6.3 %collective-permute-start.6 = (bf16[1,1536]{1,0:T(2,128)(2,1)S(1)}, bf16[1,1536]{1,0:T(2,128)(2,1)S(1)}, u32[]{:S(2)}, u32[]{:S(2)}) collective-permute-start(bf16[1,1536]{1,0:T(2,128)(2,1)S(1)} %get-tuple-element.103), channel_id=1, source_target_pairs={{8,0},{16,8},{24,16},{32,24},{40,32},{48,40},{56,48},{64,56},{72,6... | collective-permute-start | bytes 9224 | tf_op jit(solution)/shard_map/ppermute | solution.py:283
  16.8 2.8 shard_map.109
  21.1 3.2 %all-to-all-done.refs_0_.refs_5_ = bf16[4,48,1536]{2,1,0:T(8,128)(2,1)S(1)} async-done(((bf16[4,48,1536]{2,1,0:T(8,128)(2,1)}), bf16[4,48,1536]{2,1,0:T(8,128)(2,1)S(1)}, u32[]{:S(2)}, u32[]{:S(2)}) %all-to-all-start) | async-done | bytes 589856 | tf_op jit(solution)/shard_map/all_to_all | solution.py:271
  24.4 2.4 shard_map.111
  29.0 6.0 %all-to-all-start.1 = ((bf16[32,16,1536]{2,1,0:T(8,128)(2,1)}), bf16[32,16,1536]{2,1,0:T(8,128)(2,1)S(1)}, u32[]{:S(2)}, u32[]{:S(2)}) async-start(bf16[32,16,1536]{2,1,0:T(8,128)(2,1)} %bitcast.37), calls=%async_computation.1 | async-start | bytes 3145728 | tf_op jit(solution)/shard_map/all_to_all | solution.py:24
  35.3 1.8 collective-permute-start.1
  37.2 26.9 %collective-permute-done.refs_1_ = bf16[4,48,1536]{2,1,0:T(8,128)(2,1)S(1)} collective-permute-done((bf16[4,48,1536]{2,1,0:T(8,128)(2,1)}, bf16[4,48,1536]{2,1,0:T(8,128)(2,1)S(1)}, u32[]{:S(2)}, u32[]{:S(2)}) %collective-permute-start) | collective-permute-done | bytes 589856 | tf_op jit(solution)/shard_map/ppermute | solution.py:266
  64.1 2.5 collective-permute-start.2
  66.7 7.6 %collective-permute-done.2.refs_3_ = bf16[2,48,1536]{2,1,0:T(8,128)(2,1)S(1)} collective-permute-done((bf16[2,48,1536]{2,1,0:T(8,128)(2,1)S(1)}, bf16[2,48,1536]{2,1,0:T(8,128)(2,1)S(1)}, u32[]{:S(2)}, u32[]{:S(2)}) %collective-permute-start.2) | collective-permute-done | bytes 294944 | tf_op jit(solution)/shard_map/ppermute | solution.py:266
  74.3 2.8 collective-permute-done.3.refs_4_
  78.8 2.2 copy-done.5
  82.0 2.5 shard_map.112.refs_5_
  84.6 8.0 %all-to-all-start.2 = ((bf16[32,16,1536]{2,1,0:T(8,128)(2,1)}), bf16[32,16,1536]{2,1,0:T(8,128)(2,1)}, u32[]{:S(2)}, u32[]{:S(2)}) async-start(bf16[32,16,1536]{2,1,0:T(8,128)(2,1)} %bitcast.8), calls=%async_computation.2 | async-start | bytes 3145728 | tf_op jit(solution)/shard_map/all_to_all | solution.py:24
  92.9 4.6 %collective-permute-done.4 = bf16[4,4,48,1536]{3,2,1,0:T(8,128)(2,1)S(1)} collective-permute-done((bf16[4,4,48,1536]{3,2,1,0:T(8,128)(2,1)}, bf16[4,4,48,1536]{3,2,1,0:T(8,128)(2,1)S(1)}, u32[]{:S(2)}, u32[]{:S(2)}) %collective-permute-start.4) | collective-permute-done | bytes 2359328 | tf_op jit(solution)/shard_map/ppermute | solution.py:275
  100.0 6.7 %shard_map.113 = (bf16[16,2,48,1536]{3,2,1,0:T(8,128)(2,1)}, f32[512,1536]{1,0:T(8,128)}, bf16[512,1536]{1,0:T(8,128)(2,1)S(1)}) custom-call(bf16[512,1536]{1,0:T(8,128)(2,1)S(1)} %bitcast.23, bf16[16,48,1536]{2,1,0:T(8,128)(2,1)} %bitcast.26, bf16[16,48,1536]{2,1,0:T(8,128)(2,1)} %bitcast.39, bf16[512,1536]{1,0:T(8,128)(2,1)S(1)} %bitcast.34, ...), custom_call_target="tpu_custom_call" | custom-call | flops 1000 | bytes 1000 | tf_op jit(solution)/shard_map/pallas_call | solution.py:52
  107.9 21.7 %all-to-all-done.2 = bf16[32,16,1536]{2,1,0:T(8,128)(2,1)} async-done(((bf16[32,16,1536]{2,1,0:T(8,128)(2,1)}), bf16[32,16,1536]{2,1,0:T(8,128)(2,1)}, u32[]{:S(2)}, u32[]{:S(2)}) %all-to-all-start.2) | async-done | bytes 1572896 | tf_op jit(solution)/shard_map/all_to_all | solution.py:24
  129.6 6.2 %all-to-all-start.3 = ((bf16[32,16,1536]{2,1,0:T(8,128)(2,1)}), bf16[32,16,1536]{2,1,0:T(8,128)(2,1)S(1)}, u32[]{:S(2)}, u32[]{:S(2)}) async-start(bf16[32,16,1536]{2,1,0:T(8,128)(2,1)} %bitcast.36), calls=%async_computation.3 | async-start | bytes 3145728 | tf_op jit(solution)/shard_map/all_to_all | solution.py:24
  138.3 4.8 %shard_map.114 = (bf16[512,1536]{1,0:T(8,128)(2,1)}, bf16[512,1536]{1,0:T(8,128)(2,1)S(1)}) custom-call(bf16[512,512]{1,0:T(8,128)(2,1)S(1)} %copy-done.22, bf16[512,1536]{1,0:T(8,128)(2,1)} %bitcast.9.refs_1_, f32[512,1536]{1,0:T(8,128)} %get-tuple-element.56.refs_2_, bf16[512,1536]{1,0:T(8,128)(2,1)S(1)} %bitcast.35), custom_call_target="tpu_custom_call" | custom-call | flops 1000 | bytes 1000 | tf_op jit(solution)/shard_map/pallas_call | solution.py:52
  143.2 5.0 %shard_map.115 = (bf16[768,1536]{1,0:T(8,128)(2,1)S(1)}, bf16[768,1536]{1,0:T(8,128)(2,1)}) custom-call(bf16[512,1536]{1,0:T(8,128)(2,1)S(1)} %bitcast.24, bf16[512,1536]{1,0:T(8,128)(2,1)S(1)} %get-tuple-element.61.refs_1_.left_ref), custom_call_target="tpu_custom_call" | custom-call | flops 1000 | bytes 1000 | tf_op jit(solution)/shard_map/pallas_call | solution.py:52
  151.4 5.1 %shard_map.116.refs_2_ = f32[512,1536]{1,0:T(8,128)S(1)} custom-call(bf16[512,1536]{1,0:T(8,128)(2,1)S(1)} %copy-done.16, bf16[1536,1536]{1,0:T(8,128)(2,1)} %bitcast.38), custom_call_target="tpu_custom_call" | custom-call | flops 1000 | bytes 1000 | tf_op jit(solution)/shard_map/pallas_call | solution.py:137
  156.5 1.6 copy-done
  158.2 3.5 %add_convert_fusion.1 = (bf16[768,384]{1,0:T(8,128)(2,1)}, bf16[768,384]{1,0:T(8,128)(2,1)}, bf16[768,384]{1,0:T(8,128)(2,1)}, bf16[768,384]{1,0:T(8,128)(2,1)}) fusion(bf16[768,1536]{1,0:T(8,128)(2,1)} %collective-permute-done.7, u32[]{:T(128)S(6)} %mul.75, bf16[768,1536]{1,0:T(8,128)(2,1)S(1)} %copy-done.25, u32[]{:T(128)S(6)} %mul.74, u32[]{:T(128)S(6)} %mul.73, ...), kind=kLoop, calls=%fused_computation.3 | loop fusion | flops 4718592 | bytes 7077904 | tf_op jit(solution)/shard_map/convert_element_type | solution.py:384
  161.6 11.2 %all-to-all-done.3 = bf16[32,16,1536]{2,1,0:T(8,128)(2,1)S(1)} async-done(((bf16[32,16,1536]{2,1,0:T(8,128)(2,1)}), bf16[32,16,1536]{2,1,0:T(8,128)(2,1)S(1)}, u32[]{:S(2)}, u32[]{:S(2)}) %all-to-all-start.3) | async-done | bytes 1572896 | tf_op jit(solution)/shard_map/all_to_all | solution.py:24
  176.9 6.2 %all-to-all-start.4 = ((bf16[32,16,1536]{2,1,0:T(8,128)(2,1)}), bf16[32,16,1536]{2,1,0:T(8,128)(2,1)S(1)}, u32[]{:S(2)}, u32[]{:S(2)}) async-start(bf16[32,16,1536]{2,1,0:T(8,128)(2,1)} %bitcast.33), calls=%async_computation.4 | async-start | bytes 3145728 | tf_op jit(solution)/shard_map/all_to_all | solution.py:24
  183.1 1.7 collective-permute-start.8
  184.8 2.9 %collective-permute-start.9 = (bf16[768,384]{1,0:T(8,128)(2,1)}, bf16[768,384]{1,0:T(8,128)(2,1)}, u32[]{:S(2)}, u32[]{:S(2)}) collective-permute-start(bf16[768,384]{1,0:T(8,128)(2,1)} %get-tuple-element.69), channel_id=1, source_target_pairs={{0,2},{1,3},{2,0},{3,1},{4,6},{5,7},{6,4},{7,5},{8,10},{9,11},{10,... | collective-permute-start | bytes 1769480 | tf_op jit(solution)/shard_map/ppermute | solution.py:266
  194.3 3.3 %shard_map.118.refs_5_.refs_3_ = bf16[4,128,128]{2,1,0:T(8,128)(2,1)S(1)} custom-call(bf16[512,512]{1,0:T(8,128)(2,1)S(1)} %copy-done.32, bf16[512,1536]{1,0:T(8,128)(2,1)S(1)} %bitcast.32, bf16[512,1536]{1,0:T(8,128)(2,1)S(1)} %bitcast.30, bf16[512,1536]{1,0:T(8,128)(2,1)S(1)} %copy-done.14), custom_call_target="tpu_custom_call" | custom-call | flops 1000 | bytes 1000 | tf_op jit(solution)/shard_map/pallas_call | solution.py:52
  197.6 2.5 collective-permute-done.8
  200.2 13.8 %collective-permute-done.9 = bf16[768,384]{1,0:T(8,128)(2,1)} collective-permute-done((bf16[768,384]{1,0:T(8,128)(2,1)}, bf16[768,384]{1,0:T(8,128)(2,1)}, u32[]{:S(2)}, u32[]{:S(2)}) %collective-permute-start.9) | collective-permute-done | bytes 589856 | tf_op jit(solution)/shard_map/ppermute | solution.py:266
  214.0 1.7 convert_add_fusion
  216.7 2.7 collective-permute-start.14
  223.7 2.7 shard_map.119
  227.2 7.3 %all-to-all-start.5 = ((bf16[32,3,1536]{2,1,0:T(4,128)(2,1)}), bf16[32,3,1536]{2,1,0:T(4,128)(2,1)S(1)}, u32[]{:S(2)}, u32[]{:S(2)}) async-start(bf16[32,3,1536]{2,1,0:T(4,128)(2,1)} %copy-done.34), calls=%async_computation.5 | async-start | bytes 786432 | tf_op jit(solution)/shard_map/all_to_all | solution.py:410
  238.3 2.6 shard_map.120
  243.7 2.4 collective-permute-start.17
  248.8 2.4 collective-permute-start.20
  251.2 1.6 collective-permute-start.21
  255.7 5.1 %collective-permute-start.22 = (bf16[496,128]{1,0:T(8,128)(2,1)S(1)}, bf16[496,128]{1,0:T(8,128)(2,1)S(1)}, u32[]{:S(2)}, u32[]{:S(2)}) collective-permute-start(bf16[496,128]{1,0:T(8,128)(2,1)S(1)} %shard_map.121), channel_id=1, source_target_pairs={{0,4},{4,0},{1,5},{5,1},{2,6},{6,2},{3,7},{7,3},{8,12},{12,8},{9,1... | collective-permute-start | bytes 380936 | tf_op jit(solution)/shard_map/ppermute | solution.py:275
  260.8 4.1 %fusion.1 = (bf16[511,1536]{1,0:T(8,128)(2,1)}, bf16[511,1536]{1,0:T(8,128)(2,1)}) fusion(bf16[512,1536]{1,0:T(8,128)(2,1)} %copy-done.3), kind=kLoop, calls=%fused_computation.22 | loop fusion | bytes 6279168 | tf_op jit(solution)/shard_map/slice | solution.py:288
  264.8 1.9 collective-permute-start.11
  266.8 2.4 collective-permute-start.12
  270.1 4.1 %all-to-all-start.6 = ((bf16[4,496,128]{2,1,0:T(8,128)(2,1)}), bf16[4,496,128]{2,1,0:T(8,128)(2,1)}, u32[]{:S(2)}, u32[]{:S(2)}) async-start(bf16[4,496,128]{2,1,0:T(8,128)(2,1)} %broadcast_in_dim.21), calls=%async_computation.6 | async-start | bytes 1015808 | tf_op jit(solution)/shard_map/all_to_all | solution.py:271
  274.4 4.7 %fusion = bf16[1,512,1536]{2,1,0:T(8,128)(2,1)} fusion(f32[512,1536]{1,0:T(8,128)S(1)} %copy-done.1, bf16[512,1536]{1,0:T(8,128)(2,1)} %copy-done.3, bf16[1,1536]{1,0:T(2,128)(2,1)S(1)} %collective-permute-done.11, bf16[511,1536]{1,0:T(8,128)(2,1)} %get-tuple-element.102, bf16[511,1536]{1,0:T(8,128)(2,1)} %get-tuple-element.101, ...), kind=kLoop, calls=%fused_computation.1 | loop fusion | flops 12582912 | bytes 9455616 | tf_op jit(solution)/shard_map/broadcast_in_dim | solution.py:447
  279.1 5.2 %all-to-all-done.6.refs_0_ = bf16[4,496,128]{2,1,0:T(8,128)(2,1)} async-done(((bf16[4,496,128]{2,1,0:T(8,128)(2,1)}), bf16[4,496,128]{2,1,0:T(8,128)(2,1)}, u32[]{:S(2)}, u32[]{:S(2)}) %all-to-all-start.6) | async-done | bytes 507936 | tf_op jit(solution)/shard_map/all_to_all | solution.py:271
  284.3 1.9 shard_map.122
  (120 shorter events, 46.5 us)
Async XLA Ops:
  0.6 7.8 %copy-start.2 = (bf16[1,512,1536]{2,1,0:T(8,128)(2,1)S(1)}, bf16[1,512,1536]{2,1,0:T(8,128)(2,1)}, u32[]{:S(2)}) copy-start(bf16[1,512,1536]{2,1,0:T(8,128)(2,1)} %param.6) | copy-start | bytes 4718596
  0.6 16.1 %copy-start.35 = (bf16[4,128,128]{2,1,0:T(8,128)(2,1)S(1)}, bf16[4,128,128]{2,1,0:T(8,128)(2,1)}, u32[]{:S(2)}) copy-start(bf16[4,128,128]{2,1,0:T(8,128)(2,1)} %refs_0_.1) | copy-start | bytes 393220
  0.7 16.1 %copy-start.36 = (bf16[4,128,128]{2,1,0:T(8,128)(2,1)S(1)}, bf16[4,128,128]{2,1,0:T(8,128)(2,1)}, u32[]{:S(2)}) copy-start(bf16[4,128,128]{2,1,0:T(8,128)(2,1)} %refs_1_.1) | copy-start | bytes 393220
  0.7 23.7 %copy-start.37 = (f32[3,1536]{1,0:T(4,128)S(1)}, f32[3,1536]{1,0:T(4,128)}, u32[]{:S(2)}) copy-start(f32[3,1536]{1,0:T(4,128)} %refs_3_.1) | copy-start | bytes 55300
  2.6 21.8 %all-to-all-start = ((bf16[4,48,1536]{2,1,0:T(8,128)(2,1)}), bf16[4,48,1536]{2,1,0:T(8,128)(2,1)S(1)}, u32[]{:S(2)}, u32[]{:S(2)}) async-start(bf16[4,48,1536]{2,1,0:T(8,128)(2,1)} %broadcast_in_dim.8), calls=%async_computation | async-start | bytes 1179648 | tf_op jit(solution)/shard_map/all_to_all | solution.py:271
  8.5 12.6 %collective-permute-start.5 = (bf16[1,1536]{1,0:T(2,128)(2,1)S(1)}, bf16[1,1536]{1,0:T(2,128)(2,1)S(1)}, u32[]{:S(2)}, u32[]{:S(2)}) collective-permute-start(bf16[1,1536]{1,0:T(2,128)(2,1)S(1)} %get-tuple-element.104), channel_id=1, source_target_pairs={{0,8},{8,16},{16,24},{24,32},{32,40},{40,48},{48,56},{56,64},{64,7... | collective-permute-start | bytes 9224 | tf_op jit(solution)/shard_map/ppermute | solution.py:282
  10.4 10.7 %collective-permute-start.6 = (bf16[1,1536]{1,0:T(2,128)(2,1)S(1)}, bf16[1,1536]{1,0:T(2,128)(2,1)S(1)}, u32[]{:S(2)}, u32[]{:S(2)}) collective-permute-start(bf16[1,1536]{1,0:T(2,128)(2,1)S(1)} %get-tuple-element.103), channel_id=1, source_target_pairs={{8,0},{16,8},{24,16},{32,24},{40,32},{48,40},{56,48},{64,56},{72,6... | collective-permute-start | bytes 9224 | tf_op jit(solution)/shard_map/ppermute | solution.py:283
  24.4 4.7 %copy-start.19 = (bf16[4,48,1536]{2,1,0:T(8,128)(2,1)}, bf16[4,48,1536]{2,1,0:T(8,128)(2,1)S(1)}, u32[]{:S(2)}) copy-start(bf16[4,48,1536]{2,1,0:T(8,128)(2,1)S(1)} %all-to-all-done.refs_0_.refs_5_) | copy-start | bytes 1769476
  29.0 49.7 %all-to-all-start.1 = ((bf16[32,16,1536]{2,1,0:T(8,128)(2,1)}), bf16[32,16,1536]{2,1,0:T(8,128)(2,1)S(1)}, u32[]{:S(2)}, u32[]{:S(2)}) async-start(bf16[32,16,1536]{2,1,0:T(8,128)(2,1)} %bitcast.37), calls=%async_computation.1 | async-start | bytes 3145728 | tf_op jit(solution)/shard_map/all_to_all | solution.py:24
  35.0 42.1 %copy-start.20 = (bf16[4,48,1536]{2,1,0:T(8,128)(2,1)S(1)}, bf16[4,48,1536]{2,1,0:T(8,128)(2,1)}, u32[]{:S(2)}) copy-start(bf16[4,48,1536]{2,1,0:T(8,128)(2,1)} %copy-done.19) | copy-start | bytes 1769476
  35.1 29.0 %collective-permute-start = (bf16[4,48,1536]{2,1,0:T(8,128)(2,1)}, bf16[4,48,1536]{2,1,0:T(8,128)(2,1)S(1)}, u32[]{:S(2)}, u32[]{:S(2)}) collective-permute-start(bf16[4,48,1536]{2,1,0:T(8,128)(2,1)} %copy-done.19), channel_id=1, source_target_pairs={{0,64},{64,128},{128,192},{192,0},{1,65},{65,129},{129,193},{193,1... | collective-permute-start | bytes 1769480 | tf_op jit(solution)/shard_map/ppermute | solution.py:266
  35.3 31.3 %collective-permute-start.1 = (bf16[4,48,1536]{2,1,0:T(8,128)(2,1)}, bf16[4,48,1536]{2,1,0:T(8,128)(2,1)S(1)}, u32[]{:S(2)}, u32[]{:S(2)}) collective-permute-start(bf16[4,48,1536]{2,1,0:T(8,128)(2,1)} %copy-done.19), channel_id=1, source_target_pairs={{0,192},{64,0},{128,64},{192,128},{1,193},{65,1},{129,65},{193,129... | collective-permute-start | bytes 1769480 | tf_op jit(solution)/shard_map/ppermute | solution.py:266
  64.1 10.2 %collective-permute-start.2 = (bf16[2,48,1536]{2,1,0:T(8,128)(2,1)S(1)}, bf16[2,48,1536]{2,1,0:T(8,128)(2,1)S(1)}, u32[]{:S(2)}, u32[]{:S(2)}) collective-permute-start(bf16[2,48,1536]{2,1,0:T(8,128)(2,1)S(1)} %slice.44), channel_id=1, source_target_pairs={{0,64},{64,128},{128,192},{192,0},{1,65},{65,129},{129,193},{193,1... | collective-permute-start | bytes 884744 | tf_op jit(solution)/shard_map/ppermute | solution.py:266
  66.6 10.5 %collective-permute-start.3 = (bf16[2,48,1536]{2,1,0:T(8,128)(2,1)S(1)}, bf16[2,48,1536]{2,1,0:T(8,128)(2,1)S(1)}, u32[]{:S(2)}, u32[]{:S(2)}) collective-permute-start(bf16[2,48,1536]{2,1,0:T(8,128)(2,1)S(1)} %slice.45), channel_id=1, source_target_pairs={{0,192},{64,0},{128,64},{192,128},{1,193},{65,1},{129,65},{193,129... | collective-permute-start | bytes 884744 | tf_op jit(solution)/shard_map/ppermute | solution.py:266
  78.7 5.8 %copy-start.9 = (bf16[32,16,1536]{2,1,0:T(8,128)(2,1)}, bf16[32,16,1536]{2,1,0:T(8,128)(2,1)S(1)}, u32[]{:S(2)}) copy-start(bf16[32,16,1536]{2,1,0:T(8,128)(2,1)S(1)} %all-to-all-done.1) | copy-start | bytes 4718596
  78.8 2.2 copy-start.5
  84.6 14.4 %copy-start.17 = (bf16[1,512,1536]{2,1,0:T(8,128)(2,1)S(1)}, bf16[1,512,1536]{2,1,0:T(8,128)(2,1)}, u32[]{:S(2)}) copy-start(bf16[1,512,1536]{2,1,0:T(8,128)(2,1)} %param.7) | copy-start | bytes 4718596
  84.6 45.0 %all-to-all-start.2 = ((bf16[32,16,1536]{2,1,0:T(8,128)(2,1)}), bf16[32,16,1536]{2,1,0:T(8,128)(2,1)}, u32[]{:S(2)}, u32[]{:S(2)}) async-start(bf16[32,16,1536]{2,1,0:T(8,128)(2,1)} %bitcast.8), calls=%async_computation.2 | async-start | bytes 3145728 | tf_op jit(solution)/shard_map/all_to_all | solution.py:24
  92.6 4.8 %collective-permute-start.4 = (bf16[4,4,48,1536]{3,2,1,0:T(8,128)(2,1)}, bf16[4,4,48,1536]{3,2,1,0:T(8,128)(2,1)S(1)}, u32[]{:S(2)}, u32[]{:S(2)}) collective-permute-start(bf16[4,4,48,1536]{3,2,1,0:T(8,128)(2,1)} %copy-done.4), channel_id=1, source_target_pairs={{0,8},{8,0},{1,9},{9,1},{2,10},{10,2},{3,11},{11,3},{4,12},{12,4},... | collective-permute-start | bytes 7077896 | tf_op jit(solution)/shard_map/ppermute | solution.py:275
  97.5 1.5 copy-start.38
  129.6 43.2 %all-to-all-start.3 = ((bf16[32,16,1536]{2,1,0:T(8,128)(2,1)}), bf16[32,16,1536]{2,1,0:T(8,128)(2,1)S(1)}, u32[]{:S(2)}, u32[]{:S(2)}) async-start(bf16[32,16,1536]{2,1,0:T(8,128)(2,1)} %bitcast.36), calls=%async_computation.3 | async-start | bytes 3145728 | tf_op jit(solution)/shard_map/all_to_all | solution.py:24
  143.2 5.0 %copy-start.15 = (bf16[512,1536]{1,0:T(8,128)(2,1)}, bf16[512,1536]{1,0:T(8,128)(2,1)S(1)}, u32[]{:S(2)}) copy-start(bf16[512,1536]{1,0:T(8,128)(2,1)S(1)} %get-tuple-element.61.refs_1_.left_ref) | copy-start | bytes 4718596
  148.2 1.4 copy-start.24
  149.6 8.6 %collective-permute-start.7 = (bf16[768,1536]{1,0:T(8,128)(2,1)}, bf16[768,1536]{1,0:T(8,128)(2,1)}, u32[]{:S(2)}, u32[]{:S(2)}) collective-permute-start(bf16[768,1536]{1,0:T(8,128)(2,1)} %get-tuple-element.63), channel_id=1, source_target_pairs={{0,8},{8,0},{1,9},{9,1},{2,10},{10,2},{3,11},{11,3},{4,12},{12,4},... | collective-permute-start | bytes 7077896 | tf_op jit(solution)/shard_map/ppermute | solution.py:275
  151.4 6.8 %copy-start.25 = (bf16[768,1536]{1,0:T(8,128)(2,1)S(1)}, bf16[768,1536]{1,0:T(8,128)(2,1)}, u32[]{:S(2)}) copy-start(bf16[768,1536]{1,0:T(8,128)(2,1)} %copy-done.24) | copy-start | bytes 7077892
  156.5 1.6 copy-start
  172.8 2.9 %copy-start.11 = (bf16[32,16,1536]{2,1,0:T(8,128)(2,1)}, bf16[32,16,1536]{2,1,0:T(8,128)(2,1)S(1)}, u32[]{:S(2)}) copy-start(bf16[32,16,1536]{2,1,0:T(8,128)(2,1)S(1)} %all-to-all-done.3) | copy-start | bytes 4718596
  176.9 43.2 %all-to-all-start.4 = ((bf16[32,16,1536]{2,1,0:T(8,128)(2,1)}), bf16[32,16,1536]{2,1,0:T(8,128)(2,1)S(1)}, u32[]{:S(2)}, u32[]{:S(2)}) async-start(bf16[32,16,1536]{2,1,0:T(8,128)(2,1)} %bitcast.33), calls=%async_computation.4 | async-start | bytes 3145728 | tf_op jit(solution)/shard_map/all_to_all | solution.py:24
  183.1 17.1 %collective-permute-start.8 = (bf16[768,384]{1,0:T(8,128)(2,1)}, bf16[768,384]{1,0:T(8,128)(2,1)}, u32[]{:S(2)}, u32[]{:S(2)}) collective-permute-start(bf16[768,384]{1,0:T(8,128)(2,1)} %get-tuple-element.68), channel_id=1, source_target_pairs={{0,1},{1,2},{2,3},{3,0},{4,5},{5,6},{6,7},{7,4},{8,9},{9,10},{10,1... | collective-permute-start | bytes 1769480 | tf_op jit(solution)/shard_map/ppermute | solution.py:266
  184.8 29.2 %collective-permute-start.9 = (bf16[768,384]{1,0:T(8,128)(2,1)}, bf16[768,384]{1,0:T(8,128)(2,1)}, u32[]{:S(2)}, u32[]{:S(2)}) collective-permute-start(bf16[768,384]{1,0:T(8,128)(2,1)} %get-tuple-element.69), channel_id=1, source_target_pairs={{0,2},{1,3},{2,0},{3,1},{4,6},{5,7},{6,4},{7,5},{8,10},{9,11},{10,... | collective-permute-start | bytes 1769480 | tf_op jit(solution)/shard_map/ppermute | solution.py:266
  187.7 26.3 %collective-permute-start.10 = (bf16[768,384]{1,0:T(8,128)(2,1)}, bf16[768,384]{1,0:T(8,128)(2,1)}, u32[]{:S(2)}, u32[]{:S(2)}) collective-permute-start(bf16[768,384]{1,0:T(8,128)(2,1)} %get-tuple-element.70), channel_id=1, source_target_pairs={{0,3},{1,0},{2,1},{3,2},{4,7},{5,4},{6,5},{7,6},{8,11},{9,8},{10,9... | collective-permute-start | bytes 1769480 | tf_op jit(solution)/shard_map/ppermute | solution.py:266
  194.3 19.7 %copy-start.39 = (bf16[768,384]{1,0:T(8,128)(2,1)S(1)}, bf16[768,384]{1,0:T(8,128)(2,1)}, u32[]{:S(2)}) copy-start(bf16[768,384]{1,0:T(8,128)(2,1)} %get-tuple-element.77) | copy-start | bytes 1769476
  216.5 24.5 %collective-permute-start.13 = (bf16[192,384]{1,0:T(8,128)(2,1)}, bf16[192,384]{1,0:T(8,128)(2,1)}, u32[]{:S(2)}, u32[]{:S(2)}) collective-permute-start(bf16[192,384]{1,0:T(8,128)(2,1)} %get-tuple-element.107), channel_id=1, source_target_pairs={{0,64},{64,128},{128,192},{192,0},{1,65},{65,129},{129,193},{193,1... | collective-permute-start | bytes 442376 | tf_op jit(solution)/shard_map/ppermute | solution.py:266
  216.7 24.3 %collective-permute-start.14 = (bf16[192,384]{1,0:T(8,128)(2,1)}, bf16[192,384]{1,0:T(8,128)(2,1)}, u32[]{:S(2)}, u32[]{:S(2)}) collective-permute-start(bf16[192,384]{1,0:T(8,128)(2,1)} %get-tuple-element.106), channel_id=1, source_target_pairs={{0,128},{64,192},{128,0},{192,64},{1,129},{65,193},{129,1},{193,65... | collective-permute-start | bytes 442376 | tf_op jit(solution)/shard_map/ppermute | solution.py:266
  219.4 21.6 %collective-permute-start.15 = (bf16[192,384]{1,0:T(8,128)(2,1)}, bf16[192,384]{1,0:T(8,128)(2,1)}, u32[]{:S(2)}, u32[]{:S(2)}) collective-permute-start(bf16[192,384]{1,0:T(8,128)(2,1)} %get-tuple-element.105), channel_id=1, source_target_pairs={{0,192},{64,0},{128,64},{192,128},{1,193},{65,1},{129,65},{193,129... | collective-permute-start | bytes 442376 | tf_op jit(solution)/shard_map/ppermute | solution.py:266
  227.1 28.5 %copy-start.3 = (bf16[512,1536]{1,0:T(8,128)(2,1)}, bf16[512,1536]{1,0:T(8,128)(2,1)S(1)}, u32[]{:S(2)}) copy-start(bf16[512,1536]{1,0:T(8,128)(2,1)S(1)} %get-tuple-element.72.refs_4_) | copy-start | bytes 4718596
  227.2 28.3 %all-to-all-start.5 = ((bf16[32,3,1536]{2,1,0:T(4,128)(2,1)}), bf16[32,3,1536]{2,1,0:T(4,128)(2,1)S(1)}, u32[]{:S(2)}, u32[]{:S(2)}) async-start(bf16[32,3,1536]{2,1,0:T(4,128)(2,1)} %copy-done.34), calls=%async_computation.5 | async-start | bytes 786432 | tf_op jit(solution)/shard_map/all_to_all | solution.py:410
  242.1 9.0 %collective-permute-start.16 = (bf16[48,384]{1,0:T(8,128)(2,1)S(1)}, bf16[48,384]{1,0:T(8,128)(2,1)S(1)}, u32[]{:S(2)}, u32[]{:S(2)}) collective-permute-start(bf16[48,384]{1,0:T(8,128)(2,1)S(1)} %get-tuple-element.111), channel_id=1, source_target_pairs={{0,16},{16,32},{32,48},{48,0},{1,17},{17,33},{33,49},{49,1},{2,18}... | collective-permute-start | bytes 110600 | tf_op jit(solution)/shard_map/ppermute | solution.py:266
  243.7 9.1 %collective-permute-start.17 = (bf16[48,384]{1,0:T(8,128)(2,1)S(1)}, bf16[48,384]{1,0:T(8,128)(2,1)S(1)}, u32[]{:S(2)}, u32[]{:S(2)}) collective-permute-start(bf16[48,384]{1,0:T(8,128)(2,1)S(1)} %get-tuple-element.110), channel_id=1, source_target_pairs={{0,32},{16,48},{32,0},{48,16},{1,33},{17,49},{33,1},{49,17},{2,34}... | collective-permute-start | bytes 110600 | tf_op jit(solution)/shard_map/ppermute | solution.py:266
  246.1 6.7 %collective-permute-start.18 = (bf16[48,384]{1,0:T(8,128)(2,1)S(1)}, bf16[48,384]{1,0:T(8,128)(2,1)S(1)}, u32[]{:S(2)}, u32[]{:S(2)}) collective-permute-start(bf16[48,384]{1,0:T(8,128)(2,1)S(1)} %get-tuple-element.109), channel_id=1, source_target_pairs={{0,48},{16,0},{32,16},{48,32},{1,49},{17,1},{33,17},{49,33},{2,50}... | collective-permute-start | bytes 110600 | tf_op jit(solution)/shard_map/ppermute | solution.py:266
  247.5 5.8 %collective-permute-start.19 = (bf16[256,128]{1,0:T(8,128)(2,1)S(1)}, bf16[256,128]{1,0:T(8,128)(2,1)S(1)}, u32[]{:S(2)}, u32[]{:S(2)}) collective-permute-start(bf16[256,128]{1,0:T(8,128)(2,1)S(1)} %get-tuple-element.86), channel_id=1, source_target_pairs={{0,1},{1,2},{2,3},{3,0},{4,5},{5,6},{6,7},{7,4},{8,9},{9,10},{10,1... | collective-permute-start | bytes 196616 | tf_op jit(solution)/shard_map/ppermute | solution.py:266
  248.8 5.8 %collective-permute-start.20 = (bf16[256,128]{1,0:T(8,128)(2,1)S(1)}, bf16[256,128]{1,0:T(8,128)(2,1)S(1)}, u32[]{:S(2)}, u32[]{:S(2)}) collective-permute-start(bf16[256,128]{1,0:T(8,128)(2,1)S(1)} %get-tuple-element.87), channel_id=1, source_target_pairs={{0,2},{1,3},{2,0},{3,1},{4,6},{5,7},{6,4},{7,5},{8,10},{9,11},{10,... | collective-permute-start | bytes 196616 | tf_op jit(solution)/shard_map/ppermute | solution.py:266
  251.2 4.3 %collective-permute-start.21 = (bf16[256,128]{1,0:T(8,128)(2,1)S(1)}, bf16[256,128]{1,0:T(8,128)(2,1)S(1)}, u32[]{:S(2)}, u32[]{:S(2)}) collective-permute-start(bf16[256,128]{1,0:T(8,128)(2,1)S(1)} %get-tuple-element.88), channel_id=1, source_target_pairs={{0,3},{1,0},{2,1},{3,2},{4,7},{5,4},{6,5},{7,6},{8,11},{9,8},{10,9... | collective-permute-start | bytes 196616 | tf_op jit(solution)/shard_map/ppermute | solution.py:266
  255.7 13.5 %collective-permute-start.22 = (bf16[496,128]{1,0:T(8,128)(2,1)S(1)}, bf16[496,128]{1,0:T(8,128)(2,1)S(1)}, u32[]{:S(2)}, u32[]{:S(2)}) collective-permute-start(bf16[496,128]{1,0:T(8,128)(2,1)S(1)} %shard_map.121), channel_id=1, source_target_pairs={{0,4},{4,0},{1,5},{5,1},{2,6},{6,2},{3,7},{7,3},{8,12},{12,8},{9,1... | collective-permute-start | bytes 380936 | tf_op jit(solution)/shard_map/ppermute | solution.py:275
  260.8 13.6 %copy-start.1 = (f32[512,1536]{1,0:T(8,128)S(1)}, f32[512,1536]{1,0:T(8,128)}, u32[]{:S(2)}) copy-start(f32[512,1536]{1,0:T(8,128)} %copy-done) | copy-start | bytes 9437188
  264.8 9.4 %collective-permute-start.11 = (bf16[1,1536]{1,0:T(2,128)(2,1)S(1)}, bf16[1,1536]{1,0:T(2,128)(2,1)S(1)}, u32[]{:S(2)}, u32[]{:S(2)}) collective-permute-start(bf16[1,1536]{1,0:T(2,128)(2,1)S(1)} %get-tuple-element.73), channel_id=1, source_target_pairs={{8,0},{16,8},{24,16},{32,24},{40,32},{48,40},{56,48},{64,56},{72,6... | collective-permute-start | bytes 9224 | tf_op jit(solution)/shard_map/ppermute | solution.py:283
  266.8 7.6 %collective-permute-start.12 = (bf16[1,1536]{1,0:T(2,128)(2,1)S(1)}, bf16[1,1536]{1,0:T(2,128)(2,1)S(1)}, u32[]{:S(2)}, u32[]{:S(2)}) collective-permute-start(bf16[1,1536]{1,0:T(2,128)(2,1)S(1)} %get-tuple-element.74), channel_id=1, source_target_pairs={{0,8},{8,16},{16,24},{24,32},{32,40},{40,48},{48,56},{56,64},{64,7... | collective-permute-start | bytes 9224 | tf_op jit(solution)/shard_map/ppermute | solution.py:282
  270.1 14.1 %all-to-all-start.6 = ((bf16[4,496,128]{2,1,0:T(8,128)(2,1)}), bf16[4,496,128]{2,1,0:T(8,128)(2,1)}, u32[]{:S(2)}, u32[]{:S(2)}) async-start(bf16[4,496,128]{2,1,0:T(8,128)(2,1)} %broadcast_in_dim.21), calls=%async_computation.6 | async-start | bytes 1015808 | tf_op jit(solution)/shard_map/all_to_all | solution.py:271
  (22 other events, 26.8 us)
where the time goes:
time: 288 us; the launch traced here: 286 us
  waiting for transfers between devices  105 us (36%)
  starting transfers between devices  86.2 us (30%)
  Pallas kernels  41.9 us (15%)
  local copies, waits for them, and re-layouts  41.4 us (14%)
  other arithmetic  11 us (4%)
    ppermute x16, waiting for transfers between devices, shift(): lax.ppermute(values, axis, [(i, (i + step) % count) for i in range(count)])  56.4 us
    pallas_call x13, Pallas kernels, on_device(): pl.pallas_call(body, grid=(width // step if step else 1,), in_specs=[spec...  36.8 us
    unnamed x80, local copies, waits for them, and re-layouts  33.7 us
    all_to_all x4, waiting for transfers between devices, exchange(): lax.all_to_all(cut, SEQ, split_axis=0, concat_axis=0, tiled=True)  33.6 us
    all_to_all x4, starting transfers between devices, exchange(): lax.all_to_all(cut, SEQ, split_axis=0, concat_axis=0, tiled=True)  26.5 us
    ppermute x16, starting transfers between devices, shift(): lax.ppermute(values, axis, [(i, (i + step) % count) for i in range(count)])  24.1 us
    all_to_all x2, starting transfers between devices, spread_over(): return lax.all_to_all(copies, axis, split_axis=0, concat_axis=0, tiled=True)  10 us
    all_to_all x2, waiting for transfers between devices, spread_over(): return lax.all_to_all(copies, axis, split_axis=0, concat_axis=0, tiled=True)  8.4 us
  transfers between devices with their start and end apart: 30, of which 16 were waited for; matrix products, arithmetic and copies ran while one was open for 6% of the time, Pallas kernels for 12%

commit v1 on v0

--- a/solution.py
+++ b/solution.py
@@ -35,15 +35,21 @@
     return (lax.axis_index(axis) + offset % count) & (count - 1)
 
 
-def on_device(kernel, operands, outputs, needs=(), scratch=(), step=0, whole=(), kept=()):
+def on_device(kernel, operands, outputs, needs=(), scratch=(), step=0, whole={}, kept=(), stay=()):
     width = max(one.shape[-1] for one in operands)
 
     def spec(shape, entire=False):
         zeros = (0,) * (len(shape) - 1)
+        if entire is None:
+            return pl.BlockSpec((1, *shape[1:]), lambda k: (k, *zeros))
         if step and shape[-1] == width and not entire:
             return pl.BlockSpec((*shape[:-1], step), lambda k: (*zeros, k))
         return pl.BlockSpec(shape, lambda k: (*zeros, 0))
 
+    def corner(shape):
+        zeros = (0,) * len(shape)
+        return pl.BlockSpec((*[1] * (len(shape) - 2), 16, 128), lambda k: zeros)
+
     count = len(operands)
 
     def body(*refs):
@@ -52,14 +58,17 @@
     return pl.pallas_call(
         body,
         grid=(width // step if step else 1,),
-        in_specs=[spec(one.shape, k in whole) for k, one in enumerate(operands)]
-        + [pl.BlockSpec(memory_space=pl.ANY)] * len(needs),
+        in_specs=[spec(one.shape, whole.get(k, False)) for k, one in enumerate(operands)]
+        + [corner(one.shape) for one in needs],
         out_specs=[spec(one.shape) for one in outputs],
         out_shape=[pltpu.HBM(one.shape, one.dtype) if k in kept else one for k, one in enumerate(outputs)],
         scratch_shapes=scratch,
         cost_estimate=pl.CostEstimate(flops=1000, transcendentals=0, bytes_accessed=1000),
         compiler_params=pltpu.CompilerParams(vmem_limit_bytes=ROOM),
-    )(*operands, *needs)
+    )(
+        *[pltpu.with_memory_space_constraint(one, pltpu.HBM) if k in stay else one for k, one in enumerate(operands)],
+        *needs,
+    )
 
 
 def setup_kernel(lead_in, trail_in, lead_ref, lead_back, trail_ref, trail_back, to_position, to_group, *, owners):
@@ -109,19 +118,20 @@
     out_ref[...] = matmul(mix_ref[...], values_ref[...]).astype(BF16)
 
 
-def half_kernel(own_ref, before_ref, after_ref, low_ref, high_ref, out_ref):
-    out_ref[position("x")] = own_ref[...]
-    out_ref[position("x", -1)] = before_ref[...]
-    out_ref[position("x", 1)] = after_ref[...]
-    part = low_ref.shape[0]
-    out_ref[position("x", 2), :part] = low_ref[...]
-    out_ref[position("x", 2), part:] = high_ref[...]
+def place_kernel(*refs, axis):
+    for k, one in enumerate(refs[:-1]):
+        refs[-1][position(axis, -k)] = one[...]
+
+
+def place(pieces, axis, needs=()):
+    whole = like((len(pieces), *pieces[0].shape))
+    return on_device(functools.partial(place_kernel, axis=axis), pieces, [whole], needs=needs)[0]
 
 
 def project_kernel(tok_ref, mine_ref, other_ref, cotangent_ref, order_ref, weight_ref, gate_ref, send_ref):
     core = lax.axis_index("core")
-    weight_ref[:, core] = mine_ref[...]
-    weight_ref[:, 1 - core] = other_ref[...]
+    weight_ref[:, core] = mine_ref[0]
+    weight_ref[:, 1 - core] = other_ref[0]
     gate = matmul(tok_ref[...], weight_ref[...].reshape(tok_ref.shape[1], gate_ref.shape[1]))
     gate_ref[...] = gate
     d_monarch = (cotangent_ref[...].astype(F32) * gate).astype(BF16)
@@ -158,26 +168,66 @@
     core = lax.axis_index("core")
     rows = whole.shape[0] // owners
     whole[...] = matmul(tok_ref[...], d_gate_ref[...], 0, 0)
-    for k in range(owners // 2):
-        near = pl.multiple_of((2 * k + core) * rows, rows)
-        far = pl.multiple_of((2 * k + 1 - core) * rows, rows)
-        mine_ref[k * rows : (k + 1) * rows, :] = whole[pl.ds(near, rows), :].astype(BF16)
-        other_ref[k * rows : (k + 1) * rows, :] = whole[pl.ds(far, rows), :].astype(BF16)
-
-
-def backward_kernel(
-    mix_ref, delta_ref, tok_ref, before_ref, after_ref, out_ref, first_ref, last_ref, sums_ref
-):
+
+    def move(k, _):
+        near = pl.ds(pl.multiple_of((2 * k + core) * rows, rows), rows)
+        far = pl.ds(pl.multiple_of((2 * k + 1 - core) * rows, rows), rows)
+        to = pl.ds(pl.multiple_of(k * rows, rows), rows)
+        mine_ref[to, :] = whole[near, :].astype(BF16)
+        other_ref[to, :] = whole[far, :].astype(BF16)
+        return _
+
+    lax.fori_loop(0, owners // 2, move, 0)
+
+
+def split_pair(mine, other, count, step=256):
+    rows, width = mine.shape
+    share = width // count
+
+    def body(mine_ref, other_ref, *outs):
+        for k, one in enumerate(outs):
+            columns = pl.ds(pl.multiple_of(position("y", k) * share, 128), share)
+            one[...] = (mine_ref[:, columns].astype(F32) + other_ref[:, columns].astype(F32)).astype(BF16)
+
+    return pl.pallas_call(
+        body,
+        grid=(rows // step,),
+        in_specs=[pl.BlockSpec((step, width), lambda k: (k, 0))] * 2,
+        out_specs=[pl.BlockSpec((step, share), lambda k: (k, 0))] * count,
+        out_shape=[like((rows, share))] * count,
+        cost_estimate=pl.CostEstimate(flops=1000, transcendentals=0, bytes_accessed=1000),
+        compiler_params=pltpu.CompilerParams(vmem_limit_bytes=ROOM),
+    )(mine, other)
+
+
+def backward_kernel(mix_ref, delta_ref, tok_ref, before_ref, after_ref, out_ref, spread_ref):
     d_conv = matmul(mix_ref[...], delta_ref[...]).astype(BF16)
     out_ref[...] = d_conv
-    first_ref[...] = d_conv[:1]
-    last_ref[...] = d_conv[-1:]
     d_wide = d_conv.astype(F32)
     values = tok_ref[...].astype(F32)
     previous, following = with_neighbours(values, before_ref[...].astype(F32), after_ref[...].astype(F32))
     sums = [jnp.sum(d_wide * one, axis=0, keepdims=True) for one in (previous, values, following)]
-    sums = jnp.concatenate(sums, axis=0).astype(BF16)
-    sums_ref[...] = jnp.broadcast_to(sums[None], sums_ref.shape)
+    here = lax.axis_index(SEQ)
+    count, lines, step = spread_ref.shape
+    target = lax.broadcasted_iota(jnp.int32, (count, lines, step), 0)
+    line = lax.broadcasted_iota(jnp.int32, (count, lines, step), 1)
+    edge = jnp.where(target == here + 1, d_wide[-1:][None], 0.0)
+    edge = jnp.where(target == here - 1, d_wide[:1][None], edge)
+    sums = jnp.concatenate([*sums, jnp.zeros((1, step), F32)], axis=0)
+    spread_ref[...] = jnp.where(line == lines - 1, edge, sums[None]).astype(BF16)
+
+
+def tokens_kernel(d_conv_ref, spread_ref, taps_ref, gate_ref, out_ref):
+    here = lax.axis_index(SEQ)
+    edges = spread_ref[...].astype(F32)[:, -1]
+    source = lax.broadcasted_iota(jnp.int32, edges.shape, 0)
+    before = jnp.sum(jnp.where(source == here - 1, edges, 0.0), axis=0, keepdims=True)
+    after_row = jnp.sum(jnp.where(source == here + 1, edges, 0.0), axis=0, keepdims=True)
+    values = d_conv_ref[...].astype(F32)
+    previous, following = with_neighbours(values, before, after_row)
+    taps = taps_ref[...]
+    conv_back = taps[0:1] * following + taps[1:2] * values + taps[2:3] * previous
+    out_ref[...] = (conv_back + gate_ref[...]).astype(BF16)
 
 
 def add_pairs(left, right, sums):
@@ -237,6 +287,12 @@
     for one in (lanes(total(gate), size), total(factors), lanes(taps, size)):
         out_ref[line : line + one.shape[0], :] = one.astype(BF16)
         line += one.shape[0]
+
+
+def pair_kernel(one_ref, other_ref, out_ref):
+    value = (one_ref[...].astype(F32) + other_ref[...].astype(F32)).astype(BF16)
+    for k in range(out_ref.shape[0]):
+        out_ref[k] = value
 
 
 def finish_kernel(pieces, gate_ref, second_ref, first_ref, taps_ref):
@@ -266,9 +322,8 @@
     return lax.ppermute(values, axis, [(i, (i + step) % count) for i in range(count)])
 
 
-def spread_over(values, axis):
-    copies = jnp.broadcast_to(values[None], (lax.axis_size(axis), *values.shape))
-    return lax.all_to_all(copies, axis, split_axis=0, concat_axis=0, tiled=True)
+def ring(values, axis):
+    return [values] + [shift(values, axis, k) for k in range(1, lax.axis_size(axis))]
 
 
 def swap(values, axis):
@@ -282,14 +337,6 @@
     before = lax.ppermute(last, SEQ, up)
     after = lax.ppermute(first, SEQ, down)
     return before, after
-
-
-def shift_down(values, before):
-    return jnp.concatenate([before, values[:-1]], axis=0)
-
-
-def shift_up(values, after):
-    return jnp.concatenate([values[1:], after], axis=0)
 
 
 def piece(values, index, count, dim):
@@ -332,42 +379,46 @@
     x_count, z_count, y_count = lax.axis_size("x"), lax.axis_size("z_lo"), lax.axis_size("y")
 
     tok_before, tok_after = halo_rows(features[:1], features[-1:])
-    near = spread_over(gate_weight, "z_lo")
+    share = width // y_count
+    near = ring(piece(gate_weight, position("y"), y_count, 1), "z_lo")
     lead, lead_back, trail, trail_back, to_position, to_group = on_device(
-        functools.partial(setup_kernel, owners=owners), [leading, trailing], [square] * 6, kept=range(1, 6)
+        functools.partial(setup_kernel, owners=owners), [leading, trailing], [square] * 6, kept=range(1, 6), stay=[0, 1]
     )
     conv_in, send = on_device(
         forward_kernel,
         [features, tok_before, tok_after, conv_weight, lead],
         [wide, wide],
-        needs=[near],
+        needs=near,
+        stay=[0],
         step=512,
     )
     columns = exchange(send)
-    before, after = shift(near, "x", 1), shift(near, "x", -1)
-    low, high = shift(before[: z_count // 2], "x", 1), shift(after[z_count // 2 :], "x", -1)
-    (near,) = on_device(
-        half_kernel, [near, before, after, low, high], [like((x_count, *near.shape))]
-    )
+    near = place(ring(place(near, "z_lo"), "x"), "x").reshape(x_count * z_count, own, share)
+    near = ring(near, "y")
+    (send,) = on_device(mix_kernel, [trail, columns], [wide], needs=[near[1], near[-1]], step=512)
+    second_out = exchange(send)
+    near = place(near, "y")
     far = swap(near, "core")
-    (send,) = on_device(mix_kernel, [trail, columns], [wide], needs=[near], step=512)
-    second_out = exchange(send)
-
-    near, far = [one.reshape(x_count * z_count, own, width) for one in (near, far)]
+
     whole_gate, gate_act, send = on_device(
         project_kernel,
         [features, near, far, grad_out, to_position],
         [like((x_count * z_count, 2, own, width)), like((rows, width), F32), wide],
         needs=[send],
-        step=512,
-        whole=[0],
+        step=share,
+        whole={0: True, 1: None, 2: None},
     )
     whole_gate = whole_gate.reshape(width, width)
     send, second_out = lax.optimization_barrier((send, second_out))
     delta = exchange(send)
 
+    corner = swap(second_out[:16, :size], "core")
     mixed, d_gate = on_device(
-        gate_kernel, [to_position, second_out, gate_act, grad_out], [wide, wide], step=512
+        gate_kernel,
+        [to_position, second_out, gate_act, grad_out],
+        [wide, wide],
+        needs=[corner],
+        step=512,
     )
     mine, other = on_device(
         functools.partial(weight_kernel, owners=owners),
@@ -377,15 +428,15 @@
     )
     other = swap(other, "core")
     gate_back = project_back(d_gate, whole_gate)
-    pieces = [
-        (
-            piece(mine, position("y", k), y_count, 1).astype(F32)
-            + piece(other, position("y", k), y_count, 1).astype(F32)
-        ).astype(BF16)
-        for k in range(y_count)
-    ]
-    delta, *pieces = lax.optimization_barrier((delta, *pieces))
-    (send,) = on_device(mix_kernel, [trail_back, delta], [wide], needs=[gate_back], step=512)
+    pieces = split_pair(mine, other, y_count)
+    arrived = send_pieces(pieces, "y")
+    (send,) = on_device(
+        mix_kernel,
+        [trail_back, delta],
+        [wide],
+        needs=[gate_back, arrived[1], arrived[-1]],
+        step=512,
+    )
     d_first = exchange(send)
     (grad_second,) = on_device(
         second_kernel,
@@ -395,16 +446,15 @@
         needs=[send],
         step=512,
     )
-    arrived = send_pieces(pieces, "y")
     grad_second, *arrived = lax.optimization_barrier((grad_second, *arrived))
     pieces = send_pieces(cut(add_up(arrived), "x", 0), "x")
-
-    edge = like((1, width))
-    d_conv, *d_edge, spread = on_device(
+    pieces = cut(add_up(pieces), "z_lo", 0)
+
+    d_conv, spread = on_device(
         backward_kernel,
         [lead_back, d_first, features, tok_before, tok_after],
-        [wide, edge, edge, like((owners, *conv_weight.shape))],
-        needs=[grad_second],
+        [wide, like((owners, conv_weight.shape[0] + 1, width))],
+        needs=[grad_second, pieces[1]],
         step=512,
     )
     spread = lax.all_to_all(spread, SEQ, split_axis=0, concat_axis=0, tiled=True)
@@ -414,27 +464,31 @@
         [like((2 * size, size))] * y_count,
         scratch=[pltpu.VMEM((blocks, size, size), F32)],
         needs=[d_conv],
+        stay=[1, 2],
         step=512,
     )
-    factors[0], *pieces = lax.optimization_barrier((factors[0], *pieces))
-    grad_before, grad_after = halo_rows(*d_edge)
     parts = [
-        *send_pieces(cut(add_up(pieces), "z_lo", 0), "z_lo"),
+        *send_pieces(pieces, "z_lo"),
         *send_pieces(factors, "y"),
     ]
-    d_next = shift_up(d_conv, grad_after).astype(F32)
-    d_prev = shift_down(d_conv, grad_before).astype(F32)
-    conv_back = conv_weight[0] * d_next + conv_weight[1] * d_conv.astype(F32) + conv_weight[2] * d_prev
-    grad_tokens = (conv_back + gate_back).astype(BF16)
+    (grad_tokens,) = on_device(
+        tokens_kernel, [d_conv, spread, conv_weight, gate_back], [wide], step=512
+    )
 
     lines = (own * width // y_count) // size + 2 * size + 8 * (width // size)
     (packed,) = on_device(
-        functools.partial(pack_kernel, z_count=z_count), [*parts, spread], [like((lines, size))]
-    )
-    packed = (packed.astype(F32) + swap(packed, "z_hi").astype(F32)).astype(BF16)
+        functools.partial(pack_kernel, z_count=z_count),
+        [*parts, spread],
+        [like((lines, size))],
+        stay=range(len(parts)),
+    )
+    (packed,) = on_device(
+        pair_kernel, [packed, swap(packed, "z_hi")], [like((y_count, *packed.shape))]
+    )
+    packed = lax.all_to_all(packed, "y", split_axis=0, concat_axis=0, tiled=True)
     grad_gate, grad_second, grad_first, grad_conv = on_device(
         finish_kernel,
-        [spread_over(packed, "y")],
+        [packed],
         [
             like((own, width), F32),
             like((rows, size), F32),

time: 288 us -> 285 us (0.990)
  Pallas kernels: 41.9 us -> 61.8 us
  waiting for transfers between devices: 105 us -> 93.1 us
  other arithmetic: 11 us -> 2.35 us
  local copies, waits for them, and re-layouts: 41.4 us -> 34.6 us
  starting transfers between devices: 86.2 us -> 90 us
    all_to_all x4, waiting for transfers between devices: 33.6 us -> 3.16 us  [exchange(): lax.all_to_all(cut, SEQ, split_axis=0, concat_axis=0, tiled=True)]
    pallas_call x13 -> x17, Pallas kernels: 36.8 us -> 54.2 us  [on_device(): pl.pallas_call(body, grid=(width // step if step else 1,), in_specs=[spec...]
    ppermute x16 -> x21, waiting for transfers between devices: 56.4 us -> 72.1 us  [shift(): lax.ppermute(values, axis, [(i, (i + step) % count) for i in range(count)])]
    ppermute x16 -> x21, starting transfers between devices: 24.1 us -> 34.5 us  [shift(): lax.ppermute(values, axis, [(i, (i + step) % count) for i in range(count)])]
    ppermute x3 -> x4, waiting for transfers between devices: 4.6 us -> 14.9 us  [swap(): return lax.ppermute(values, axis, [(0, 1), (1, 0)])]
    all_to_all x2 -> x1, starting transfers between devices: 10 us -> 4.14 us  [shards(): lax.all_to_all(packed, 'y', split_axis=0, concat_axis=0, tiled=True)]
    all_to_all x2 -> x1, waiting for transfers between devices: 8.4 us -> 2.87 us  [shards(): lax.all_to_all(packed, 'y', split_axis=0, concat_axis=0, tiled=True)]
    broadcast_in_dim x1 -> x0, other arithmetic: 4.69 us -> none  [shards(): grad_tokens[None]]
  transfers between devices with their start and end apart: 30 -> 33, of which waited for: 16 -> 17; matrix products, arithmetic and copies ran while one was open for 6% -> 2% of each run, Pallas kernels for 12% -> 15%
where the time goes in v1:
time: 285 us; the launch traced here: 283 us
  waiting for transfers between devices  93.1 us (33%)
  starting transfers between devices  90 us (32%)
  Pallas kernels  61.8 us (22%)
  local copies, waits for them, and re-layouts  34.6 us (12%)
    ppermute x21, waiting for transfers between devices, shift(): lax.ppermute(values, axis, [(i, (i + step) % count) for i in range(count)])  72.1 us
    pallas_call x17, Pallas kernels, on_device(): pl.pallas_call(body, grid=(width // step if step else 1,), in_specs=[spec...  54.2 us
    ppermute x21, starting transfers between devices, shift(): lax.ppermute(values, axis, [(i, (i + step) % count) for i in range(count)])  34.5 us
    unnamed x94, local copies, waits for them, and re-layouts  31.7 us
    all_to_all x4, starting transfers between devices, exchange(): lax.all_to_all(cut, SEQ, split_axis=0, concat_axis=0, tiled=True)  30.3 us
    ppermute x4, waiting for transfers between devices, swap(): return lax.ppermute(values, axis, [(0, 1), (1, 0)])  14.9 us
    all_to_all x1, starting transfers between devices, shards(): lax.all_to_all(spread, SEQ, split_axis=0, concat_axis=0, tiled=True)  6.76 us
    ppermute x1, starting transfers between devices, halo_rows(): after = lax.ppermute(first, SEQ, down)  6.34 us
  transfers between devices with their start and end apart: 33, of which 17 were waited for; matrix products, arithmetic and copies ran while one was open for 2% of the time, Pallas kernels for 15%

profile of v1, /device:TPU:6, one launch (start us, length us, event | category | flops | bytes accessed | tf_op | source)
XLA Modules:
  0.0 282.9 jit_solution(8757363227825405537)
XLA Ops:
  1.6 1.9 collective-permute-start
  3.5 3.3 %collective-permute-start.1 = (bf16[48,384]{1,0:T(8,128)(2,1)S(1)}, bf16[48,384]{1,0:T(8,128)(2,1)S(1)}, u32[]{:S(2)}, u32[]{:S(2)}) collective-permute-start(bf16[48,384]{1,0:T(8,128)(2,1)S(1)} %constant_dynamic-slice_fusion.refs_0_.refs_5_), channel_id=1, source_target_pairs={{0,32},{16,48},{32,0},{48,16},{1,33},{17,49},{33,1},{49,17},{2,34}... | collective-permute-start | bytes 110600 | tf_op jit(solution)/shard_map/ppermute | solution.py:322
  8.5 1.9 collective-permute-start.10
  10.4 6.3 %collective-permute-start.11 = (bf16[1,1536]{1,0:T(2,128)(2,1)S(1)}, bf16[1,1536]{1,0:T(2,128)(2,1)S(1)}, u32[]{:S(2)}, u32[]{:S(2)}) collective-permute-start(bf16[1,1536]{1,0:T(2,128)(2,1)S(1)} %get-tuple-element.78), channel_id=1, source_target_pairs={{8,0},{16,8},{24,16},{32,24},{40,32},{48,40},{56,48},{64,56},{72,6... | collective-permute-start | bytes 9224 | tf_op jit(solution)/shard_map/ppermute | solution.py:338
  16.8 3.8 %shard_map.109 = (bf16[512,512]{1,0:T(8,128)(2,1)S(1)}, bf16[512,512]{1,0:T(8,128)(2,1)}, bf16[512,512]{1,0:T(8,128)(2,1)}, bf16[512,512]{1,0:T(8,128)(2,1)}, bf...) custom-call(bf16[4,128,128]{2,1,0:T(8,128)(2,1)} %refs_0_.1, bf16[4,128,128]{2,1,0:T(8,128)(2,1)} %refs_1_.1), custom_call_target="tpu_custom_call" | custom-call | flops 1000 | bytes 1000 | tf_op jit(solution)/shard_map/pallas_call | solution.py:58
  21.4 4.5 %shard_map.113 = (bf16[512,1536]{1,0:T(8,128)(2,1)S(1)}, bf16[512,1536]{1,0:T(8,128)(2,1)}) custom-call(bf16[512,1536]{1,0:T(8,128)(2,1)} %bitcast.20, bf16[1,1536]{1,0:T(2,128)(2,1)S(1)} %collective-permute-done.10.refs_1_.refs_3_, bf16[1,1536]{1,0:T(2,128)(2,1)S(1)} %collective-permute-done.11.refs_2_.refs_4_, f32[3,1536]{1,0:T(4,128)S(1)} %copy-done.34, ...), custom_call_target="tpu_custom_call" | custom-call | flops 1000 | bytes 1000 | tf_op jit(solution)/shard_map/pallas_call | solution.py:58
  27.0 6.1 %all-to-all-start = ((bf16[32,16,1536]{2,1,0:T(8,128)(2,1)}), bf16[32,16,1536]{2,1,0:T(8,128)(2,1)S(1)}, u32[]{:S(2)}, u32[]{:S(2)}) async-start(bf16[32,16,1536]{2,1,0:T(8,128)(2,1)} %bitcast.5), calls=%async_computation | async-start | bytes 3145728 | tf_op jit(solution)/shard_map/all_to_all | solution.py:24
  33.4 2.7 collective-permute-start.4
  36.1 13.6 %collective-permute-done.3.refs_1_ = bf16[4,48,384]{2,1,0:T(8,128)(2,1)S(1)} collective-permute-done((bf16[4,48,384]{2,1,0:T(8,128)(2,1)S(1)}, bf16[4,48,384]{2,1,0:T(8,128)(2,1)S(1)}, u32[]{:S(2)}, u32[]{:S(2)}) %collective-permute-start.3) | collective-permute-done | bytes 147488 | tf_op jit(solution)/shard_map/ppermute | solution.py:322
  50.8 2.4 collective-permute-done.5.refs_3_
  54.0 1.6 collective-permute-start.6
  55.6 1.7 collective-permute-start.8
  57.3 13.6 %collective-permute-done.6.refs_1_.refs_2_ = bf16[16,48,384]{2,1,0:T(8,128)(2,1)S(1)} collective-permute-done((bf16[16,48,384]{2,1,0:T(8,128)(2,1)}, bf16[16,48,384]{2,1,0:T(8,128)(2,1)S(1)}, u32[]{:S(2)}, u32[]{:S(2)}) %collective-permute-start.6) | collective-permute-done | bytes 589856 | tf_op jit(solution)/shard_map/ppermute | solution.py:322
  72.3 2.6 shard_map.114.refs_5_
  74.9 9.3 %all-to-all-start.1 = ((bf16[32,16,1536]{2,1,0:T(8,128)(2,1)}), bf16[32,16,1536]{2,1,0:T(8,128)(2,1)}, u32[]{:S(2)}, u32[]{:S(2)}) async-start(bf16[32,16,1536]{2,1,0:T(8,128)(2,1)} %bitcast.7), calls=%async_computation.1 | async-start | bytes 3145728 | tf_op jit(solution)/shard_map/all_to_all | solution.py:24
  84.2 2.8 collective-permute-start.7
  87.0 14.4 %collective-permute-done.7.refs_2_ = bf16[16,48,384]{2,1,0:T(8,128)(2,1)S(1)} collective-permute-done((bf16[16,48,384]{2,1,0:T(8,128)(2,1)}, bf16[16,48,384]{2,1,0:T(8,128)(2,1)S(1)}, u32[]{:S(2)}, u32[]{:S(2)}) %collective-permute-start.7) | collective-permute-done | bytes 589856 | tf_op jit(solution)/shard_map/ppermute | solution.py:322
  105.1 4.5 %collective-permute-done.9.refs_2_ = bf16[4,16,48,384]{3,2,1,0:T(8,128)(2,1)S(1)} collective-permute-done((bf16[4,16,48,384]{3,2,1,0:T(8,128)(2,1)S(1)}, bf16[4,16,48,384]{3,2,1,0:T(8,128)(2,1)S(1)}, u32[]{:S(2)}, u32[]{:S(2)}) %collective-permute-start.9) | collective-permute-done | bytes 2359328 | tf_op jit(solution)/shard_map/ppermute | solution.py:330
  111.2 8.4 %shard_map.115 = (bf16[16,2,48,1536]{3,2,1,0:T(8,128)(2,1)}, f32[512,1536]{1,0:T(8,128)}, bf16[512,1536]{1,0:T(8,128)(2,1)S(1)}) custom-call(bf16[512,1536]{1,0:T(8,128)(2,1)S(1)} %bitcast.21, bf16[4,16,48,384]{3,2,1,0:T(8,128)(2,1)} %copy-done.6, bf16[4,16,48,384]{3,2,1,0:T(8,128)(2,1)} %copy-done.38, bf16[512,1536]{1,0:T(8,128)(2,1)S(1)} %bitcast.27, ...), custom_call_target="tpu_custom_call" | custom-call | flops 1000 | bytes 1000 | tf_op jit(solution)/shard_map/pallas_call | solution.py:58
  121.2 7.2 %all-to-all-start.2 = ((bf16[32,16,1536]{2,1,0:T(8,128)(2,1)}), bf16[32,16,1536]{2,1,0:T(8,128)(2,1)}, u32[]{:S(2)}, u32[]{:S(2)}) async-start(bf16[32,16,1536]{2,1,0:T(8,128)(2,1)} %bitcast.29), calls=%async_computation.2 | async-start | bytes 3145728 | tf_op jit(solution)/shard_map/all_to_all | solution.py:24
  132.7 4.9 %shard_map.116 = (bf16[512,1536]{1,0:T(8,128)(2,1)}, bf16[512,1536]{1,0:T(8,128)(2,1)S(1)}) custom-call(bf16[512,512]{1,0:T(8,128)(2,1)S(1)} %copy-done.13, bf16[512,1536]{1,0:T(8,128)(2,1)} %bitcast.8.refs_1_, f32[512,1536]{1,0:T(8,128)} %get-tuple-element.48.refs_2_, bf16[512,1536]{1,0:T(8,128)(2,1)S(1)} %bitcast.28, ...), custom_call_target="tpu_custom_call" | custom-call | flops 1000 | bytes 1000 | tf_op jit(solution)/shard_map/pallas_call | solution.py:58
  137.5 4.6 %shard_map.118 = (bf16[768,1536]{1,0:T(8,128)(2,1)S(1)}, bf16[768,1536]{1,0:T(8,128)(2,1)}) custom-call(bf16[512,1536]{1,0:T(8,128)(2,1)S(1)} %bitcast.22, bf16[512,1536]{1,0:T(8,128)(2,1)S(1)} %get-tuple-element.53.left_ref.refs_1_), custom_call_target="tpu_custom_call" | custom-call | flops 1000 | bytes 1000 | tf_op jit(solution)/shard_map/pallas_call | solution.py:58
  142.3 4.6 %collective-permute-done.13.other_ref = bf16[768,1536]{1,0:T(8,128)(2,1)S(1)} collective-permute-done((bf16[768,1536]{1,0:T(8,128)(2,1)}, bf16[768,1536]{1,0:T(8,128)(2,1)S(1)}, u32[]{:S(2)}, u32[]{:S(2)}) %collective-permute-start.13) | collective-permute-done | bytes 2359328 | tf_op jit(solution)/shard_map/ppermute | solution.py:330
  148.3 2.7 shard_map.119
  154.1 1.8 collective-permute-start.15
  156.0 5.0 %shard_map.117.refs_2_.refs_3_ = f32[512,1536]{1,0:T(8,128)S(1)} custom-call(bf16[512,1536]{1,0:T(8,128)(2,1)S(1)} %get-tuple-element.53.left_ref.refs_1_, bf16[1536,1536]{1,0:T(8,128)(2,1)} %bitcast.30), custom_call_target="tpu_custom_call" | custom-call | flops 1000 | bytes 1000 | tf_op jit(solution)/shard_map/pallas_call | solution.py:147
  160.9 1.6 copy-done.1
  162.6 6.8 %collective-permute-done.14.refs_3_ = bf16[768,384]{1,0:T(8,128)(2,1)S(1)} collective-permute-done((bf16[768,384]{1,0:T(8,128)(2,1)S(1)}, bf16[768,384]{1,0:T(8,128)(2,1)S(1)}, u32[]{:S(2)}, u32[]{:S(2)}) %collective-permute-start.14) | collective-permute-done | bytes 589856 | tf_op jit(solution)/shard_map/ppermute | solution.py:322
  174.2 3.0 %shard_map.120.refs_3_ = bf16[512,1536]{1,0:T(8,128)(2,1)S(1)} custom-call(bf16[512,512]{1,0:T(8,128)(2,1)S(1)} %copy-done.33, bf16[512,1536]{1,0:T(8,128)(2,1)} %bitcast.11.refs_1_, f32[512,1536]{1,0:T(8,128)} %copy-done.1, bf16[768,384]{1,0:T(8,128)(2,1)S(1)} %copy-done.20, bf16[768,384]{1,0:T(8,128)(2,1)S(1)} %copy-done.23), custom_call_target="tpu_custom_call" | custom-call | flops 1000 | bytes 1000 | tf_op jit(solution)/shard_map/pallas_call | solution.py:58
  178.4 7.7 %all-to-all-start.3 = ((bf16[32,16,1536]{2,1,0:T(8,128)(2,1)}), bf16[32,16,1536]{2,1,0:T(8,128)(2,1)}, u32[]{:S(2)}, u32[]{:S(2)}) async-start(bf16[32,16,1536]{2,1,0:T(8,128)(2,1)} %bitcast.26), calls=%async_computation.3 | async-start | bytes 3145728 | tf_op jit(solution)/shard_map/all_to_all | solution.py:24
  186.1 2.0 collective-permute-start.16
  190.6 4.3 %shard_map.121.refs_5_.refs_3_ = bf16[4,128,128]{2,1,0:T(8,128)(2,1)S(1)} custom-call(bf16[512,512]{1,0:T(8,128)(2,1)S(1)} %copy-done.32, bf16[512,1536]{1,0:T(8,128)(2,1)} %bitcast.11.refs_1_, bf16[512,1536]{1,0:T(8,128)(2,1)S(1)} %bitcast.25, bf16[512,1536]{1,0:T(8,128)(2,1)S(1)} %copy-done.5), custom_call_target="tpu_custom_call" | custom-call | flops 1000 | bytes 1000 | tf_op jit(solution)/shard_map/pallas_call | solution.py:58
  194.9 8.5 %collective-permute-done.16 = bf16[768,384]{1,0:T(8,128)(2,1)} collective-permute-done((bf16[768,384]{1,0:T(8,128)(2,1)}, bf16[768,384]{1,0:T(8,128)(2,1)}, u32[]{:S(2)}, u32[]{:S(2)}) %collective-permute-start.16) | collective-permute-done | bytes 589856 | tf_op jit(solution)/shard_map/ppermute | solution.py:322
  207.3 2.3 collective-permute-start.17
  209.6 9.2 %collective-permute-done.19 = bf16[192,384]{1,0:T(8,128)(2,1)S(1)} collective-permute-done((bf16[192,384]{1,0:T(8,128)(2,1)}, bf16[192,384]{1,0:T(8,128)(2,1)S(1)}, u32[]{:S(2)}, u32[]{:S(2)}) %collective-permute-start.19) | collective-permute-done | bytes 147488 | tf_op jit(solution)/shard_map/ppermute | solution.py:322
  220.5 2.6 all-to-all-done.3
  223.1 4.7 %shard_map.122 = (bf16[512,1536]{1,0:T(8,128)(2,1)S(1)}, bf16[32,4,1536]{2,1,0:T(4,128)(2,1)}) custom-call(bf16[512,512]{1,0:T(8,128)(2,1)S(1)} %copy-done.31, bf16[512,1536]{1,0:T(8,128)(2,1)} %bitcast.14.refs_1_, bf16[512,1536]{1,0:T(8,128)(2,1)S(1)} %bitcast.23, bf16[1,1536]{1,0:T(2,128)(2,1)S(1)} %collective-permute-done.10.refs_1_.refs_3_, ...), custom_call_target="tpu_custom_call" | custom-call | flops 1000 | bytes 1000 | tf_op jit(solution)/shard_map/pallas_call | solution.py:58
  228.9 6.8 %all-to-all-start.4 = ((bf16[32,4,1536]{2,1,0:T(4,128)(2,1)}), bf16[32,4,1536]{2,1,0:T(4,128)(2,1)}, u32[]{:S(2)}, u32[]{:S(2)}) async-start(bf16[32,4,1536]{2,1,0:T(4,128)(2,1)} %get-tuple-element.68), calls=%async_computation.4 | async-start | bytes 786432 | tf_op jit(solution)/shard_map/all_to_all | solution.py:460
  239.7 4.2 %shard_map.124 = (bf16[256,128]{1,0:T(8,128)(2,1)S(1)}, bf16[256,128]{1,0:T(8,128)(2,1)S(1)}, bf16[256,128]{1,0:T(8,128)(2,1)S(1)}, bf16[256,128]{1,0:T(8,128)(2,1)S(1)}) custom-call(bf16[512,512]{1,0:T(8,128)(2,1)S(1)} %copy-done.14, bf16[512,1536]{1,0:T(8,128)(2,1)} %bitcast.14.refs_1_, bf16[512,1536]{1,0:T(8,128)(2,1)} %copy-done.27, ...), custom_call_target="tpu_custom_call" | custom-call | flops 1000 | bytes 1000 | tf_op jit(solution)/shard_map/pallas_call | solution.py:58
  244.9 3.2 %collective-permute-start.24 = (bf16[256,128]{1,0:T(8,128)(2,1)S(1)}, bf16[256,128]{1,0:T(8,128)(2,1)S(1)}, u32[]{:S(2)}, u32[]{:S(2)}) collective-permute-start(bf16[256,128]{1,0:T(8,128)(2,1)S(1)} %get-tuple-element.72), channel_id=1, source_target_pairs={{0,2},{1,3},{2,0},{3,1},{4,6},{5,7},{6,4},{7,5},{8,10},{9,11},{10,... | collective-permute-start | bytes 196616 | tf_op jit(solution)/shard_map/ppermute | solution.py:322
  249.1 2.4 collective-permute-start.21
  253.9 1.6 collective-permute-done.22.refs_3_
  257.6 5.5 %collective-permute-start.26 = (bf16[496,128]{1,0:T(8,128)(2,1)S(1)}, bf16[496,128]{1,0:T(8,128)(2,1)S(1)}, u32[]{:S(2)}, u32[]{:S(2)}) collective-permute-start(bf16[496,128]{1,0:T(8,128)(2,1)S(1)} %shard_map.125.refs_0_), channel_id=1, source_target_pairs={{0,4},{4,0},{1,5},{5,1},{2,6},{6,2},{3,7},{7,3},{8,12},{12,8},{9,1... | collective-permute-start | bytes 380936 | tf_op jit(solution)/shard_map/ppermute | solution.py:330
  263.1 4.8 %collective-permute-done.26.refs_1_ = bf16[496,128]{1,0:T(8,128)(2,1)S(1)} collective-permute-done((bf16[496,128]{1,0:T(8,128)(2,1)S(1)}, bf16[496,128]{1,0:T(8,128)(2,1)S(1)}, u32[]{:S(2)}, u32[]{:S(2)}) %collective-permute-start.26) | collective-permute-done | bytes 127008 | tf_op jit(solution)/shard_map/ppermute | solution.py:330
  268.7 4.1 %all-to-all-start.5 = ((bf16[4,496,128]{2,1,0:T(8,128)(2,1)}), bf16[4,496,128]{2,1,0:T(8,128)(2,1)}, u32[]{:S(2)}, u32[]{:S(2)}) async-start(bf16[4,496,128]{2,1,0:T(8,128)(2,1)} %copy-done.25), calls=%async_computation.5 | async-start | bytes 1015808 | tf_op jit(solution)/shard_map/all_to_all | solution.py:488
  274.3 3.8 %shard_map.123 = bf16[512,1536]{1,0:T(8,128)(2,1)} custom-call(bf16[512,1536]{1,0:T(8,128)(2,1)S(1)} %copy-done.11, bf16[32,4,1536]{2,1,0:T(4,128)(2,1)} %all-to-all-done.4.refs_1_.refs_8_, f32[3,1536]{1,0:T(4,128)S(1)} %copy-done.35, f32[512,1536]{1,0:T(8,128)S(1)} %copy-done.2), custom_call_target="tpu_custom_call" | custom-call | flops 1000 | bytes 1000 | tf_op jit(solution)/shard_map/pallas_call | solution.py:58
  278.0 2.9 %all-to-all-done.5.refs_0_ = bf16[4,496,128]{2,1,0:T(8,128)(2,1)} async-done(((bf16[4,496,128]{2,1,0:T(8,128)(2,1)}), bf16[4,496,128]{2,1,0:T(8,128)(2,1)}, u32[]{:S(2)}, u32[]{:S(2)}) %all-to-all-start.5) | async-done | bytes 507936 | tf_op jit(solution)/shard_map/all_to_all | solution.py:488
  280.9 1.9 shard_map.127
  (138 shorter events, 52.0 us)
Async XLA Ops:
  1.6 19.0 %collective-permute-start = (bf16[48,384]{1,0:T(8,128)(2,1)S(1)}, bf16[48,384]{1,0:T(8,128)(2,1)S(1)}, u32[]{:S(2)}, u32[]{:S(2)}) collective-permute-start(bf16[48,384]{1,0:T(8,128)(2,1)S(1)} %constant_dynamic-slice_fusion.refs_0_.refs_5_), channel_id=1, source_target_pairs={{0,16},{16,32},{32,48},{48,0},{1,17},{17,33},{33,49},{49,1},{2,18}... | collective-permute-start | bytes 110600 | tf_op jit(solution)/shard_map/ppermute | solution.py:322
  3.5 17.1 %collective-permute-start.1 = (bf16[48,384]{1,0:T(8,128)(2,1)S(1)}, bf16[48,384]{1,0:T(8,128)(2,1)S(1)}, u32[]{:S(2)}, u32[]{:S(2)}) collective-permute-start(bf16[48,384]{1,0:T(8,128)(2,1)S(1)} %constant_dynamic-slice_fusion.refs_0_.refs_5_), channel_id=1, source_target_pairs={{0,32},{16,48},{32,0},{48,16},{1,33},{17,49},{33,1},{49,17},{2,34}... | collective-permute-start | bytes 110600 | tf_op jit(solution)/shard_map/ppermute | solution.py:322
  6.7 13.9 %collective-permute-start.2 = (bf16[48,384]{1,0:T(8,128)(2,1)S(1)}, bf16[48,384]{1,0:T(8,128)(2,1)S(1)}, u32[]{:S(2)}, u32[]{:S(2)}) collective-permute-start(bf16[48,384]{1,0:T(8,128)(2,1)S(1)} %constant_dynamic-slice_fusion.refs_0_.refs_5_), channel_id=1, source_target_pairs={{0,48},{16,0},{32,16},{48,32},{1,49},{17,1},{33,17},{49,33},{2,50}... | collective-permute-start | bytes 110600 | tf_op jit(solution)/shard_map/ppermute | solution.py:322
  8.5 12.1 %collective-permute-start.10 = (bf16[1,1536]{1,0:T(2,128)(2,1)S(1)}, bf16[1,1536]{1,0:T(2,128)(2,1)S(1)}, u32[]{:S(2)}, u32[]{:S(2)}) collective-permute-start(bf16[1,1536]{1,0:T(2,128)(2,1)S(1)} %get-tuple-element.79), channel_id=1, source_target_pairs={{0,8},{8,16},{16,24},{24,32},{32,40},{40,48},{48,56},{56,64},{64,7... | collective-permute-start | bytes 9224 | tf_op jit(solution)/shard_map/ppermute | solution.py:337
  10.4 10.1 %collective-permute-start.11 = (bf16[1,1536]{1,0:T(2,128)(2,1)S(1)}, bf16[1,1536]{1,0:T(2,128)(2,1)S(1)}, u32[]{:S(2)}, u32[]{:S(2)}) collective-permute-start(bf16[1,1536]{1,0:T(2,128)(2,1)S(1)} %get-tuple-element.78), channel_id=1, source_target_pairs={{8,0},{16,8},{24,16},{32,24},{40,32},{48,40},{56,48},{64,56},{72,6... | collective-permute-start | bytes 9224 | tf_op jit(solution)/shard_map/ppermute | solution.py:338
  27.0 43.9 %all-to-all-start = ((bf16[32,16,1536]{2,1,0:T(8,128)(2,1)}), bf16[32,16,1536]{2,1,0:T(8,128)(2,1)S(1)}, u32[]{:S(2)}, u32[]{:S(2)}) async-start(bf16[32,16,1536]{2,1,0:T(8,128)(2,1)} %bitcast.5), calls=%async_computation | async-start | bytes 3145728 | tf_op jit(solution)/shard_map/all_to_all | solution.py:24
  33.1 16.6 %collective-permute-start.3 = (bf16[4,48,384]{2,1,0:T(8,128)(2,1)S(1)}, bf16[4,48,384]{2,1,0:T(8,128)(2,1)S(1)}, u32[]{:S(2)}, u32[]{:S(2)}) collective-permute-start(bf16[4,48,384]{2,1,0:T(8,128)(2,1)S(1)} %shard_map.110.refs_0_), channel_id=1, source_target_pairs={{0,64},{64,128},{128,192},{192,0},{1,65},{65,129},{129,193},{193,1... | collective-permute-start | bytes 442376 | tf_op jit(solution)/shard_map/ppermute | solution.py:322
  33.4 17.4 %collective-permute-start.4 = (bf16[4,48,384]{2,1,0:T(8,128)(2,1)S(1)}, bf16[4,48,384]{2,1,0:T(8,128)(2,1)S(1)}, u32[]{:S(2)}, u32[]{:S(2)}) collective-permute-start(bf16[4,48,384]{2,1,0:T(8,128)(2,1)S(1)} %shard_map.110.refs_0_), channel_id=1, source_target_pairs={{0,128},{64,192},{128,0},{192,64},{1,129},{65,193},{129,1},{193,65... | collective-permute-start | bytes 442376 | tf_op jit(solution)/shard_map/ppermute | solution.py:322
  36.1 17.1 %collective-permute-start.5 = (bf16[4,48,384]{2,1,0:T(8,128)(2,1)S(1)}, bf16[4,48,384]{2,1,0:T(8,128)(2,1)S(1)}, u32[]{:S(2)}, u32[]{:S(2)}) collective-permute-start(bf16[4,48,384]{2,1,0:T(8,128)(2,1)S(1)} %shard_map.110.refs_0_), channel_id=1, source_target_pairs={{0,192},{64,0},{128,64},{192,128},{1,193},{65,1},{129,65},{193,129... | collective-permute-start | bytes 442376 | tf_op jit(solution)/shard_map/ppermute | solution.py:322
  54.0 16.8 %collective-permute-start.6 = (bf16[16,48,384]{2,1,0:T(8,128)(2,1)}, bf16[16,48,384]{2,1,0:T(8,128)(2,1)S(1)}, u32[]{:S(2)}, u32[]{:S(2)}) collective-permute-start(bf16[16,48,384]{2,1,0:T(8,128)(2,1)} %bitcast.1.refs_0_), channel_id=1, source_target_pairs={{0,1},{1,2},{2,3},{3,0},{4,5},{5,6},{6,7},{7,4},{8,9},{9,10},{10,1... | collective-permute-start | bytes 1769480 | tf_op jit(solution)/shard_map/ppermute | solution.py:322
  55.6 15.3 %collective-permute-start.8 = (bf16[16,48,384]{2,1,0:T(8,128)(2,1)}, bf16[16,48,384]{2,1,0:T(8,128)(2,1)S(1)}, u32[]{:S(2)}, u32[]{:S(2)}) collective-permute-start(bf16[16,48,384]{2,1,0:T(8,128)(2,1)} %bitcast.1.refs_0_), channel_id=1, source_target_pairs={{0,3},{1,0},{2,1},{3,2},{4,7},{5,4},{6,5},{7,6},{8,11},{9,8},{10,9... | collective-permute-start | bytes 1769480 | tf_op jit(solution)/shard_map/ppermute | solution.py:322
  70.8 4.0 %copy-start.15 = (bf16[16,48,384]{2,1,0:T(8,128)(2,1)}, bf16[16,48,384]{2,1,0:T(8,128)(2,1)S(1)}, u32[]{:S(2)}) copy-start(bf16[16,48,384]{2,1,0:T(8,128)(2,1)S(1)} %collective-permute-done.6.refs_1_.refs_2_) | copy-start | bytes 1769476
  70.9 4.0 %copy-start.17 = (bf16[16,48,384]{2,1,0:T(8,128)(2,1)}, bf16[16,48,384]{2,1,0:T(8,128)(2,1)S(1)}, u32[]{:S(2)}) copy-start(bf16[16,48,384]{2,1,0:T(8,128)(2,1)S(1)} %collective-permute-done.8.refs_3_) | copy-start | bytes 1769476
  74.9 46.3 %all-to-all-start.1 = ((bf16[32,16,1536]{2,1,0:T(8,128)(2,1)}), bf16[32,16,1536]{2,1,0:T(8,128)(2,1)}, u32[]{:S(2)}, u32[]{:S(2)}) async-start(bf16[32,16,1536]{2,1,0:T(8,128)(2,1)} %bitcast.7), calls=%async_computation.1 | async-start | bytes 3145728 | tf_op jit(solution)/shard_map/all_to_all | solution.py:24
  84.2 27.0 %copy-start.3 = (bf16[1,512,1536]{2,1,0:T(8,128)(2,1)S(1)}, bf16[1,512,1536]{2,1,0:T(8,128)(2,1)}, u32[]{:S(2)}) copy-start(bf16[1,512,1536]{2,1,0:T(8,128)(2,1)} %param.6) | copy-start | bytes 4718596
  84.2 26.9 %copy-start.7 = (bf16[1,512,1536]{2,1,0:T(8,128)(2,1)S(1)}, bf16[1,512,1536]{2,1,0:T(8,128)(2,1)}, u32[]{:S(2)}) copy-start(bf16[1,512,1536]{2,1,0:T(8,128)(2,1)} %param.7) | copy-start | bytes 4718596
  84.2 26.9 %copy-start.12 = (bf16[512,512]{1,0:T(8,128)(2,1)S(1)}, bf16[512,512]{1,0:T(8,128)(2,1)}, u32[]{:S(2)}) copy-start(bf16[512,512]{1,0:T(8,128)(2,1)} %get-tuple-element.42.refs_4_.refs_0_) | copy-start | bytes 1572868
  84.2 17.2 %collective-permute-start.7 = (bf16[16,48,384]{2,1,0:T(8,128)(2,1)}, bf16[16,48,384]{2,1,0:T(8,128)(2,1)S(1)}, u32[]{:S(2)}, u32[]{:S(2)}) collective-permute-start(bf16[16,48,384]{2,1,0:T(8,128)(2,1)} %bitcast.1.refs_0_), channel_id=1, source_target_pairs={{0,2},{1,3},{2,0},{3,1},{4,6},{5,7},{6,4},{7,5},{8,10},{9,11},{10,... | collective-permute-start | bytes 1769480 | tf_op jit(solution)/shard_map/ppermute | solution.py:322
  104.8 4.8 %copy-start.6 = (bf16[4,16,48,384]{3,2,1,0:T(8,128)(2,1)}, bf16[4,16,48,384]{3,2,1,0:T(8,128)(2,1)S(1)}, u32[]{:S(2)}) copy-start(bf16[4,16,48,384]{3,2,1,0:T(8,128)(2,1)S(1)} %shard_map.112.refs_1_) | copy-start | bytes 7077892
  104.8 4.8 %collective-permute-start.9 = (bf16[4,16,48,384]{3,2,1,0:T(8,128)(2,1)S(1)}, bf16[4,16,48,384]{3,2,1,0:T(8,128)(2,1)S(1)}, u32[]{:S(2)}, u32[]{:S(2)}) collective-permute-start(bf16[4,16,48,384]{3,2,1,0:T(8,128)(2,1)S(1)} %shard_map.112.refs_1_), channel_id=1, source_target_pairs={{0,8},{8,0},{1,9},{9,1},{2,10},{10,2},{3,11},{11,3},{4,12},{12,4},... | collective-permute-start | bytes 7077896 | tf_op jit(solution)/shard_map/ppermute | solution.py:330
  121.2 49.8 %all-to-all-start.2 = ((bf16[32,16,1536]{2,1,0:T(8,128)(2,1)}), bf16[32,16,1536]{2,1,0:T(8,128)(2,1)}, u32[]{:S(2)}, u32[]{:S(2)}) async-start(bf16[32,16,1536]{2,1,0:T(8,128)(2,1)} %bitcast.29), calls=%async_computation.2 | async-start | bytes 3145728 | tf_op jit(solution)/shard_map/all_to_all | solution.py:24
  129.1 1.2 collective-permute-start.12
  142.2 4.7 %collective-permute-start.13 = (bf16[768,1536]{1,0:T(8,128)(2,1)}, bf16[768,1536]{1,0:T(8,128)(2,1)S(1)}, u32[]{:S(2)}, u32[]{:S(2)}) collective-permute-start(bf16[768,1536]{1,0:T(8,128)(2,1)} %get-tuple-element.56), channel_id=1, source_target_pairs={{0,8},{8,0},{1,9},{9,1},{2,10},{10,2},{3,11},{11,3},{4,12},{12,4},... | collective-permute-start | bytes 7077896 | tf_op jit(solution)/shard_map/ppermute | solution.py:330
  152.7 16.6 %collective-permute-start.14 = (bf16[768,384]{1,0:T(8,128)(2,1)S(1)}, bf16[768,384]{1,0:T(8,128)(2,1)S(1)}, u32[]{:S(2)}, u32[]{:S(2)}) collective-permute-start(bf16[768,384]{1,0:T(8,128)(2,1)S(1)} %get-tuple-element.57), channel_id=1, source_target_pairs={{0,1},{1,2},{2,3},{3,0},{4,5},{5,6},{6,7},{7,4},{8,9},{9,10},{10,1... | collective-permute-start | bytes 1769480 | tf_op jit(solution)/shard_map/ppermute | solution.py:322
  154.1 16.0 %collective-permute-start.15 = (bf16[768,384]{1,0:T(8,128)(2,1)S(1)}, bf16[768,384]{1,0:T(8,128)(2,1)S(1)}, u32[]{:S(2)}, u32[]{:S(2)}) collective-permute-start(bf16[768,384]{1,0:T(8,128)(2,1)S(1)} %get-tuple-element.58), channel_id=1, source_target_pairs={{0,3},{1,0},{2,1},{3,2},{4,7},{5,4},{6,5},{7,6},{8,11},{9,8},{10,9... | collective-permute-start | bytes 1769480 | tf_op jit(solution)/shard_map/ppermute | solution.py:322
  178.4 44.7 %all-to-all-start.3 = ((bf16[32,16,1536]{2,1,0:T(8,128)(2,1)}), bf16[32,16,1536]{2,1,0:T(8,128)(2,1)}, u32[]{:S(2)}, u32[]{:S(2)}) async-start(bf16[32,16,1536]{2,1,0:T(8,128)(2,1)} %bitcast.26), calls=%async_computation.3 | async-start | bytes 3145728 | tf_op jit(solution)/shard_map/all_to_all | solution.py:24
  186.1 17.3 %collective-permute-start.16 = (bf16[768,384]{1,0:T(8,128)(2,1)}, bf16[768,384]{1,0:T(8,128)(2,1)}, u32[]{:S(2)}, u32[]{:S(2)}) collective-permute-start(bf16[768,384]{1,0:T(8,128)(2,1)} %copy-done.37), channel_id=1, source_target_pairs={{0,2},{1,3},{2,0},{3,1},{4,6},{5,7},{6,4},{7,5},{8,10},{9,11},{10,... | collective-permute-start | bytes 1769480 | tf_op jit(solution)/shard_map/ppermute | solution.py:322
  190.6 12.9 %copy-start.21 = (bf16[768,384]{1,0:T(8,128)(2,1)S(1)}, bf16[768,384]{1,0:T(8,128)(2,1)}, u32[]{:S(2)}) copy-start(bf16[768,384]{1,0:T(8,128)(2,1)} %copy-done.19) | copy-start | bytes 1769476
  190.6 12.9 %copy-start.24 = (bf16[768,384]{1,0:T(8,128)(2,1)S(1)}, bf16[768,384]{1,0:T(8,128)(2,1)}, u32[]{:S(2)}) copy-start(bf16[768,384]{1,0:T(8,128)(2,1)} %copy-done.22) | copy-start | bytes 1769476
  190.6 12.9 %copy-start.29 = (bf16[768,384]{1,0:T(8,128)(2,1)S(1)}, bf16[768,384]{1,0:T(8,128)(2,1)}, u32[]{:S(2)}) copy-start(bf16[768,384]{1,0:T(8,128)(2,1)} %copy-done.28) | copy-start | bytes 1769476
  204.8 18.3 %copy-start.31 = (bf16[512,512]{1,0:T(8,128)(2,1)S(1)}, bf16[512,512]{1,0:T(8,128)(2,1)}, u32[]{:S(2)}) copy-start(bf16[512,512]{1,0:T(8,128)(2,1)} %get-tuple-element.50.refs_0_) | copy-start | bytes 1572868
  205.6 13.3 %collective-permute-start.19 = (bf16[192,384]{1,0:T(8,128)(2,1)}, bf16[192,384]{1,0:T(8,128)(2,1)S(1)}, u32[]{:S(2)}, u32[]{:S(2)}) collective-permute-start(bf16[192,384]{1,0:T(8,128)(2,1)} %get-tuple-element.81), channel_id=1, source_target_pairs={{0,192},{64,0},{128,64},{192,128},{1,193},{65,1},{129,65},{193,129... | collective-permute-start | bytes 442376 | tf_op jit(solution)/shard_map/ppermute | solution.py:322
  206.4 12.5 %collective-permute-start.18 = (bf16[192,384]{1,0:T(8,128)(2,1)}, bf16[192,384]{1,0:T(8,128)(2,1)S(1)}, u32[]{:S(2)}, u32[]{:S(2)}) collective-permute-start(bf16[192,384]{1,0:T(8,128)(2,1)} %get-tuple-element.82), channel_id=1, source_target_pairs={{0,128},{64,192},{128,0},{192,64},{1,129},{65,193},{129,1},{193,65... | collective-permute-start | bytes 442376 | tf_op jit(solution)/shard_map/ppermute | solution.py:322
  207.3 11.5 %collective-permute-start.17 = (bf16[192,384]{1,0:T(8,128)(2,1)S(1)}, bf16[192,384]{1,0:T(8,128)(2,1)}, u32[]{:S(2)}, u32[]{:S(2)}) collective-permute-start(bf16[192,384]{1,0:T(8,128)(2,1)S(1)} %get-tuple-element.80), channel_id=1, source_target_pairs={{0,64},{64,128},{128,192},{192,0},{1,65},{65,129},{129,193},{193,1... | collective-permute-start | bytes 442376 | tf_op jit(solution)/shard_map/ppermute | solution.py:322
  228.9 26.6 %all-to-all-start.4 = ((bf16[32,4,1536]{2,1,0:T(4,128)(2,1)}), bf16[32,4,1536]{2,1,0:T(4,128)(2,1)}, u32[]{:S(2)}, u32[]{:S(2)}) async-start(bf16[32,4,1536]{2,1,0:T(4,128)(2,1)} %get-tuple-element.68), calls=%async_computation.4 | async-start | bytes 786432 | tf_op jit(solution)/shard_map/all_to_all | solution.py:460
  235.7 15.8 %collective-permute-start.20 = (bf16[48,384]{1,0:T(8,128)(2,1)S(1)}, bf16[48,384]{1,0:T(8,128)(2,1)S(1)}, u32[]{:S(2)}, u32[]{:S(2)}) collective-permute-start(bf16[48,384]{1,0:T(8,128)(2,1)S(1)} %get-tuple-element.86.refs_6_), channel_id=1, source_target_pairs={{0,16},{16,32},{32,48},{48,0},{1,17},{17,33},{33,49},{49,1},{2,18}... | collective-permute-start | bytes 110600 | tf_op jit(solution)/shard_map/ppermute | solution.py:322
  239.7 9.4 %copy-start.43 = (bf16[48,384]{1,0:T(8,128)(2,1)S(1)}, bf16[48,384]{1,0:T(8,128)(2,1)}, u32[]{:S(2)}) copy-start(bf16[48,384]{1,0:T(8,128)(2,1)} %get-tuple-element.84) | copy-start | bytes 110596
  239.7 11.8 %copy-start.42 = (bf16[48,384]{1,0:T(8,128)(2,1)S(1)}, bf16[48,384]{1,0:T(8,128)(2,1)}, u32[]{:S(2)}) copy-start(bf16[48,384]{1,0:T(8,128)(2,1)} %get-tuple-element.83) | copy-start | bytes 110596
  239.7 33.2 %copy-start.2 = (f32[512,1536]{1,0:T(8,128)S(1)}, f32[512,1536]{1,0:T(8,128)}, u32[]{:S(2)}) copy-start(f32[512,1536]{1,0:T(8,128)} %copy-done.1) | copy-start | bytes 9437188
  244.5 28.3 %copy-start.35 = (f32[3,1536]{1,0:T(4,128)S(1)}, f32[3,1536]{1,0:T(4,128)}, u32[]{:S(2)}) copy-start(f32[3,1536]{1,0:T(4,128)} %refs_2_.1) | copy-start | bytes 55300
  244.5 11.0 %collective-permute-start.23 = (bf16[256,128]{1,0:T(8,128)(2,1)S(1)}, bf16[256,128]{1,0:T(8,128)(2,1)S(1)}, u32[]{:S(2)}, u32[]{:S(2)}) collective-permute-start(bf16[256,128]{1,0:T(8,128)(2,1)S(1)} %get-tuple-element.71), channel_id=1, source_target_pairs={{0,1},{1,2},{2,3},{3,0},{4,5},{5,6},{6,7},{7,4},{8,9},{9,10},{10,1... | collective-permute-start | bytes 196616 | tf_op jit(solution)/shard_map/ppermute | solution.py:322
  244.9 10.6 %collective-permute-start.24 = (bf16[256,128]{1,0:T(8,128)(2,1)S(1)}, bf16[256,128]{1,0:T(8,128)(2,1)S(1)}, u32[]{:S(2)}, u32[]{:S(2)}) collective-permute-start(bf16[256,128]{1,0:T(8,128)(2,1)S(1)} %get-tuple-element.72), channel_id=1, source_target_pairs={{0,2},{1,3},{2,0},{3,1},{4,6},{5,7},{6,4},{7,5},{8,10},{9,11},{10,... | collective-permute-start | bytes 196616 | tf_op jit(solution)/shard_map/ppermute | solution.py:322
  248.1 7.4 %collective-permute-start.25 = (bf16[256,128]{1,0:T(8,128)(2,1)S(1)}, bf16[256,128]{1,0:T(8,128)(2,1)}, u32[]{:S(2)}, u32[]{:S(2)}) collective-permute-start(bf16[256,128]{1,0:T(8,128)(2,1)S(1)} %get-tuple-element.73), channel_id=1, source_target_pairs={{0,3},{1,0},{2,1},{3,2},{4,7},{5,4},{6,5},{7,6},{8,11},{9,8},{10,9... | collective-permute-start | bytes 196616 | tf_op jit(solution)/shard_map/ppermute | solution.py:322
  249.1 4.9 %collective-permute-start.21 = (bf16[48,384]{1,0:T(8,128)(2,1)S(1)}, bf16[48,384]{1,0:T(8,128)(2,1)S(1)}, u32[]{:S(2)}, u32[]{:S(2)}) collective-permute-start(bf16[48,384]{1,0:T(8,128)(2,1)S(1)} %copy-done.43), channel_id=1, source_target_pairs={{0,32},{16,48},{32,0},{48,16},{1,33},{17,49},{33,1},{49,17},{2,34}... | collective-permute-start | bytes 110600 | tf_op jit(solution)/shard_map/ppermute | solution.py:322
  251.4 4.1 %copy-start.44 = (bf16[48,384]{1,0:T(8,128)(2,1)}, bf16[48,384]{1,0:T(8,128)(2,1)S(1)}, u32[]{:S(2)}) copy-start(bf16[48,384]{1,0:T(8,128)(2,1)S(1)} %collective-permute-done.20.refs_1_) | copy-start | bytes 110596
  251.5 4.0 %collective-permute-start.22 = (bf16[48,384]{1,0:T(8,128)(2,1)S(1)}, bf16[48,384]{1,0:T(8,128)(2,1)S(1)}, u32[]{:S(2)}, u32[]{:S(2)}) collective-permute-start(bf16[48,384]{1,0:T(8,128)(2,1)S(1)} %copy-done.42), channel_id=1, source_target_pairs={{0,48},{16,0},{32,16},{48,32},{1,49},{17,1},{33,17},{49,33},{2,50}... | collective-permute-start | bytes 110600 | tf_op jit(solution)/shard_map/ppermute | solution.py:322
  257.6 10.3 %collective-permute-start.26 = (bf16[496,128]{1,0:T(8,128)(2,1)S(1)}, bf16[496,128]{1,0:T(8,128)(2,1)S(1)}, u32[]{:S(2)}, u32[]{:S(2)}) collective-permute-start(bf16[496,128]{1,0:T(8,128)(2,1)S(1)} %shard_map.125.refs_0_), channel_id=1, source_target_pairs={{0,4},{4,0},{1,5},{5,1},{2,6},{6,2},{3,7},{7,3},{8,12},{12,8},{9,1... | collective-permute-start | bytes 380936 | tf_op jit(solution)/shard_map/ppermute | solution.py:330
  268.7 12.2 %all-to-all-start.5 = ((bf16[4,496,128]{2,1,0:T(8,128)(2,1)}), bf16[4,496,128]{2,1,0:T(8,128)(2,1)}, u32[]{:S(2)}, u32[]{:S(2)}) async-start(bf16[4,496,128]{2,1,0:T(8,128)(2,1)} %copy-done.25), calls=%async_computation.5 | async-start | bytes 1015808 | tf_op jit(solution)/shard_map/all_to_all | solution.py:488
  (32 other events, 34.6 us)

commit v2 on v1

--- a/solution.py
+++ b/solution.py
@@ -46,10 +46,6 @@
             return pl.BlockSpec((*shape[:-1], step), lambda k: (*zeros, k))
         return pl.BlockSpec(shape, lambda k: (*zeros, 0))
 
-    def corner(shape):
-        zeros = (0,) * len(shape)
-        return pl.BlockSpec((*[1] * (len(shape) - 2), 16, 128), lambda k: zeros)
-
     count = len(operands)
 
     def body(*refs):
@@ -59,7 +55,7 @@
         body,
         grid=(width // step if step else 1,),
         in_specs=[spec(one.shape, whole.get(k, False)) for k, one in enumerate(operands)]
-        + [corner(one.shape) for one in needs],
+        + [pl.BlockSpec(memory_space=pl.ANY)] * len(needs),
         out_specs=[spec(one.shape) for one in outputs],
         out_shape=[pltpu.HBM(one.shape, one.dtype) if k in kept else one for k, one in enumerate(outputs)],
         scratch_shapes=scratch,
@@ -67,7 +63,7 @@
         compiler_params=pltpu.CompilerParams(vmem_limit_bytes=ROOM),
     )(
         *[pltpu.with_memory_space_constraint(one, pltpu.HBM) if k in stay else one for k, one in enumerate(operands)],
-        *needs,
+        *[pltpu.with_memory_space_constraint(one, pltpu.HBM) for one in needs],
     )
 
 
@@ -389,13 +385,14 @@
         [features, tok_before, tok_after, conv_weight, lead],
         [wide, wide],
         needs=near,
+        kept=[1],
         stay=[0],
         step=512,
     )
     columns = exchange(send)
     near = place(ring(place(near, "z_lo"), "x"), "x").reshape(x_count * z_count, own, share)
     near = ring(near, "y")
-    (send,) = on_device(mix_kernel, [trail, columns], [wide], needs=[near[1], near[-1]], step=512)
+    (send,) = on_device(mix_kernel, [trail, columns], [wide], needs=[near[1], near[-1]], kept=[0], step=512)
     second_out = exchange(send)
     near = place(near, "y")
     far = swap(near, "core")
@@ -405,6 +402,7 @@
         [features, near, far, grad_out, to_position],
         [like((x_count * z_count, 2, own, width)), like((rows, width), F32), wide],
         needs=[send],
+        kept=[2],
         step=share,
         whole={0: True, 1: None, 2: None},
     )
@@ -435,6 +433,7 @@
         [trail_back, delta],
         [wide],
         needs=[gate_back, arrived[1], arrived[-1]],
+        kept=[0],
         step=512,
     )
     d_first = exchange(send)
@@ -455,6 +454,7 @@
         [lead_back, d_first, features, tok_before, tok_after],
         [wide, like((owners, conv_weight.shape[0] + 1, width))],
         needs=[grad_second, pieces[1]],
+        kept=[0, 1],
         step=512,
     )
     spread = lax.all_to_all(spread, SEQ, split_axis=0, concat_axis=0, tiled=True)

time: 285 us -> 280 us (0.982)
  local copies, waits for them, and re-layouts: 34.6 us -> 26.3 us
  waiting for transfers between devices: 93.1 us -> 96.5 us
    unnamed x94 -> x98, local copies, waits for them, and re-layouts: 31.7 us -> 23.4 us
  transfers between devices with their start and end apart: 33 -> 33, of which waited for: 17 -> 17; matrix products, arithmetic and copies ran while one was open for 2% -> 2% of each run, Pallas kernels for 15% -> 16%
where the time goes in v2:
time: 280 us; the launch traced here: 278 us
  waiting for transfers between devices  96.5 us (34%)
  starting transfers between devices  90.1 us (32%)
  Pallas kernels  62.6 us (22%)
  local copies, waits for them, and re-layouts  26.3 us (9%)
    ppermute x21, waiting for transfers between devices, shift(): lax.ppermute(values, axis, [(i, (i + step) % count) for i in range(count)])  73.3 us
    pallas_call x17, Pallas kernels, on_device(): pl.pallas_call(body, grid=(width // step if step else 1,), in_specs=[spec...  54.9 us
    ppermute x21, starting transfers between devices, shift(): lax.ppermute(values, axis, [(i, (i + step) % count) for i in range(count)])  34.7 us
    all_to_all x4, starting transfers between devices, exchange(): lax.all_to_all(cut, SEQ, split_axis=0, concat_axis=0, tiled=True)  30.1 us
    unnamed x98, local copies, waits for them, and re-layouts  23.4 us
    ppermute x4, waiting for transfers between devices, swap(): return lax.ppermute(values, axis, [(0, 1), (1, 0)])  14.9 us
    all_to_all x1, starting transfers between devices, shards(): lax.all_to_all(spread, SEQ, split_axis=0, concat_axis=0, tiled=True)  6.76 us
    ppermute x1, starting transfers between devices, halo_rows(): after = lax.ppermute(first, SEQ, down)  6.34 us
  transfers between devices with their start and end apart: 33, of which 17 were waited for; matrix products, arithmetic and copies ran while one was open for 2% of the time, Pallas kernels for 16%

profile of v2, /device:TPU:6, one launch (start us, length us, event | category | flops | bytes accessed | tf_op | source)
XLA Modules:
  0.0 278.2 jit_solution(10938897617954499006)
XLA Ops:
  1.6 1.9 collective-permute-start
  3.5 3.3 %collective-permute-start.1 = (bf16[48,384]{1,0:T(8,128)(2,1)S(1)}, bf16[48,384]{1,0:T(8,128)(2,1)S(1)}, u32[]{:S(2)}, u32[]{:S(2)}) collective-permute-start(bf16[48,384]{1,0:T(8,128)(2,1)S(1)} %constant_dynamic-slice_fusion.refs_0_.refs_5_), channel_id=1, source_target_pairs={{0,32},{16,48},{32,0},{48,16},{1,33},{17,49},{33,1},{49,17},{2,34}... | collective-permute-start | bytes 110600 | tf_op jit(solution)/shard_map/ppermute | solution.py:318
  8.5 1.9 collective-permute-start.10
  10.5 6.3 %collective-permute-start.11 = (bf16[1,1536]{1,0:T(2,128)(2,1)S(1)}, bf16[1,1536]{1,0:T(2,128)(2,1)S(1)}, u32[]{:S(2)}, u32[]{:S(2)}) collective-permute-start(bf16[1,1536]{1,0:T(2,128)(2,1)S(1)} %get-tuple-element.78), channel_id=1, source_target_pairs={{8,0},{16,8},{24,16},{32,24},{40,32},{48,40},{56,48},{64,56},{72,6... | collective-permute-start | bytes 9224 | tf_op jit(solution)/shard_map/ppermute | solution.py:334
  16.8 3.8 %shard_map.109 = (bf16[512,512]{1,0:T(8,128)(2,1)S(1)}, bf16[512,512]{1,0:T(8,128)(2,1)}, bf16[512,512]{1,0:T(8,128)(2,1)}, bf16[512,512]{1,0:T(8,128)(2,1)}, bf...) custom-call(bf16[4,128,128]{2,1,0:T(8,128)(2,1)} %refs_0_.1, bf16[4,128,128]{2,1,0:T(8,128)(2,1)} %refs_1_.1), custom_call_target="tpu_custom_call" | custom-call | flops 1000 | bytes 1000 | tf_op jit(solution)/shard_map/pallas_call | solution.py:54
  22.0 4.5 %shard_map.113 = (bf16[512,1536]{1,0:T(8,128)(2,1)S(1)}, bf16[512,1536]{1,0:T(8,128)(2,1)}) custom-call(bf16[512,1536]{1,0:T(8,128)(2,1)} %bitcast.20, bf16[1,1536]{1,0:T(2,128)(2,1)S(1)} %collective-permute-done.10.refs_1_.refs_3_, bf16[1,1536]{1,0:T(2,128)(2,1)S(1)} %collective-permute-done.11.refs_2_.refs_4_, f32[3,1536]{1,0:T(4,128)S(1)} %copy-done.32, ...), custom_call_target="tpu_custom_call" | custom-call | flops 1000 | bytes 1000 | tf_op jit(solution)/shard_map/pallas_call | solution.py:54
  27.8 6.2 %all-to-all-start = ((bf16[32,16,1536]{2,1,0:T(8,128)(2,1)}), bf16[32,16,1536]{2,1,0:T(8,128)(2,1)S(1)}, u32[]{:S(2)}, u32[]{:S(2)}) async-start(bf16[32,16,1536]{2,1,0:T(8,128)(2,1)} %bitcast.32), calls=%async_computation | async-start | bytes 3145728 | tf_op jit(solution)/shard_map/all_to_all | solution.py:24
  34.3 2.7 collective-permute-start.4
  37.0 13.6 %collective-permute-done.3.refs_1_ = bf16[4,48,384]{2,1,0:T(8,128)(2,1)S(1)} collective-permute-done((bf16[4,48,384]{2,1,0:T(8,128)(2,1)S(1)}, bf16[4,48,384]{2,1,0:T(8,128)(2,1)S(1)}, u32[]{:S(2)}, u32[]{:S(2)}) %collective-permute-start.3) | collective-permute-done | bytes 147488 | tf_op jit(solution)/shard_map/ppermute | solution.py:318
  51.7 2.4 collective-permute-done.5.refs_3_
  54.9 1.6 collective-permute-start.6
  56.5 1.7 collective-permute-start.8
  58.2 13.6 %collective-permute-done.6.refs_1_.refs_2_ = bf16[16,48,384]{2,1,0:T(8,128)(2,1)S(1)} collective-permute-done((bf16[16,48,384]{2,1,0:T(8,128)(2,1)}, bf16[16,48,384]{2,1,0:T(8,128)(2,1)S(1)}, u32[]{:S(2)}, u32[]{:S(2)}) %collective-permute-start.6) | collective-permute-done | bytes 589856 | tf_op jit(solution)/shard_map/ppermute | solution.py:318
  73.8 2.6 shard_map.114.refs_5_
  76.4 9.3 %all-to-all-start.1 = ((bf16[32,16,1536]{2,1,0:T(8,128)(2,1)}), bf16[32,16,1536]{2,1,0:T(8,128)(2,1)}, u32[]{:S(2)}, u32[]{:S(2)}) async-start(bf16[32,16,1536]{2,1,0:T(8,128)(2,1)} %bitcast.28), calls=%async_computation.1 | async-start | bytes 3145728 | tf_op jit(solution)/shard_map/all_to_all | solution.py:24
  85.7 2.8 %collective-permute-start.7 = (bf16[16,48,384]{2,1,0:T(8,128)(2,1)}, bf16[16,48,384]{2,1,0:T(8,128)(2,1)S(1)}, u32[]{:S(2)}, u32[]{:S(2)}) collective-permute-start(bf16[16,48,384]{2,1,0:T(8,128)(2,1)} %bitcast.1.refs_0_), channel_id=1, source_target_pairs={{0,2},{1,3},{2,0},{3,1},{4,6},{5,7},{6,4},{7,5},{8,10},{9,11},{10,... | collective-permute-start | bytes 1769480 | tf_op jit(solution)/shard_map/ppermute | solution.py:318
  88.5 14.4 %collective-permute-done.7.refs_2_ = bf16[16,48,384]{2,1,0:T(8,128)(2,1)S(1)} collective-permute-done((bf16[16,48,384]{2,1,0:T(8,128)(2,1)}, bf16[16,48,384]{2,1,0:T(8,128)(2,1)S(1)}, u32[]{:S(2)}, u32[]{:S(2)}) %collective-permute-start.7) | collective-permute-done | bytes 589856 | tf_op jit(solution)/shard_map/ppermute | solution.py:318
  106.6 4.5 %collective-permute-done.9.refs_2_ = bf16[4,16,48,384]{3,2,1,0:T(8,128)(2,1)S(1)} collective-permute-done((bf16[4,16,48,384]{3,2,1,0:T(8,128)(2,1)S(1)}, bf16[4,16,48,384]{3,2,1,0:T(8,128)(2,1)S(1)}, u32[]{:S(2)}, u32[]{:S(2)}) %collective-permute-start.9) | collective-permute-done | bytes 2359328 | tf_op jit(solution)/shard_map/ppermute | solution.py:326
  112.5 8.2 %shard_map.115 = (bf16[16,2,48,1536]{3,2,1,0:T(8,128)(2,1)}, f32[512,1536]{1,0:T(8,128)}, bf16[512,1536]{1,0:T(8,128)(2,1)}) custom-call(bf16[512,1536]{1,0:T(8,128)(2,1)S(1)} %bitcast.21, bf16[4,16,48,384]{3,2,1,0:T(8,128)(2,1)S(1)} %shard_map.112.refs_1_, bf16[4,16,48,384]{3,2,1,0:T(8,128)(2,1)} %copy-done.36, bf16[512,1536]{1,0:T(8,128)(2,1)S(1)} %bitcast.26, ...), custom_call_target="tpu_custom_call" | custom-call | flops 1000 | bytes 1000 | tf_op jit(solution)/shard_map/pallas_call | solution.py:54
  120.7 2.0 all-to-all-done.1
  122.7 6.9 %all-to-all-start.2 = ((bf16[32,16,1536]{2,1,0:T(8,128)(2,1)}), bf16[32,16,1536]{2,1,0:T(8,128)(2,1)}, u32[]{:S(2)}, u32[]{:S(2)}) async-start(bf16[32,16,1536]{2,1,0:T(8,128)(2,1)} %bitcast.31), calls=%async_computation.2 | async-start | bytes 3145728 | tf_op jit(solution)/shard_map/all_to_all | solution.py:24
  134.5 4.9 %shard_map.116 = (bf16[512,1536]{1,0:T(8,128)(2,1)}, bf16[512,1536]{1,0:T(8,128)(2,1)S(1)}) custom-call(bf16[512,512]{1,0:T(8,128)(2,1)S(1)} %copy-done.8, bf16[512,1536]{1,0:T(8,128)(2,1)} %bitcast.8.refs_1_, f32[512,1536]{1,0:T(8,128)} %get-tuple-element.48.refs_2_, bf16[512,1536]{1,0:T(8,128)(2,1)S(1)} %bitcast.27, bf16[16,128]{1,0:T(8,128)(2,1)} %copy-done.48), custom_call_target="tpu_custom_call" | custom-call | flops 1000 | bytes 1000 | tf_op jit(solution)/shard_map/pallas_call | solution.py:54
  139.3 4.6 %shard_map.118 = (bf16[768,1536]{1,0:T(8,128)(2,1)S(1)}, bf16[768,1536]{1,0:T(8,128)(2,1)}) custom-call(bf16[512,1536]{1,0:T(8,128)(2,1)S(1)} %bitcast.22, bf16[512,1536]{1,0:T(8,128)(2,1)S(1)} %get-tuple-element.53.left_ref.refs_1_), custom_call_target="tpu_custom_call" | custom-call | flops 1000 | bytes 1000 | tf_op jit(solution)/shard_map/pallas_call | solution.py:54
  144.1 4.6 %collective-permute-done.13.other_ref = bf16[768,1536]{1,0:T(8,128)(2,1)S(1)} collective-permute-done((bf16[768,1536]{1,0:T(8,128)(2,1)}, bf16[768,1536]{1,0:T(8,128)(2,1)S(1)}, u32[]{:S(2)}, u32[]{:S(2)}) %collective-permute-start.13) | collective-permute-done | bytes 2359328 | tf_op jit(solution)/shard_map/ppermute | solution.py:326
  150.1 2.7 shard_map.119
  155.1 1.8 collective-permute-start.15
  156.9 5.0 %shard_map.117.refs_2_.refs_3_ = f32[512,1536]{1,0:T(8,128)S(1)} custom-call(bf16[512,1536]{1,0:T(8,128)(2,1)S(1)} %get-tuple-element.53.left_ref.refs_1_, bf16[1536,1536]{1,0:T(8,128)(2,1)} %bitcast.30), custom_call_target="tpu_custom_call" | custom-call | flops 1000 | bytes 1000 | tf_op jit(solution)/shard_map/pallas_call | solution.py:143
  161.9 1.6 copy-done.1
  163.5 6.8 %collective-permute-done.14.refs_3_ = bf16[768,384]{1,0:T(8,128)(2,1)S(1)} collective-permute-done((bf16[768,384]{1,0:T(8,128)(2,1)S(1)}, bf16[768,384]{1,0:T(8,128)(2,1)S(1)}, u32[]{:S(2)}, u32[]{:S(2)}) %collective-permute-start.14) | collective-permute-done | bytes 589856 | tf_op jit(solution)/shard_map/ppermute | solution.py:318
  172.1 4.0 %shard_map.120.refs_3_ = bf16[512,1536]{1,0:T(8,128)(2,1)} custom-call(bf16[512,512]{1,0:T(8,128)(2,1)S(1)} %copy-done.23, bf16[512,1536]{1,0:T(8,128)(2,1)} %bitcast.11.refs_1_, f32[512,1536]{1,0:T(8,128)} %copy-done.1, bf16[768,384]{1,0:T(8,128)(2,1)} %copy-done.38, bf16[768,384]{1,0:T(8,128)(2,1)} %collective-permute-done.15.refs_4_), custom_call_target="tpu_custom_call" | custom-call | flops 1000 | bytes 1000 | tf_op jit(solution)/shard_map/pallas_call | solution.py:54
  176.1 7.7 %all-to-all-start.3 = ((bf16[32,16,1536]{2,1,0:T(8,128)(2,1)}), bf16[32,16,1536]{2,1,0:T(8,128)(2,1)}, u32[]{:S(2)}, u32[]{:S(2)}) async-start(bf16[32,16,1536]{2,1,0:T(8,128)(2,1)} %bitcast.29), calls=%async_computation.3 | async-start | bytes 3145728 | tf_op jit(solution)/shard_map/all_to_all | solution.py:24
  183.8 2.1 collective-permute-start.16
  187.0 4.3 %shard_map.121.refs_5_.refs_3_ = bf16[4,128,128]{2,1,0:T(8,128)(2,1)S(1)} custom-call(bf16[512,512]{1,0:T(8,128)(2,1)S(1)} %copy-done.22, bf16[512,1536]{1,0:T(8,128)(2,1)} %bitcast.11.refs_1_, bf16[512,1536]{1,0:T(8,128)(2,1)S(1)} %bitcast.25, bf16[512,1536]{1,0:T(8,128)(2,1)} %shard_map.120.refs_3_), custom_call_target="tpu_custom_call" | custom-call | flops 1000 | bytes 1000 | tf_op jit(solution)/shard_map/pallas_call | solution.py:54
  191.3 9.8 %collective-permute-done.16 = bf16[768,384]{1,0:T(8,128)(2,1)} collective-permute-done((bf16[768,384]{1,0:T(8,128)(2,1)}, bf16[768,384]{1,0:T(8,128)(2,1)}, u32[]{:S(2)}, u32[]{:S(2)}) %collective-permute-start.16) | collective-permute-done | bytes 589856 | tf_op jit(solution)/shard_map/ppermute | solution.py:318
  205.2 2.3 collective-permute-start.17
  207.5 9.1 %collective-permute-done.19 = bf16[192,384]{1,0:T(8,128)(2,1)S(1)} collective-permute-done((bf16[192,384]{1,0:T(8,128)(2,1)}, bf16[192,384]{1,0:T(8,128)(2,1)S(1)}, u32[]{:S(2)}, u32[]{:S(2)}) %collective-permute-start.19) | collective-permute-done | bytes 147488 | tf_op jit(solution)/shard_map/ppermute | solution.py:318
  217.4 3.5 %all-to-all-done.3 = bf16[32,16,1536]{2,1,0:T(8,128)(2,1)} async-done(((bf16[32,16,1536]{2,1,0:T(8,128)(2,1)}), bf16[32,16,1536]{2,1,0:T(8,128)(2,1)}, u32[]{:S(2)}, u32[]{:S(2)}) %all-to-all-start.3) | async-done | bytes 1572896 | tf_op jit(solution)/shard_map/all_to_all | solution.py:24
  220.8 4.7 %shard_map.122 = (bf16[512,1536]{1,0:T(8,128)(2,1)}, bf16[32,4,1536]{2,1,0:T(4,128)(2,1)}) custom-call(bf16[512,512]{1,0:T(8,128)(2,1)S(1)} %copy-done.21, bf16[512,1536]{1,0:T(8,128)(2,1)} %bitcast.14.refs_1_, bf16[512,1536]{1,0:T(8,128)(2,1)S(1)} %bitcast.23, bf16[1,1536]{1,0:T(2,128)(2,1)S(1)} %collective-permute-done.10.refs_1_.refs_3_, ...), custom_call_target="tpu_custom_call" | custom-call | flops 1000 | bytes 1000 | tf_op jit(solution)/shard_map/pallas_call | solution.py:54
  225.5 6.8 %all-to-all-start.4 = ((bf16[32,4,1536]{2,1,0:T(4,128)(2,1)}), bf16[32,4,1536]{2,1,0:T(4,128)(2,1)}, u32[]{:S(2)}, u32[]{:S(2)}) async-start(bf16[32,4,1536]{2,1,0:T(4,128)(2,1)} %get-tuple-element.68), calls=%async_computation.4 | async-start | bytes 786432 | tf_op jit(solution)/shard_map/all_to_all | solution.py:460
  234.9 4.2 %shard_map.124 = (bf16[256,128]{1,0:T(8,128)(2,1)S(1)}, bf16[256,128]{1,0:T(8,128)(2,1)S(1)}, bf16[256,128]{1,0:T(8,128)(2,1)S(1)}, bf16[256,128]{1,0:T(8,128)(2,1)S(1)}) custom-call(bf16[512,512]{1,0:T(8,128)(2,1)S(1)} %copy-done.9, bf16[512,1536]{1,0:T(8,128)(2,1)} %bitcast.14.refs_1_, bf16[512,1536]{1,0:T(8,128)(2,1)} %copy-done.15, ...), custom_call_target="tpu_custom_call" | custom-call | flops 1000 | bytes 1000 | tf_op jit(solution)/shard_map/pallas_call | solution.py:54
  240.2 3.2 %collective-permute-start.24 = (bf16[256,128]{1,0:T(8,128)(2,1)S(1)}, bf16[256,128]{1,0:T(8,128)(2,1)S(1)}, u32[]{:S(2)}, u32[]{:S(2)}) collective-permute-start(bf16[256,128]{1,0:T(8,128)(2,1)S(1)} %get-tuple-element.72), channel_id=1, source_target_pairs={{0,2},{1,3},{2,0},{3,1},{4,6},{5,7},{6,4},{7,5},{8,10},{9,11},{10,... | collective-permute-start | bytes 196616 | tf_op jit(solution)/shard_map/ppermute | solution.py:318
  244.4 2.4 collective-permute-start.21
  252.9 5.5 %collective-permute-start.26 = (bf16[496,128]{1,0:T(8,128)(2,1)S(1)}, bf16[496,128]{1,0:T(8,128)(2,1)S(1)}, u32[]{:S(2)}, u32[]{:S(2)}) collective-permute-start(bf16[496,128]{1,0:T(8,128)(2,1)S(1)} %shard_map.125.refs_0_), channel_id=1, source_target_pairs={{0,4},{4,0},{1,5},{5,1},{2,6},{6,2},{3,7},{7,3},{8,12},{12,8},{9,1... | collective-permute-start | bytes 380936 | tf_op jit(solution)/shard_map/ppermute | solution.py:326
  258.4 4.8 %collective-permute-done.26.refs_1_ = bf16[496,128]{1,0:T(8,128)(2,1)S(1)} collective-permute-done((bf16[496,128]{1,0:T(8,128)(2,1)S(1)}, bf16[496,128]{1,0:T(8,128)(2,1)S(1)}, u32[]{:S(2)}, u32[]{:S(2)}) %collective-permute-start.26) | collective-permute-done | bytes 127008 | tf_op jit(solution)/shard_map/ppermute | solution.py:326
  264.0 4.1 %all-to-all-start.5 = ((bf16[4,496,128]{2,1,0:T(8,128)(2,1)}), bf16[4,496,128]{2,1,0:T(8,128)(2,1)}, u32[]{:S(2)}, u32[]{:S(2)}) async-start(bf16[4,496,128]{2,1,0:T(8,128)(2,1)} %copy-done.14), calls=%async_computation.5 | async-start | bytes 1015808 | tf_op jit(solution)/shard_map/all_to_all | solution.py:488
  269.6 3.8 %shard_map.123 = bf16[512,1536]{1,0:T(8,128)(2,1)} custom-call(bf16[512,1536]{1,0:T(8,128)(2,1)S(1)} %copy-done.6, bf16[32,4,1536]{2,1,0:T(4,128)(2,1)} %all-to-all-done.4.refs_1_.refs_8_, f32[3,1536]{1,0:T(4,128)S(1)} %copy-done.33, f32[512,1536]{1,0:T(8,128)S(1)} %copy-done.2), custom_call_target="tpu_custom_call" | custom-call | flops 1000 | bytes 1000 | tf_op jit(solution)/shard_map/pallas_call | solution.py:54
  273.3 2.9 %all-to-all-done.5.refs_0_ = bf16[4,496,128]{2,1,0:T(8,128)(2,1)} async-done(((bf16[4,496,128]{2,1,0:T(8,128)(2,1)}), bf16[4,496,128]{2,1,0:T(8,128)(2,1)}, u32[]{:S(2)}, u32[]{:S(2)}) %all-to-all-start.5) | async-done | bytes 507936 | tf_op jit(solution)/shard_map/all_to_all | solution.py:488
  276.2 1.9 shard_map.127
  (142 shorter events, 44.3 us)
Async XLA Ops:
  1.6 19.1 %copy-start.24 = (bf16[48,384]{1,0:T(8,128)(2,1)}, bf16[48,384]{1,0:T(8,128)(2,1)S(1)}, u32[]{:S(2)}) copy-start(bf16[48,384]{1,0:T(8,128)(2,1)S(1)} %constant_dynamic-slice_fusion.refs_0_.refs_5_) | copy-start | bytes 110596
  1.6 19.1 %collective-permute-start = (bf16[48,384]{1,0:T(8,128)(2,1)S(1)}, bf16[48,384]{1,0:T(8,128)(2,1)S(1)}, u32[]{:S(2)}, u32[]{:S(2)}) collective-permute-start(bf16[48,384]{1,0:T(8,128)(2,1)S(1)} %constant_dynamic-slice_fusion.refs_0_.refs_5_), channel_id=1, source_target_pairs={{0,16},{16,32},{32,48},{48,0},{1,17},{17,33},{33,49},{49,1},{2,18}... | collective-permute-start | bytes 110600 | tf_op jit(solution)/shard_map/ppermute | solution.py:318
  3.5 17.2 %collective-permute-start.1 = (bf16[48,384]{1,0:T(8,128)(2,1)S(1)}, bf16[48,384]{1,0:T(8,128)(2,1)S(1)}, u32[]{:S(2)}, u32[]{:S(2)}) collective-permute-start(bf16[48,384]{1,0:T(8,128)(2,1)S(1)} %constant_dynamic-slice_fusion.refs_0_.refs_5_), channel_id=1, source_target_pairs={{0,32},{16,48},{32,0},{48,16},{1,33},{17,49},{33,1},{49,17},{2,34}... | collective-permute-start | bytes 110600 | tf_op jit(solution)/shard_map/ppermute | solution.py:318
  6.7 13.9 %collective-permute-start.2 = (bf16[48,384]{1,0:T(8,128)(2,1)S(1)}, bf16[48,384]{1,0:T(8,128)(2,1)S(1)}, u32[]{:S(2)}, u32[]{:S(2)}) collective-permute-start(bf16[48,384]{1,0:T(8,128)(2,1)S(1)} %constant_dynamic-slice_fusion.refs_0_.refs_5_), channel_id=1, source_target_pairs={{0,48},{16,0},{32,16},{48,32},{1,49},{17,1},{33,17},{49,33},{2,50}... | collective-permute-start | bytes 110600 | tf_op jit(solution)/shard_map/ppermute | solution.py:318
  8.5 12.1 %collective-permute-start.10 = (bf16[1,1536]{1,0:T(2,128)(2,1)S(1)}, bf16[1,1536]{1,0:T(2,128)(2,1)S(1)}, u32[]{:S(2)}, u32[]{:S(2)}) collective-permute-start(bf16[1,1536]{1,0:T(2,128)(2,1)S(1)} %get-tuple-element.79), channel_id=1, source_target_pairs={{0,8},{8,16},{16,24},{24,32},{32,40},{40,48},{48,56},{56,64},{64,7... | collective-permute-start | bytes 9224 | tf_op jit(solution)/shard_map/ppermute | solution.py:333
  10.5 10.2 %collective-permute-start.11 = (bf16[1,1536]{1,0:T(2,128)(2,1)S(1)}, bf16[1,1536]{1,0:T(2,128)(2,1)S(1)}, u32[]{:S(2)}, u32[]{:S(2)}) collective-permute-start(bf16[1,1536]{1,0:T(2,128)(2,1)S(1)} %get-tuple-element.78), channel_id=1, source_target_pairs={{8,0},{16,8},{24,16},{32,24},{40,32},{48,40},{56,48},{64,56},{72,6... | collective-permute-start | bytes 9224 | tf_op jit(solution)/shard_map/ppermute | solution.py:334
  27.8 6.2 %copy-start.31 = (bf16[48,384]{1,0:T(8,128)(2,1)S(1)}, bf16[48,384]{1,0:T(8,128)(2,1)}, u32[]{:S(2)}) copy-start(bf16[48,384]{1,0:T(8,128)(2,1)} %copy-done.30) | copy-start | bytes 110596
  27.8 44.0 %all-to-all-start = ((bf16[32,16,1536]{2,1,0:T(8,128)(2,1)}), bf16[32,16,1536]{2,1,0:T(8,128)(2,1)S(1)}, u32[]{:S(2)}, u32[]{:S(2)}) async-start(bf16[32,16,1536]{2,1,0:T(8,128)(2,1)} %bitcast.32), calls=%async_computation | async-start | bytes 3145728 | tf_op jit(solution)/shard_map/all_to_all | solution.py:24
  34.0 16.5 %collective-permute-start.3 = (bf16[4,48,384]{2,1,0:T(8,128)(2,1)S(1)}, bf16[4,48,384]{2,1,0:T(8,128)(2,1)S(1)}, u32[]{:S(2)}, u32[]{:S(2)}) collective-permute-start(bf16[4,48,384]{2,1,0:T(8,128)(2,1)S(1)} %shard_map.110.refs_0_), channel_id=1, source_target_pairs={{0,64},{64,128},{128,192},{192,0},{1,65},{65,129},{129,193},{193,1... | collective-permute-start | bytes 442376 | tf_op jit(solution)/shard_map/ppermute | solution.py:318
  34.3 17.4 %collective-permute-start.4 = (bf16[4,48,384]{2,1,0:T(8,128)(2,1)S(1)}, bf16[4,48,384]{2,1,0:T(8,128)(2,1)S(1)}, u32[]{:S(2)}, u32[]{:S(2)}) collective-permute-start(bf16[4,48,384]{2,1,0:T(8,128)(2,1)S(1)} %shard_map.110.refs_0_), channel_id=1, source_target_pairs={{0,128},{64,192},{128,0},{192,64},{1,129},{65,193},{129,1},{193,65... | collective-permute-start | bytes 442376 | tf_op jit(solution)/shard_map/ppermute | solution.py:318
  37.0 17.1 %collective-permute-start.5 = (bf16[4,48,384]{2,1,0:T(8,128)(2,1)S(1)}, bf16[4,48,384]{2,1,0:T(8,128)(2,1)S(1)}, u32[]{:S(2)}, u32[]{:S(2)}) collective-permute-start(bf16[4,48,384]{2,1,0:T(8,128)(2,1)S(1)} %shard_map.110.refs_0_), channel_id=1, source_target_pairs={{0,192},{64,0},{128,64},{192,128},{1,193},{65,1},{129,65},{193,129... | collective-permute-start | bytes 442376 | tf_op jit(solution)/shard_map/ppermute | solution.py:318
  54.9 16.8 %collective-permute-start.6 = (bf16[16,48,384]{2,1,0:T(8,128)(2,1)}, bf16[16,48,384]{2,1,0:T(8,128)(2,1)S(1)}, u32[]{:S(2)}, u32[]{:S(2)}) collective-permute-start(bf16[16,48,384]{2,1,0:T(8,128)(2,1)} %bitcast.1.refs_0_), channel_id=1, source_target_pairs={{0,1},{1,2},{2,3},{3,0},{4,5},{5,6},{6,7},{7,4},{8,9},{9,10},{10,1... | collective-permute-start | bytes 1769480 | tf_op jit(solution)/shard_map/ppermute | solution.py:318
  56.5 15.3 %collective-permute-start.8 = (bf16[16,48,384]{2,1,0:T(8,128)(2,1)}, bf16[16,48,384]{2,1,0:T(8,128)(2,1)S(1)}, u32[]{:S(2)}, u32[]{:S(2)}) collective-permute-start(bf16[16,48,384]{2,1,0:T(8,128)(2,1)} %bitcast.1.refs_0_), channel_id=1, source_target_pairs={{0,3},{1,0},{2,1},{3,2},{4,7},{5,4},{6,5},{7,6},{8,11},{9,8},{10,9... | collective-permute-start | bytes 1769480 | tf_op jit(solution)/shard_map/ppermute | solution.py:318
  76.4 46.3 %all-to-all-start.1 = ((bf16[32,16,1536]{2,1,0:T(8,128)(2,1)}), bf16[32,16,1536]{2,1,0:T(8,128)(2,1)}, u32[]{:S(2)}, u32[]{:S(2)}) async-start(bf16[32,16,1536]{2,1,0:T(8,128)(2,1)} %bitcast.28), calls=%async_computation.1 | async-start | bytes 3145728 | tf_op jit(solution)/shard_map/all_to_all | solution.py:24
  85.7 26.8 %copy-start.3 = (bf16[1,512,1536]{2,1,0:T(8,128)(2,1)S(1)}, bf16[1,512,1536]{2,1,0:T(8,128)(2,1)}, u32[]{:S(2)}) copy-start(bf16[1,512,1536]{2,1,0:T(8,128)(2,1)} %param.6) | copy-start | bytes 4718596
  85.7 26.8 %copy-start.4 = (bf16[1,512,1536]{2,1,0:T(8,128)(2,1)S(1)}, bf16[1,512,1536]{2,1,0:T(8,128)(2,1)}, u32[]{:S(2)}) copy-start(bf16[1,512,1536]{2,1,0:T(8,128)(2,1)} %param.7) | copy-start | bytes 4718596
  85.7 26.8 %copy-start.7 = (bf16[512,512]{1,0:T(8,128)(2,1)S(1)}, bf16[512,512]{1,0:T(8,128)(2,1)}, u32[]{:S(2)}) copy-start(bf16[512,512]{1,0:T(8,128)(2,1)} %get-tuple-element.42.refs_4_.refs_0_) | copy-start | bytes 1572868
  85.7 17.2 %collective-permute-start.7 = (bf16[16,48,384]{2,1,0:T(8,128)(2,1)}, bf16[16,48,384]{2,1,0:T(8,128)(2,1)S(1)}, u32[]{:S(2)}, u32[]{:S(2)}) collective-permute-start(bf16[16,48,384]{2,1,0:T(8,128)(2,1)} %bitcast.1.refs_0_), channel_id=1, source_target_pairs={{0,2},{1,3},{2,0},{3,1},{4,6},{5,7},{6,4},{7,5},{8,10},{9,11},{10,... | collective-permute-start | bytes 1769480 | tf_op jit(solution)/shard_map/ppermute | solution.py:318
  106.3 4.8 %collective-permute-start.9 = (bf16[4,16,48,384]{3,2,1,0:T(8,128)(2,1)S(1)}, bf16[4,16,48,384]{3,2,1,0:T(8,128)(2,1)S(1)}, u32[]{:S(2)}, u32[]{:S(2)}) collective-permute-start(bf16[4,16,48,384]{3,2,1,0:T(8,128)(2,1)S(1)} %shard_map.112.refs_1_), channel_id=1, source_target_pairs={{0,8},{8,0},{1,9},{9,1},{2,10},{10,2},{3,11},{11,3},{4,12},{12,4},... | collective-permute-start | bytes 7077896 | tf_op jit(solution)/shard_map/ppermute | solution.py:326
  122.7 48.4 %all-to-all-start.2 = ((bf16[32,16,1536]{2,1,0:T(8,128)(2,1)}), bf16[32,16,1536]{2,1,0:T(8,128)(2,1)}, u32[]{:S(2)}, u32[]{:S(2)}) async-start(bf16[32,16,1536]{2,1,0:T(8,128)(2,1)} %bitcast.31), calls=%async_computation.2 | async-start | bytes 3145728 | tf_op jit(solution)/shard_map/all_to_all | solution.py:24
  130.2 1.2 collective-permute-start.12
  143.9 4.7 %collective-permute-start.13 = (bf16[768,1536]{1,0:T(8,128)(2,1)}, bf16[768,1536]{1,0:T(8,128)(2,1)S(1)}, u32[]{:S(2)}, u32[]{:S(2)}) collective-permute-start(bf16[768,1536]{1,0:T(8,128)(2,1)} %get-tuple-element.56), channel_id=1, source_target_pairs={{0,8},{8,0},{1,9},{9,1},{2,10},{10,2},{3,11},{11,3},{4,12},{12,4},... | collective-permute-start | bytes 7077896 | tf_op jit(solution)/shard_map/ppermute | solution.py:326
  153.6 16.6 %collective-permute-start.14 = (bf16[768,384]{1,0:T(8,128)(2,1)S(1)}, bf16[768,384]{1,0:T(8,128)(2,1)S(1)}, u32[]{:S(2)}, u32[]{:S(2)}) collective-permute-start(bf16[768,384]{1,0:T(8,128)(2,1)S(1)} %get-tuple-element.57), channel_id=1, source_target_pairs={{0,1},{1,2},{2,3},{3,0},{4,5},{5,6},{6,7},{7,4},{8,9},{9,10},{10,1... | collective-permute-start | bytes 1769480 | tf_op jit(solution)/shard_map/ppermute | solution.py:318
  155.1 16.0 %collective-permute-start.15 = (bf16[768,384]{1,0:T(8,128)(2,1)S(1)}, bf16[768,384]{1,0:T(8,128)(2,1)}, u32[]{:S(2)}, u32[]{:S(2)}) collective-permute-start(bf16[768,384]{1,0:T(8,128)(2,1)S(1)} %get-tuple-element.58), channel_id=1, source_target_pairs={{0,3},{1,0},{2,1},{3,2},{4,7},{5,4},{6,5},{7,6},{8,11},{9,8},{10,9... | collective-permute-start | bytes 1769480 | tf_op jit(solution)/shard_map/ppermute | solution.py:318
  176.1 44.7 %all-to-all-start.3 = ((bf16[32,16,1536]{2,1,0:T(8,128)(2,1)}), bf16[32,16,1536]{2,1,0:T(8,128)(2,1)}, u32[]{:S(2)}, u32[]{:S(2)}) async-start(bf16[32,16,1536]{2,1,0:T(8,128)(2,1)} %bitcast.29), calls=%async_computation.3 | async-start | bytes 3145728 | tf_op jit(solution)/shard_map/all_to_all | solution.py:24
  183.8 17.3 %collective-permute-start.16 = (bf16[768,384]{1,0:T(8,128)(2,1)}, bf16[768,384]{1,0:T(8,128)(2,1)}, u32[]{:S(2)}, u32[]{:S(2)}) collective-permute-start(bf16[768,384]{1,0:T(8,128)(2,1)} %copy-done.35), channel_id=1, source_target_pairs={{0,2},{1,3},{2,0},{3,1},{4,6},{5,7},{6,4},{7,5},{8,10},{9,11},{10,... | collective-permute-start | bytes 1769480 | tf_op jit(solution)/shard_map/ppermute | solution.py:318
  187.0 14.1 %copy-start.19 = (bf16[768,384]{1,0:T(8,128)(2,1)S(1)}, bf16[768,384]{1,0:T(8,128)(2,1)}, u32[]{:S(2)}) copy-start(bf16[768,384]{1,0:T(8,128)(2,1)} %copy-done.18) | copy-start | bytes 1769476
  187.0 14.1 %copy-start.39 = (bf16[768,384]{1,0:T(8,128)(2,1)S(1)}, bf16[768,384]{1,0:T(8,128)(2,1)}, u32[]{:S(2)}) copy-start(bf16[768,384]{1,0:T(8,128)(2,1)} %copy-done.38) | copy-start | bytes 1769476
  191.3 12.2 %copy-start.16 = (bf16[4,128,128]{2,1,0:T(8,128)(2,1)}, bf16[4,128,128]{2,1,0:T(8,128)(2,1)S(1)}, u32[]{:S(2)}) copy-start(bf16[4,128,128]{2,1,0:T(8,128)(2,1)S(1)} %shard_map.121.refs_5_.refs_3_) | copy-start | bytes 393220
  202.6 18.2 %copy-start.21 = (bf16[512,512]{1,0:T(8,128)(2,1)S(1)}, bf16[512,512]{1,0:T(8,128)(2,1)}, u32[]{:S(2)}) copy-start(bf16[512,512]{1,0:T(8,128)(2,1)} %get-tuple-element.50.refs_0_) | copy-start | bytes 1572868
  203.4 13.2 %collective-permute-start.19 = (bf16[192,384]{1,0:T(8,128)(2,1)}, bf16[192,384]{1,0:T(8,128)(2,1)S(1)}, u32[]{:S(2)}, u32[]{:S(2)}) collective-permute-start(bf16[192,384]{1,0:T(8,128)(2,1)} %get-tuple-element.81), channel_id=1, source_target_pairs={{0,192},{64,0},{128,64},{192,128},{1,193},{65,1},{129,65},{193,129... | collective-permute-start | bytes 442376 | tf_op jit(solution)/shard_map/ppermute | solution.py:318
  204.2 12.4 %collective-permute-start.18 = (bf16[192,384]{1,0:T(8,128)(2,1)}, bf16[192,384]{1,0:T(8,128)(2,1)S(1)}, u32[]{:S(2)}, u32[]{:S(2)}) collective-permute-start(bf16[192,384]{1,0:T(8,128)(2,1)} %get-tuple-element.82), channel_id=1, source_target_pairs={{0,128},{64,192},{128,0},{192,64},{1,129},{65,193},{129,1},{193,65... | collective-permute-start | bytes 442376 | tf_op jit(solution)/shard_map/ppermute | solution.py:318
  205.2 11.4 %collective-permute-start.17 = (bf16[192,384]{1,0:T(8,128)(2,1)S(1)}, bf16[192,384]{1,0:T(8,128)(2,1)S(1)}, u32[]{:S(2)}, u32[]{:S(2)}) collective-permute-start(bf16[192,384]{1,0:T(8,128)(2,1)S(1)} %get-tuple-element.80), channel_id=1, source_target_pairs={{0,64},{64,128},{128,192},{192,0},{1,65},{65,129},{129,193},{193,1... | collective-permute-start | bytes 442376 | tf_op jit(solution)/shard_map/ppermute | solution.py:318
  220.8 11.5 %copy-start.40 = (bf16[48,384]{1,0:T(8,128)(2,1)S(1)}, bf16[48,384]{1,0:T(8,128)(2,1)}, u32[]{:S(2)}) copy-start(bf16[48,384]{1,0:T(8,128)(2,1)} %get-tuple-element.86.refs_6_) | copy-start | bytes 110596
  220.8 13.0 %copy-start.17 = (bf16[4,128,128]{2,1,0:T(8,128)(2,1)S(1)}, bf16[4,128,128]{2,1,0:T(8,128)(2,1)}, u32[]{:S(2)}) copy-start(bf16[4,128,128]{2,1,0:T(8,128)(2,1)} %copy-done.16) | copy-start | bytes 393220
  225.5 25.3 %all-to-all-start.4 = ((bf16[32,4,1536]{2,1,0:T(4,128)(2,1)}), bf16[32,4,1536]{2,1,0:T(4,128)(2,1)}, u32[]{:S(2)}, u32[]{:S(2)}) async-start(bf16[32,4,1536]{2,1,0:T(4,128)(2,1)} %get-tuple-element.68), calls=%async_computation.4 | async-start | bytes 786432 | tf_op jit(solution)/shard_map/all_to_all | solution.py:460
  232.3 14.5 %collective-permute-start.20 = (bf16[48,384]{1,0:T(8,128)(2,1)S(1)}, bf16[48,384]{1,0:T(8,128)(2,1)S(1)}, u32[]{:S(2)}, u32[]{:S(2)}) collective-permute-start(bf16[48,384]{1,0:T(8,128)(2,1)S(1)} %copy-done.40), channel_id=1, source_target_pairs={{0,16},{16,32},{32,48},{48,0},{1,17},{17,33},{33,49},{49,1},{2,18}... | collective-permute-start | bytes 110600 | tf_op jit(solution)/shard_map/ppermute | solution.py:318
  234.9 9.5 %copy-start.44 = (bf16[48,384]{1,0:T(8,128)(2,1)S(1)}, bf16[48,384]{1,0:T(8,128)(2,1)}, u32[]{:S(2)}) copy-start(bf16[48,384]{1,0:T(8,128)(2,1)} %get-tuple-element.84) | copy-start | bytes 110596
  234.9 11.9 %copy-start.43 = (bf16[48,384]{1,0:T(8,128)(2,1)S(1)}, bf16[48,384]{1,0:T(8,128)(2,1)}, u32[]{:S(2)}) copy-start(bf16[48,384]{1,0:T(8,128)(2,1)} %get-tuple-element.83) | copy-start | bytes 110596
  234.9 33.3 %copy-start.2 = (f32[512,1536]{1,0:T(8,128)S(1)}, f32[512,1536]{1,0:T(8,128)}, u32[]{:S(2)}) copy-start(f32[512,1536]{1,0:T(8,128)} %copy-done.1) | copy-start | bytes 9437188
  239.7 28.5 %copy-start.33 = (f32[3,1536]{1,0:T(4,128)S(1)}, f32[3,1536]{1,0:T(4,128)}, u32[]{:S(2)}) copy-start(f32[3,1536]{1,0:T(4,128)} %refs_2_.1) | copy-start | bytes 55300
  239.7 11.1 %collective-permute-start.23 = (bf16[256,128]{1,0:T(8,128)(2,1)S(1)}, bf16[256,128]{1,0:T(8,128)(2,1)S(1)}, u32[]{:S(2)}, u32[]{:S(2)}) collective-permute-start(bf16[256,128]{1,0:T(8,128)(2,1)S(1)} %get-tuple-element.71), channel_id=1, source_target_pairs={{0,1},{1,2},{2,3},{3,0},{4,5},{5,6},{6,7},{7,4},{8,9},{9,10},{10,1... | collective-permute-start | bytes 196616 | tf_op jit(solution)/shard_map/ppermute | solution.py:318
  240.2 10.6 %collective-permute-start.24 = (bf16[256,128]{1,0:T(8,128)(2,1)S(1)}, bf16[256,128]{1,0:T(8,128)(2,1)S(1)}, u32[]{:S(2)}, u32[]{:S(2)}) collective-permute-start(bf16[256,128]{1,0:T(8,128)(2,1)S(1)} %get-tuple-element.72), channel_id=1, source_target_pairs={{0,2},{1,3},{2,0},{3,1},{4,6},{5,7},{6,4},{7,5},{8,10},{9,11},{10,... | collective-permute-start | bytes 196616 | tf_op jit(solution)/shard_map/ppermute | solution.py:318
  243.4 7.4 %collective-permute-start.25 = (bf16[256,128]{1,0:T(8,128)(2,1)S(1)}, bf16[256,128]{1,0:T(8,128)(2,1)}, u32[]{:S(2)}, u32[]{:S(2)}) collective-permute-start(bf16[256,128]{1,0:T(8,128)(2,1)S(1)} %get-tuple-element.73), channel_id=1, source_target_pairs={{0,3},{1,0},{2,1},{3,2},{4,7},{5,4},{6,5},{7,6},{8,11},{9,8},{10,9... | collective-permute-start | bytes 196616 | tf_op jit(solution)/shard_map/ppermute | solution.py:318
  244.4 4.9 %collective-permute-start.21 = (bf16[48,384]{1,0:T(8,128)(2,1)S(1)}, bf16[48,384]{1,0:T(8,128)(2,1)S(1)}, u32[]{:S(2)}, u32[]{:S(2)}) collective-permute-start(bf16[48,384]{1,0:T(8,128)(2,1)S(1)} %copy-done.44), channel_id=1, source_target_pairs={{0,32},{16,48},{32,0},{48,16},{1,33},{17,49},{33,1},{49,17},{2,34}... | collective-permute-start | bytes 110600 | tf_op jit(solution)/shard_map/ppermute | solution.py:318
  246.8 4.0 %collective-permute-start.22 = (bf16[48,384]{1,0:T(8,128)(2,1)S(1)}, bf16[48,384]{1,0:T(8,128)(2,1)S(1)}, u32[]{:S(2)}, u32[]{:S(2)}) collective-permute-start(bf16[48,384]{1,0:T(8,128)(2,1)S(1)} %copy-done.43), channel_id=1, source_target_pairs={{0,48},{16,0},{32,16},{48,32},{1,49},{17,1},{33,17},{49,33},{2,50}... | collective-permute-start | bytes 110600 | tf_op jit(solution)/shard_map/ppermute | solution.py:318
  252.9 10.3 %collective-permute-start.26 = (bf16[496,128]{1,0:T(8,128)(2,1)S(1)}, bf16[496,128]{1,0:T(8,128)(2,1)S(1)}, u32[]{:S(2)}, u32[]{:S(2)}) collective-permute-start(bf16[496,128]{1,0:T(8,128)(2,1)S(1)} %shard_map.125.refs_0_), channel_id=1, source_target_pairs={{0,4},{4,0},{1,5},{5,1},{2,6},{6,2},{3,7},{7,3},{8,12},{12,8},{9,1... | collective-permute-start | bytes 380936 | tf_op jit(solution)/shard_map/ppermute | solution.py:326
  264.0 12.2 %all-to-all-start.5 = ((bf16[4,496,128]{2,1,0:T(8,128)(2,1)}), bf16[4,496,128]{2,1,0:T(8,128)(2,1)}, u32[]{:S(2)}, u32[]{:S(2)}) async-start(bf16[4,496,128]{2,1,0:T(8,128)(2,1)} %copy-done.14), calls=%async_computation.5 | async-start | bytes 1015808 | tf_op jit(solution)/shard_map/all_to_all | solution.py:488
  (34 other events, 54.3 us)

commit v3 on v2

--- a/solution.py
+++ b/solution.py
@@ -67,8 +67,7 @@
     )
 
 
-def setup_kernel(lead_in, trail_in, lead_ref, lead_back, trail_ref, trail_back, to_position, to_group, *, owners):
-    blocks, size, _ = lead_in.shape
+def orders(blocks, size, owners):
     per = size // owners
     rows = blocks * size
     line = lax.broadcasted_iota(jnp.int32, (rows, rows), 0)
@@ -77,18 +76,30 @@
     inner, block = lax.div(rest, blocks), lax.rem(rest, blocks)
     by_position = (line == (block * owners + owner) * per + inner).astype(F32).astype(BF16)
     by_group = (line == (inner * owners + owner) * blocks + block).astype(F32).astype(BF16)
+    return by_position, by_group
+
+
+def diagonal(ref):
+    blocks, size, _ = ref.shape
+    rows = blocks * size
+    line = lax.broadcasted_iota(jnp.int32, (rows, rows), 0)
+    column = lax.broadcasted_iota(jnp.int32, (rows, rows), 1)
+    tall = ref[...].reshape(rows, size).astype(F32)
+    wide = jnp.concatenate([tall] * blocks, axis=1)
+    return jnp.where(lax.div(line, size) == lax.div(column, size), wide, 0.0).astype(BF16)
+
+
+def lead_kernel(lead_in, lead_ref, *, owners):
+    by_position, _ = orders(*lead_in.shape[:2], owners)
+    lead_ref[...] = matmul(by_position, diagonal(lead_in), 0, 0).astype(BF16)
+
+
+def setup_kernel(lead_in, trail_in, lead_back, trail_ref, trail_back, to_position, to_group, *, owners):
+    by_position, by_group = orders(*lead_in.shape[:2], owners)
     to_position[...] = by_position
     to_group[...] = by_group
-    same = lax.div(line, size) == lax.div(column, size)
-
-    def diagonal(ref):
-        tall = ref[...].reshape(rows, size).astype(F32)
-        return jnp.where(same, jnp.concatenate([tall] * blocks, axis=1), 0.0).astype(BF16)
-
-    lead = diagonal(lead_in)
     trail = diagonal(trail_in)
-    lead_ref[...] = matmul(by_position, lead, 0, 0).astype(BF16)
-    lead_back[...] = matmul(lead, by_position, 0, 0).astype(BF16)
+    lead_back[...] = matmul(diagonal(lead_in), by_position, 0, 0).astype(BF16)
     trail_ref[...] = matmul(by_group, matmul(trail, by_group).astype(BF16), 0, 0).astype(BF16)
     trail_back[...] = matmul(by_group, matmul(trail, by_group, 0, 0).astype(BF16), 0, 0).astype(BF16)
 
@@ -377,22 +388,30 @@
     tok_before, tok_after = halo_rows(features[:1], features[-1:])
     share = width // y_count
     near = ring(piece(gate_weight, position("y"), y_count, 1), "z_lo")
-    lead, lead_back, trail, trail_back, to_position, to_group = on_device(
-        functools.partial(setup_kernel, owners=owners), [leading, trailing], [square] * 6, kept=range(1, 6), stay=[0, 1]
+    (lead,) = on_device(
+        functools.partial(lead_kernel, owners=owners), [leading], [square], stay=[0]
     )
     conv_in, send = on_device(
         forward_kernel,
         [features, tok_before, tok_after, conv_weight, lead],
         [wide, wide],
         needs=near,
-        kept=[1],
-        stay=[0],
+        kept=[0, 1],
+        stay=[0, 3],
         step=512,
+    )
+    lead_back, trail, trail_back, to_position, to_group = on_device(
+        functools.partial(setup_kernel, owners=owners),
+        [leading, trailing],
+        [square] * 5,
+        needs=[send],
+        kept=range(5),
+        stay=[0, 1],
     )
     columns = exchange(send)
     near = place(ring(place(near, "z_lo"), "x"), "x").reshape(x_count * z_count, own, share)
     near = ring(near, "y")
-    (send,) = on_device(mix_kernel, [trail, columns], [wide], needs=[near[1], near[-1]], kept=[0], step=512)
+    (send,) = on_device(mix_kernel, [trail, columns], [wide], needs=[near[1], near[-1]], kept=[0], stay=[0], step=512)
     second_out = exchange(send)
     near = place(near, "y")
     far = swap(near, "core")
@@ -434,6 +453,7 @@
         [wide],
         needs=[gate_back, arrived[1], arrived[-1]],
         kept=[0],
+        stay=[0],
         step=512,
     )
     d_first = exchange(send)
@@ -447,13 +467,13 @@
     )
     grad_second, *arrived = lax.optimization_barrier((grad_second, *arrived))
     pieces = send_pieces(cut(add_up(arrived), "x", 0), "x")
-    pieces = cut(add_up(pieces), "z_lo", 0)
+    pieces = send_pieces(cut(add_up(pieces), "z_lo", 0), "z_lo")
 
     d_conv, spread = on_device(
         backward_kernel,
         [lead_back, d_first, features, tok_before, tok_after],
         [wide, like((owners, conv_weight.shape[0] + 1, width))],
-        needs=[grad_second, pieces[1]],
+        needs=[grad_second, *pieces[1:]],
         kept=[0, 1],
         step=512,
     )
@@ -464,11 +484,12 @@
         [like((2 * size, size))] * y_count,
         scratch=[pltpu.VMEM((blocks, size, size), F32)],
         needs=[d_conv],
-        stay=[1, 2],
+        kept=range(y_count),
+        stay=[0, 1, 2],
         step=512,
     )
     parts = [
-        *send_pieces(pieces, "z_lo"),
+        *pieces,
         *send_pieces(factors, "y"),
     ]
     (grad_tokens,) = on_device(
@@ -483,7 +504,7 @@
         stay=range(len(parts)),
     )
     (packed,) = on_device(
-        pair_kernel, [packed, swap(packed, "z_hi")], [like((y_count, *packed.shape))]
+        pair_kernel, [packed, swap(packed, "z_hi")], [like((y_count, *packed.shape))], kept=[0]
     )
     packed = lax.all_to_all(packed, "y", split_axis=0, concat_axis=0, tiled=True)
     grad_gate, grad_second, grad_first, grad_conv = on_device(

time: 280 us -> 279 us (level); the launches traced: 278 us -> 274 us
  waiting for transfers between devices: 96.5 us -> 90.7 us
  local copies, waits for them, and re-layouts: 26.3 us -> 21.4 us
  starting transfers between devices: 90.1 us -> 94.9 us
    unnamed x98 -> x84, local copies, waits for them, and re-layouts: 23.4 us -> 18.5 us
    all_to_all x4, waiting for transfers between devices: 5.44 us -> 2.06 us  [exchange(): lax.all_to_all(cut, SEQ, split_axis=0, concat_axis=0, tiled=True)]
    pallas_call x17 -> x18, Pallas kernels: 54.9 us -> 57 us  [on_device(): pl.pallas_call(body, grid=(width // step if step else 1,), in_specs=[spec...]
  transfers between devices with their start and end apart: 33 -> 33, of which waited for: 17 -> 20; matrix products, arithmetic and copies ran while one was open for 2% -> 2% of each run, Pallas kernels for 16% -> 16%
where the time goes in v3:
time: 279 us; the launch traced here: 274 us
  starting transfers between devices  94.9 us (34%)
  waiting for transfers between devices  90.7 us (33%)
  Pallas kernels  64.7 us (23%)
  local copies, waits for them, and re-layouts  21.4 us (8%)
    ppermute x21, waiting for transfers between devices, shift(): lax.ppermute(values, axis, [(i, (i + step) % count) for i in range(count)])  72.2 us
    pallas_call x18, Pallas kernels, on_device(): pl.pallas_call(body, grid=(width // step if step else 1,), in_specs=[spec...  57 us
    ppermute x21, starting transfers between devices, shift(): lax.ppermute(values, axis, [(i, (i + step) % count) for i in range(count)])  35.7 us
    all_to_all x4, starting transfers between devices, exchange(): lax.all_to_all(cut, SEQ, split_axis=0, concat_axis=0, tiled=True)  32.5 us
    unnamed x84, local copies, waits for them, and re-layouts  18.5 us
    ppermute x4, waiting for transfers between devices, swap(): return lax.ppermute(values, axis, [(0, 1), (1, 0)])  13.6 us
    all_to_all x1, starting transfers between devices, shards(): lax.all_to_all(spread, SEQ, split_axis=0, concat_axis=0, tiled=True)  8.32 us
    ppermute x1, starting transfers between devices, halo_rows(): after = lax.ppermute(first, SEQ, down)  6.34 us
  transfers between devices with their start and end apart: 33, of which 20 were waited for; matrix products, arithmetic and copies ran while one was open for 2% of the time, Pallas kernels for 16%

profile of v3, /device:TPU:6, one launch (start us, length us, event | category | flops | bytes accessed | tf_op | source)
XLA Modules:
  0.0 274.3 jit_solution(7722229228486759709)
XLA Ops:
  1.6 1.9 collective-permute-start.2
  3.5 3.3 %collective-permute-start.3 = (bf16[48,384]{1,0:T(8,128)(2,1)S(1)}, bf16[48,384]{1,0:T(8,128)(2,1)S(1)}, u32[]{:S(2)}, u32[]{:S(2)}) collective-permute-start(bf16[48,384]{1,0:T(8,128)(2,1)S(1)} %constant_dynamic-slice_fusion.refs_5_.refs_0_), channel_id=1, source_target_pairs={{0,32},{16,48},{32,0},{48,16},{1,33},{17,49},{33,1},{49,17},{2,34}... | collective-permute-start | bytes 110600 | tf_op jit(solution)/shard_map/ppermute | solution.py:329
  8.5 1.9 collective-permute-start
  10.5 6.3 %collective-permute-start.1 = (bf16[1,1536]{1,0:T(2,128)(2,1)S(1)}, bf16[1,1536]{1,0:T(2,128)(2,1)S(1)}, u32[]{:S(2)}, u32[]{:S(2)}) collective-permute-start(bf16[1,1536]{1,0:T(2,128)(2,1)S(1)} %get-tuple-element.76), channel_id=1, source_target_pairs={{8,0},{16,8},{24,16},{32,24},{40,32},{48,40},{56,48},{64,56},{72,6... | collective-permute-start | bytes 9224 | tf_op jit(solution)/shard_map/ppermute | solution.py:345
  18.9 4.5 %shard_map.110 = (bf16[512,1536]{1,0:T(8,128)(2,1)}, bf16[512,1536]{1,0:T(8,128)(2,1)}) custom-call(bf16[512,1536]{1,0:T(8,128)(2,1)} %bitcast.20, bf16[1,1536]{1,0:T(2,128)(2,1)S(1)} %collective-permute-done.refs_1_.refs_3_, bf16[1,1536]{1,0:T(2,128)(2,1)S(1)} %collective-permute-done.1.refs_2_.refs_4_, f32[3,1536]{1,0:T(4,128)} %refs_2_.1, ...), custom_call_target="tpu_custom_call" | custom-call | flops 1000 | bytes 1000 | tf_op jit(solution)/shard_map/pallas_call | solution.py:54
  23.4 8.6 %all-to-all-start = ((bf16[32,16,1536]{2,1,0:T(8,128)(2,1)}), bf16[32,16,1536]{2,1,0:T(8,128)(2,1)S(1)}, u32[]{:S(2)}, u32[]{:S(2)}) async-start(bf16[32,16,1536]{2,1,0:T(8,128)(2,1)} %bitcast.34), calls=%async_computation | async-start | bytes 3145728 | tf_op jit(solution)/shard_map/all_to_all | solution.py:24
  32.3 2.7 collective-permute-start.6
  35.0 13.6 %collective-permute-done.5.refs_1_ = bf16[4,48,384]{2,1,0:T(8,128)(2,1)S(1)} collective-permute-done((bf16[4,48,384]{2,1,0:T(8,128)(2,1)S(1)}, bf16[4,48,384]{2,1,0:T(8,128)(2,1)S(1)}, u32[]{:S(2)}, u32[]{:S(2)}) %collective-permute-start.5) | collective-permute-done | bytes 147488 | tf_op jit(solution)/shard_map/ppermute | solution.py:329
  49.7 2.4 collective-permute-done.7.refs_3_
  52.1 1.7 collective-permute-start.8
  53.8 1.7 collective-permute-start.10
  55.4 3.5 %shard_map.111 = (bf16[512,512]{1,0:T(8,128)(2,1)}, bf16[512,512]{1,0:T(8,128)(2,1)}, bf16[512,512]{1,0:T(8,128)(2,1)}, bf16[512,512]{1,0:T(8,128)(2,1)}, bf16[512,512]{1,0:T(8,128)(2,1)}) custom-call(bf16[4,128,128]{2,1,0:T(8,128)(2,1)} %refs_0_.3, bf16[4,128,128]{2,1,0:T(8,128)(2,1)} %refs_1_.1, bf16[512,1536]{1,0:T(8,128)(2,1)} %get-tuple-element.41.refs_2_), custom_call_target="tpu_custom_call" | custom-call | flops 1000 | bytes 1000 | tf_op jit(solution)/shard_map/pallas_call | solution.py:54
  58.9 9.9 %collective-permute-done.8.refs_1_.refs_2_ = bf16[16,48,384]{2,1,0:T(8,128)(2,1)S(1)} collective-permute-done((bf16[16,48,384]{2,1,0:T(8,128)(2,1)S(1)}, bf16[16,48,384]{2,1,0:T(8,128)(2,1)S(1)}, u32[]{:S(2)}, u32[]{:S(2)}) %collective-permute-start.8) | collective-permute-done | bytes 589856 | tf_op jit(solution)/shard_map/ppermute | solution.py:329
  69.9 3.6 %shard_map.115.refs_5_ = bf16[512,1536]{1,0:T(8,128)(2,1)} custom-call(bf16[512,512]{1,0:T(8,128)(2,1)} %get-tuple-element.43.refs_0_, bf16[512,1536]{1,0:T(8,128)(2,1)S(1)} %bitcast.24, bf16[16,48,384]{2,1,0:T(8,128)(2,1)} %copy-done.9, bf16[16,48,384]{2,1,0:T(8,128)(2,1)} %copy-done.11), custom_call_target="tpu_custom_call" | custom-call | flops 1000 | bytes 1000 | tf_op jit(solution)/shard_map/pallas_call | solution.py:54
  73.4 9.3 %all-to-all-start.1 = ((bf16[32,16,1536]{2,1,0:T(8,128)(2,1)}), bf16[32,16,1536]{2,1,0:T(8,128)(2,1)}, u32[]{:S(2)}, u32[]{:S(2)}) async-start(bf16[32,16,1536]{2,1,0:T(8,128)(2,1)} %bitcast.32), calls=%async_computation.1 | async-start | bytes 3145728 | tf_op jit(solution)/shard_map/all_to_all | solution.py:24
  82.7 2.8 %collective-permute-start.9 = (bf16[16,48,384]{2,1,0:T(8,128)(2,1)}, bf16[16,48,384]{2,1,0:T(8,128)(2,1)S(1)}, u32[]{:S(2)}, u32[]{:S(2)}) collective-permute-start(bf16[16,48,384]{2,1,0:T(8,128)(2,1)} %bitcast.30), channel_id=1, source_target_pairs={{0,2},{1,3},{2,0},{3,1},{4,6},{5,7},{6,4},{7,5},{8,10},{9,11},{10,... | collective-permute-start | bytes 1769480 | tf_op jit(solution)/shard_map/ppermute | solution.py:329
  85.5 14.4 %collective-permute-done.9.refs_2_ = bf16[16,48,384]{2,1,0:T(8,128)(2,1)S(1)} collective-permute-done((bf16[16,48,384]{2,1,0:T(8,128)(2,1)}, bf16[16,48,384]{2,1,0:T(8,128)(2,1)S(1)}, u32[]{:S(2)}, u32[]{:S(2)}) %collective-permute-start.9) | collective-permute-done | bytes 589856 | tf_op jit(solution)/shard_map/ppermute | solution.py:329
  103.6 4.5 %collective-permute-done.11.refs_2_ = bf16[4,16,48,384]{3,2,1,0:T(8,128)(2,1)S(1)} collective-permute-done((bf16[4,16,48,384]{3,2,1,0:T(8,128)(2,1)S(1)}, bf16[4,16,48,384]{3,2,1,0:T(8,128)(2,1)S(1)}, u32[]{:S(2)}, u32[]{:S(2)}) %collective-permute-start.11) | collective-permute-done | bytes 2359328 | tf_op jit(solution)/shard_map/ppermute | solution.py:337
  109.5 8.2 %shard_map.116 = (bf16[16,2,48,1536]{3,2,1,0:T(8,128)(2,1)}, f32[512,1536]{1,0:T(8,128)}, bf16[512,1536]{1,0:T(8,128)(2,1)}) custom-call(bf16[512,1536]{1,0:T(8,128)(2,1)S(1)} %bitcast.21, bf16[4,16,48,384]{3,2,1,0:T(8,128)(2,1)S(1)} %shard_map.114.refs_1_, bf16[4,16,48,384]{3,2,1,0:T(8,128)(2,1)} %copy-done.31, bf16[512,1536]{1,0:T(8,128)(2,1)S(1)} %bitcast.26, ...), custom_call_target="tpu_custom_call" | custom-call | flops 1000 | bytes 1000 | tf_op jit(solution)/shard_map/pallas_call | solution.py:54
  117.7 2.0 all-to-all-done.1
  119.7 6.9 %all-to-all-start.2 = ((bf16[32,16,1536]{2,1,0:T(8,128)(2,1)}), bf16[32,16,1536]{2,1,0:T(8,128)(2,1)}, u32[]{:S(2)}, u32[]{:S(2)}) async-start(bf16[32,16,1536]{2,1,0:T(8,128)(2,1)} %bitcast.36), calls=%async_computation.2 | async-start | bytes 3145728 | tf_op jit(solution)/shard_map/all_to_all | solution.py:24
  131.5 4.9 %shard_map.117 = (bf16[512,1536]{1,0:T(8,128)(2,1)}, bf16[512,1536]{1,0:T(8,128)(2,1)S(1)}) custom-call(bf16[512,512]{1,0:T(8,128)(2,1)S(1)} %copy-done.8, bf16[512,1536]{1,0:T(8,128)(2,1)} %bitcast.8.refs_1_, f32[512,1536]{1,0:T(8,128)} %get-tuple-element.46.refs_2_, bf16[512,1536]{1,0:T(8,128)(2,1)S(1)} %bitcast.27, bf16[16,128]{1,0:T(8,128)(2,1)} %copy-done.41), custom_call_target="tpu_custom_call" | custom-call | flops 1000 | bytes 1000 | tf_op jit(solution)/shard_map/pallas_call | solution.py:54
  136.4 4.6 %shard_map.119 = (bf16[768,1536]{1,0:T(8,128)(2,1)S(1)}, bf16[768,1536]{1,0:T(8,128)(2,1)}) custom-call(bf16[512,1536]{1,0:T(8,128)(2,1)S(1)} %bitcast.22, bf16[512,1536]{1,0:T(8,128)(2,1)S(1)} %get-tuple-element.51.left_ref.refs_1_), custom_call_target="tpu_custom_call" | custom-call | flops 1000 | bytes 1000 | tf_op jit(solution)/shard_map/pallas_call | solution.py:54
  141.1 4.6 %collective-permute-done.13.other_ref = bf16[768,1536]{1,0:T(8,128)(2,1)S(1)} collective-permute-done((bf16[768,1536]{1,0:T(8,128)(2,1)}, bf16[768,1536]{1,0:T(8,128)(2,1)S(1)}, u32[]{:S(2)}, u32[]{:S(2)}) %collective-permute-start.13) | collective-permute-done | bytes 2359328 | tf_op jit(solution)/shard_map/ppermute | solution.py:337
  147.1 2.7 shard_map.120
  152.0 1.9 collective-permute-start.15
  153.9 5.0 %shard_map.118.refs_2_.refs_3_ = f32[512,1536]{1,0:T(8,128)S(1)} custom-call(bf16[512,1536]{1,0:T(8,128)(2,1)S(1)} %get-tuple-element.51.left_ref.refs_1_, bf16[1536,1536]{1,0:T(8,128)(2,1)} %bitcast.35), custom_call_target="tpu_custom_call" | custom-call | flops 1000 | bytes 1000 | tf_op jit(solution)/shard_map/pallas_call | solution.py:154
  158.9 1.6 copy-done.1
  160.5 6.8 %collective-permute-done.14.refs_3_ = bf16[768,384]{1,0:T(8,128)(2,1)S(1)} collective-permute-done((bf16[768,384]{1,0:T(8,128)(2,1)S(1)}, bf16[768,384]{1,0:T(8,128)(2,1)S(1)}, u32[]{:S(2)}, u32[]{:S(2)}) %collective-permute-start.14) | collective-permute-done | bytes 589856 | tf_op jit(solution)/shard_map/ppermute | solution.py:329
  168.1 4.2 %shard_map.121.refs_3_ = bf16[512,1536]{1,0:T(8,128)(2,1)} custom-call(bf16[512,512]{1,0:T(8,128)(2,1)} %get-tuple-element.49.refs_0_, bf16[512,1536]{1,0:T(8,128)(2,1)} %bitcast.11.refs_1_, f32[512,1536]{1,0:T(8,128)} %copy-done.1, bf16[768,384]{1,0:T(8,128)(2,1)} %copy-done.33, bf16[768,384]{1,0:T(8,128)(2,1)} %collective-permute-done.15.refs_4_), custom_call_target="tpu_custom_call" | custom-call | flops 1000 | bytes 1000 | tf_op jit(solution)/shard_map/pallas_call | solution.py:54
  172.3 7.7 %all-to-all-start.3 = ((bf16[32,16,1536]{2,1,0:T(8,128)(2,1)}), bf16[32,16,1536]{2,1,0:T(8,128)(2,1)}, u32[]{:S(2)}, u32[]{:S(2)}) async-start(bf16[32,16,1536]{2,1,0:T(8,128)(2,1)} %bitcast.33), calls=%async_computation.3 | async-start | bytes 3145728 | tf_op jit(solution)/shard_map/all_to_all | solution.py:24
  180.0 2.1 collective-permute-start.16
  183.2 4.3 %shard_map.122.refs_5_.refs_3_ = bf16[4,128,128]{2,1,0:T(8,128)(2,1)S(1)} custom-call(bf16[512,512]{1,0:T(8,128)(2,1)S(1)} %copy-done.20, bf16[512,1536]{1,0:T(8,128)(2,1)} %bitcast.11.refs_1_, bf16[512,1536]{1,0:T(8,128)(2,1)S(1)} %bitcast.25, bf16[512,1536]{1,0:T(8,128)(2,1)} %shard_map.121.refs_3_), custom_call_target="tpu_custom_call" | custom-call | flops 1000 | bytes 1000 | tf_op jit(solution)/shard_map/pallas_call | solution.py:54
  187.5 9.8 %collective-permute-done.16 = bf16[768,384]{1,0:T(8,128)(2,1)} collective-permute-done((bf16[768,384]{1,0:T(8,128)(2,1)}, bf16[768,384]{1,0:T(8,128)(2,1)}, u32[]{:S(2)}, u32[]{:S(2)}) %collective-permute-start.16) | collective-permute-done | bytes 589856 | tf_op jit(solution)/shard_map/ppermute | solution.py:329
  201.4 2.3 collective-permute-start.17
  203.7 9.1 %collective-permute-done.19 = bf16[192,384]{1,0:T(8,128)(2,1)S(1)} collective-permute-done((bf16[192,384]{1,0:T(8,128)(2,1)}, bf16[192,384]{1,0:T(8,128)(2,1)S(1)}, u32[]{:S(2)}, u32[]{:S(2)}) %collective-permute-start.19) | collective-permute-done | bytes 147488 | tf_op jit(solution)/shard_map/ppermute | solution.py:329
  214.9 2.0 collective-permute-start.21
  216.8 2.9 %collective-permute-start.22 = (bf16[48,384]{1,0:T(8,128)(2,1)S(1)}, bf16[48,384]{1,0:T(8,128)(2,1)S(1)}, u32[]{:S(2)}, u32[]{:S(2)}) collective-permute-start(bf16[48,384]{1,0:T(8,128)(2,1)S(1)} %get-tuple-element.82), channel_id=1, source_target_pairs={{0,48},{16,0},{32,16},{48,32},{1,49},{17,1},{33,17},{49,33},{2,50}... | collective-permute-start | bytes 110600 | tf_op jit(solution)/shard_map/ppermute | solution.py:329
  222.0 4.8 %shard_map.123 = (bf16[512,1536]{1,0:T(8,128)(2,1)}, bf16[32,4,1536]{2,1,0:T(4,128)(2,1)}) custom-call(bf16[512,512]{1,0:T(8,128)(2,1)S(1)} %copy-done.19, bf16[512,1536]{1,0:T(8,128)(2,1)} %bitcast.14.refs_1_, bf16[512,1536]{1,0:T(8,128)(2,1)S(1)} %bitcast.23, bf16[1,1536]{1,0:T(2,128)(2,1)S(1)} %collective-permute-done.refs_1_.refs_3_, ...), custom_call_target="tpu_custom_call" | custom-call | flops 1000 | bytes 1000 | tf_op jit(solution)/shard_map/pallas_call | solution.py:54
  226.8 8.3 %all-to-all-start.4 = ((bf16[32,4,1536]{2,1,0:T(4,128)(2,1)}), bf16[32,4,1536]{2,1,0:T(4,128)(2,1)}, u32[]{:S(2)}, u32[]{:S(2)}) async-start(bf16[32,4,1536]{2,1,0:T(4,128)(2,1)} %get-tuple-element.66), calls=%async_computation.4 | async-start | bytes 786432 | tf_op jit(solution)/shard_map/all_to_all | solution.py:480
  235.1 5.0 %shard_map.125 = (bf16[256,128]{1,0:T(8,128)(2,1)}, bf16[256,128]{1,0:T(8,128)(2,1)}, bf16[256,128]{1,0:T(8,128)(2,1)}, bf16[256,128]{1,0:T(8,128)(2,1)}) custom-call(bf16[512,512]{1,0:T(8,128)(2,1)} %get-tuple-element.42.refs_4_.refs_0_, bf16[512,1536]{1,0:T(8,128)(2,1)} %bitcast.14.refs_1_, bf16[512,1536]{1,0:T(8,128)(2,1)} %get-tuple-element.67.refs_2_, ...), custom_call_target="tpu_custom_call" | custom-call | flops 1000 | bytes 1000 | tf_op jit(solution)/shard_map/pallas_call | solution.py:54
  240.6 3.2 %collective-permute-start.24 = (bf16[256,128]{1,0:T(8,128)(2,1)}, bf16[256,128]{1,0:T(8,128)(2,1)S(1)}, u32[]{:S(2)}, u32[]{:S(2)}) collective-permute-start(bf16[256,128]{1,0:T(8,128)(2,1)} %get-tuple-element.70), channel_id=1, source_target_pairs={{0,2},{1,3},{2,0},{3,1},{4,6},{5,7},{6,4},{7,5},{8,10},{9,11},{10,... | collective-permute-start | bytes 196616 | tf_op jit(solution)/shard_map/ppermute | solution.py:329
  250.4 5.5 %collective-permute-start.26 = (bf16[496,128]{1,0:T(8,128)(2,1)S(1)}, bf16[496,128]{1,0:T(8,128)(2,1)S(1)}, u32[]{:S(2)}, u32[]{:S(2)}) collective-permute-start(bf16[496,128]{1,0:T(8,128)(2,1)S(1)} %shard_map.126.refs_0_), channel_id=1, source_target_pairs={{0,4},{4,0},{1,5},{5,1},{2,6},{6,2},{3,7},{7,3},{8,12},{12,8},{9,1... | collective-permute-start | bytes 380936 | tf_op jit(solution)/shard_map/ppermute | solution.py:337
  255.9 3.4 %collective-permute-done.26.refs_1_ = bf16[496,128]{1,0:T(8,128)(2,1)S(1)} collective-permute-done((bf16[496,128]{1,0:T(8,128)(2,1)S(1)}, bf16[496,128]{1,0:T(8,128)(2,1)S(1)}, u32[]{:S(2)}, u32[]{:S(2)}) %collective-permute-start.26) | collective-permute-done | bytes 127008 | tf_op jit(solution)/shard_map/ppermute | solution.py:337
  260.2 4.1 %all-to-all-start.5 = ((bf16[4,496,128]{2,1,0:T(8,128)(2,1)}), bf16[4,496,128]{2,1,0:T(8,128)(2,1)}, u32[]{:S(2)}, u32[]{:S(2)}) async-start(bf16[4,496,128]{2,1,0:T(8,128)(2,1)} %shard_map.127), calls=%async_computation.5 | async-start | bytes 1015808 | tf_op jit(solution)/shard_map/all_to_all | solution.py:509
  265.8 3.8 %shard_map.124 = bf16[512,1536]{1,0:T(8,128)(2,1)} custom-call(bf16[512,1536]{1,0:T(8,128)(2,1)S(1)} %copy-done.6, bf16[32,4,1536]{2,1,0:T(4,128)(2,1)} %all-to-all-done.4.refs_1_.refs_8_, f32[3,1536]{1,0:T(4,128)S(1)} %copy-done.29, f32[512,1536]{1,0:T(8,128)S(1)} %copy-done.2), custom_call_target="tpu_custom_call" | custom-call | flops 1000 | bytes 1000 | tf_op jit(solution)/shard_map/pallas_call | solution.py:54
  269.5 2.9 %all-to-all-done.5.refs_0_ = bf16[4,496,128]{2,1,0:T(8,128)(2,1)} async-done(((bf16[4,496,128]{2,1,0:T(8,128)(2,1)}), bf16[4,496,128]{2,1,0:T(8,128)(2,1)}, u32[]{:S(2)}, u32[]{:S(2)}) %all-to-all-start.5) | async-done | bytes 507936 | tf_op jit(solution)/shard_map/all_to_all | solution.py:509
  272.4 1.9 shard_map.128
  (129 shorter events, 40.6 us)
Async XLA Ops:
  1.6 16.7 %copy-start.21 = (bf16[48,384]{1,0:T(8,128)(2,1)}, bf16[48,384]{1,0:T(8,128)(2,1)S(1)}, u32[]{:S(2)}) copy-start(bf16[48,384]{1,0:T(8,128)(2,1)S(1)} %constant_dynamic-slice_fusion.refs_5_.refs_0_) | copy-start | bytes 110596
  1.6 16.7 %collective-permute-start.2 = (bf16[48,384]{1,0:T(8,128)(2,1)S(1)}, bf16[48,384]{1,0:T(8,128)(2,1)S(1)}, u32[]{:S(2)}, u32[]{:S(2)}) collective-permute-start(bf16[48,384]{1,0:T(8,128)(2,1)S(1)} %constant_dynamic-slice_fusion.refs_5_.refs_0_), channel_id=1, source_target_pairs={{0,16},{16,32},{32,48},{48,0},{1,17},{17,33},{33,49},{49,1},{2,18}... | collective-permute-start | bytes 110600 | tf_op jit(solution)/shard_map/ppermute | solution.py:329
  3.5 14.8 %collective-permute-start.3 = (bf16[48,384]{1,0:T(8,128)(2,1)S(1)}, bf16[48,384]{1,0:T(8,128)(2,1)S(1)}, u32[]{:S(2)}, u32[]{:S(2)}) collective-permute-start(bf16[48,384]{1,0:T(8,128)(2,1)S(1)} %constant_dynamic-slice_fusion.refs_5_.refs_0_), channel_id=1, source_target_pairs={{0,32},{16,48},{32,0},{48,16},{1,33},{17,49},{33,1},{49,17},{2,34}... | collective-permute-start | bytes 110600 | tf_op jit(solution)/shard_map/ppermute | solution.py:329
  6.7 11.5 %collective-permute-start.4 = (bf16[48,384]{1,0:T(8,128)(2,1)S(1)}, bf16[48,384]{1,0:T(8,128)(2,1)S(1)}, u32[]{:S(2)}, u32[]{:S(2)}) collective-permute-start(bf16[48,384]{1,0:T(8,128)(2,1)S(1)} %constant_dynamic-slice_fusion.refs_5_.refs_0_), channel_id=1, source_target_pairs={{0,48},{16,0},{32,16},{48,32},{1,49},{17,1},{33,17},{49,33},{2,50}... | collective-permute-start | bytes 110600 | tf_op jit(solution)/shard_map/ppermute | solution.py:329
  8.5 9.7 %collective-permute-start = (bf16[1,1536]{1,0:T(2,128)(2,1)S(1)}, bf16[1,1536]{1,0:T(2,128)(2,1)S(1)}, u32[]{:S(2)}, u32[]{:S(2)}) collective-permute-start(bf16[1,1536]{1,0:T(2,128)(2,1)S(1)} %get-tuple-element.77), channel_id=1, source_target_pairs={{0,8},{8,16},{16,24},{24,32},{32,40},{40,48},{48,56},{56,64},{64,7... | collective-permute-start | bytes 9224 | tf_op jit(solution)/shard_map/ppermute | solution.py:344
  10.5 7.8 %collective-permute-start.1 = (bf16[1,1536]{1,0:T(2,128)(2,1)S(1)}, bf16[1,1536]{1,0:T(2,128)(2,1)S(1)}, u32[]{:S(2)}, u32[]{:S(2)}) collective-permute-start(bf16[1,1536]{1,0:T(2,128)(2,1)S(1)} %get-tuple-element.76), channel_id=1, source_target_pairs={{8,0},{16,8},{24,16},{32,24},{40,32},{48,40},{56,48},{64,56},{72,6... | collective-permute-start | bytes 9224 | tf_op jit(solution)/shard_map/ppermute | solution.py:345
  23.4 8.6 %copy-start.24 = (bf16[48,384]{1,0:T(8,128)(2,1)S(1)}, bf16[48,384]{1,0:T(8,128)(2,1)}, u32[]{:S(2)}) copy-start(bf16[48,384]{1,0:T(8,128)(2,1)} %copy-done.23) | copy-start | bytes 110596
  23.4 8.6 %copy-start.26 = (bf16[48,384]{1,0:T(8,128)(2,1)S(1)}, bf16[48,384]{1,0:T(8,128)(2,1)}, u32[]{:S(2)}) copy-start(bf16[48,384]{1,0:T(8,128)(2,1)} %copy-done.25) | copy-start | bytes 110596
  23.4 8.6 %copy-start.28 = (bf16[48,384]{1,0:T(8,128)(2,1)S(1)}, bf16[48,384]{1,0:T(8,128)(2,1)}, u32[]{:S(2)}) copy-start(bf16[48,384]{1,0:T(8,128)(2,1)} %copy-done.27) | copy-start | bytes 110596
  23.4 45.5 %all-to-all-start = ((bf16[32,16,1536]{2,1,0:T(8,128)(2,1)}), bf16[32,16,1536]{2,1,0:T(8,128)(2,1)S(1)}, u32[]{:S(2)}, u32[]{:S(2)}) async-start(bf16[32,16,1536]{2,1,0:T(8,128)(2,1)} %bitcast.34), calls=%async_computation | async-start | bytes 3145728 | tf_op jit(solution)/shard_map/all_to_all | solution.py:24
  32.0 16.5 %collective-permute-start.5 = (bf16[4,48,384]{2,1,0:T(8,128)(2,1)S(1)}, bf16[4,48,384]{2,1,0:T(8,128)(2,1)S(1)}, u32[]{:S(2)}, u32[]{:S(2)}) collective-permute-start(bf16[4,48,384]{2,1,0:T(8,128)(2,1)S(1)} %shard_map.112.refs_0_), channel_id=1, source_target_pairs={{0,64},{64,128},{128,192},{192,0},{1,65},{65,129},{129,193},{193,1... | collective-permute-start | bytes 442376 | tf_op jit(solution)/shard_map/ppermute | solution.py:329
  32.3 17.4 %collective-permute-start.6 = (bf16[4,48,384]{2,1,0:T(8,128)(2,1)S(1)}, bf16[4,48,384]{2,1,0:T(8,128)(2,1)S(1)}, u32[]{:S(2)}, u32[]{:S(2)}) collective-permute-start(bf16[4,48,384]{2,1,0:T(8,128)(2,1)S(1)} %shard_map.112.refs_0_), channel_id=1, source_target_pairs={{0,128},{64,192},{128,0},{192,64},{1,129},{65,193},{129,1},{193,65... | collective-permute-start | bytes 442376 | tf_op jit(solution)/shard_map/ppermute | solution.py:329
  35.0 17.1 %collective-permute-start.7 = (bf16[4,48,384]{2,1,0:T(8,128)(2,1)S(1)}, bf16[4,48,384]{2,1,0:T(8,128)(2,1)S(1)}, u32[]{:S(2)}, u32[]{:S(2)}) collective-permute-start(bf16[4,48,384]{2,1,0:T(8,128)(2,1)S(1)} %shard_map.112.refs_0_), channel_id=1, source_target_pairs={{0,192},{64,0},{128,64},{192,128},{1,193},{65,1},{129,65},{193,129... | collective-permute-start | bytes 442376 | tf_op jit(solution)/shard_map/ppermute | solution.py:329
  52.1 16.7 %copy-start.13 = (bf16[4,4,48,384]{3,2,1,0:T(8,128)(2,1)}, bf16[4,4,48,384]{3,2,1,0:T(8,128)(2,1)S(1)}, u32[]{:S(2)}) copy-start(bf16[4,4,48,384]{3,2,1,0:T(8,128)(2,1)S(1)} %shard_map.113) | copy-start | bytes 1769476
  52.1 16.7 %collective-permute-start.8 = (bf16[16,48,384]{2,1,0:T(8,128)(2,1)S(1)}, bf16[16,48,384]{2,1,0:T(8,128)(2,1)S(1)}, u32[]{:S(2)}, u32[]{:S(2)}) collective-permute-start(bf16[16,48,384]{2,1,0:T(8,128)(2,1)S(1)} %bitcast.28), channel_id=1, source_target_pairs={{0,1},{1,2},{2,3},{3,0},{4,5},{5,6},{6,7},{7,4},{8,9},{9,10},{10,1... | collective-permute-start | bytes 1769480 | tf_op jit(solution)/shard_map/ppermute | solution.py:329
  53.8 15.1 %collective-permute-start.10 = (bf16[16,48,384]{2,1,0:T(8,128)(2,1)S(1)}, bf16[16,48,384]{2,1,0:T(8,128)(2,1)S(1)}, u32[]{:S(2)}, u32[]{:S(2)}) collective-permute-start(bf16[16,48,384]{2,1,0:T(8,128)(2,1)S(1)} %bitcast.29), channel_id=1, source_target_pairs={{0,3},{1,0},{2,1},{3,2},{4,7},{5,4},{6,5},{7,6},{8,11},{9,8},{10,9... | collective-permute-start | bytes 1769480 | tf_op jit(solution)/shard_map/ppermute | solution.py:329
  73.4 46.3 %all-to-all-start.1 = ((bf16[32,16,1536]{2,1,0:T(8,128)(2,1)}), bf16[32,16,1536]{2,1,0:T(8,128)(2,1)}, u32[]{:S(2)}, u32[]{:S(2)}) async-start(bf16[32,16,1536]{2,1,0:T(8,128)(2,1)} %bitcast.32), calls=%async_computation.1 | async-start | bytes 3145728 | tf_op jit(solution)/shard_map/all_to_all | solution.py:24
  82.7 26.8 %copy-start.3 = (bf16[1,512,1536]{2,1,0:T(8,128)(2,1)S(1)}, bf16[1,512,1536]{2,1,0:T(8,128)(2,1)}, u32[]{:S(2)}) copy-start(bf16[1,512,1536]{2,1,0:T(8,128)(2,1)} %param.6) | copy-start | bytes 4718596
  82.7 26.8 %copy-start.4 = (bf16[1,512,1536]{2,1,0:T(8,128)(2,1)S(1)}, bf16[1,512,1536]{2,1,0:T(8,128)(2,1)}, u32[]{:S(2)}) copy-start(bf16[1,512,1536]{2,1,0:T(8,128)(2,1)} %param.7) | copy-start | bytes 4718596
  82.7 26.8 %copy-start.7 = (bf16[512,512]{1,0:T(8,128)(2,1)S(1)}, bf16[512,512]{1,0:T(8,128)(2,1)}, u32[]{:S(2)}) copy-start(bf16[512,512]{1,0:T(8,128)(2,1)} %get-tuple-element.42.refs_4_.refs_0_) | copy-start | bytes 1572868
  82.7 17.2 %collective-permute-start.9 = (bf16[16,48,384]{2,1,0:T(8,128)(2,1)}, bf16[16,48,384]{2,1,0:T(8,128)(2,1)S(1)}, u32[]{:S(2)}, u32[]{:S(2)}) collective-permute-start(bf16[16,48,384]{2,1,0:T(8,128)(2,1)} %bitcast.30), channel_id=1, source_target_pairs={{0,2},{1,3},{2,0},{3,1},{4,6},{5,7},{6,4},{7,5},{8,10},{9,11},{10,... | collective-permute-start | bytes 1769480 | tf_op jit(solution)/shard_map/ppermute | solution.py:329
  103.3 4.8 %collective-permute-start.11 = (bf16[4,16,48,384]{3,2,1,0:T(8,128)(2,1)S(1)}, bf16[4,16,48,384]{3,2,1,0:T(8,128)(2,1)S(1)}, u32[]{:S(2)}, u32[]{:S(2)}) collective-permute-start(bf16[4,16,48,384]{3,2,1,0:T(8,128)(2,1)S(1)} %shard_map.114.refs_1_), channel_id=1, source_target_pairs={{0,8},{8,0},{1,9},{9,1},{2,10},{10,2},{3,11},{11,3},{4,12},{12,4},... | collective-permute-start | bytes 7077896 | tf_op jit(solution)/shard_map/ppermute | solution.py:337
  119.7 48.4 %all-to-all-start.2 = ((bf16[32,16,1536]{2,1,0:T(8,128)(2,1)}), bf16[32,16,1536]{2,1,0:T(8,128)(2,1)}, u32[]{:S(2)}, u32[]{:S(2)}) async-start(bf16[32,16,1536]{2,1,0:T(8,128)(2,1)} %bitcast.36), calls=%async_computation.2 | async-start | bytes 3145728 | tf_op jit(solution)/shard_map/all_to_all | solution.py:24
  127.3 1.2 collective-permute-start.12
  141.0 4.7 %collective-permute-start.13 = (bf16[768,1536]{1,0:T(8,128)(2,1)}, bf16[768,1536]{1,0:T(8,128)(2,1)S(1)}, u32[]{:S(2)}, u32[]{:S(2)}) collective-permute-start(bf16[768,1536]{1,0:T(8,128)(2,1)} %get-tuple-element.54), channel_id=1, source_target_pairs={{0,8},{8,0},{1,9},{9,1},{2,10},{10,2},{3,11},{11,3},{4,12},{12,4},... | collective-permute-start | bytes 7077896 | tf_op jit(solution)/shard_map/ppermute | solution.py:337
  150.7 16.6 %collective-permute-start.14 = (bf16[768,384]{1,0:T(8,128)(2,1)S(1)}, bf16[768,384]{1,0:T(8,128)(2,1)S(1)}, u32[]{:S(2)}, u32[]{:S(2)}) collective-permute-start(bf16[768,384]{1,0:T(8,128)(2,1)S(1)} %get-tuple-element.55), channel_id=1, source_target_pairs={{0,1},{1,2},{2,3},{3,0},{4,5},{5,6},{6,7},{7,4},{8,9},{9,10},{10,1... | collective-permute-start | bytes 1769480 | tf_op jit(solution)/shard_map/ppermute | solution.py:329
  152.0 16.1 %collective-permute-start.15 = (bf16[768,384]{1,0:T(8,128)(2,1)S(1)}, bf16[768,384]{1,0:T(8,128)(2,1)}, u32[]{:S(2)}, u32[]{:S(2)}) collective-permute-start(bf16[768,384]{1,0:T(8,128)(2,1)S(1)} %get-tuple-element.56), channel_id=1, source_target_pairs={{0,3},{1,0},{2,1},{3,2},{4,7},{5,4},{6,5},{7,6},{8,11},{9,8},{10,9... | collective-permute-start | bytes 1769480 | tf_op jit(solution)/shard_map/ppermute | solution.py:329
  172.3 49.1 %all-to-all-start.3 = ((bf16[32,16,1536]{2,1,0:T(8,128)(2,1)}), bf16[32,16,1536]{2,1,0:T(8,128)(2,1)}, u32[]{:S(2)}, u32[]{:S(2)}) async-start(bf16[32,16,1536]{2,1,0:T(8,128)(2,1)} %bitcast.33), calls=%async_computation.3 | async-start | bytes 3145728 | tf_op jit(solution)/shard_map/all_to_all | solution.py:24
  180.0 17.3 %collective-permute-start.16 = (bf16[768,384]{1,0:T(8,128)(2,1)}, bf16[768,384]{1,0:T(8,128)(2,1)}, u32[]{:S(2)}, u32[]{:S(2)}) collective-permute-start(bf16[768,384]{1,0:T(8,128)(2,1)} %copy-done.30), channel_id=1, source_target_pairs={{0,2},{1,3},{2,0},{3,1},{4,6},{5,7},{6,4},{7,5},{8,10},{9,11},{10,... | collective-permute-start | bytes 1769480 | tf_op jit(solution)/shard_map/ppermute | solution.py:329
  183.2 14.1 %copy-start.18 = (bf16[768,384]{1,0:T(8,128)(2,1)S(1)}, bf16[768,384]{1,0:T(8,128)(2,1)}, u32[]{:S(2)}) copy-start(bf16[768,384]{1,0:T(8,128)(2,1)} %copy-done.17) | copy-start | bytes 1769476
  183.2 14.1 %copy-start.34 = (bf16[768,384]{1,0:T(8,128)(2,1)S(1)}, bf16[768,384]{1,0:T(8,128)(2,1)}, u32[]{:S(2)}) copy-start(bf16[768,384]{1,0:T(8,128)(2,1)} %copy-done.33) | copy-start | bytes 1769476
  187.5 12.1 %copy-start.15 = (bf16[4,128,128]{2,1,0:T(8,128)(2,1)}, bf16[4,128,128]{2,1,0:T(8,128)(2,1)S(1)}, u32[]{:S(2)}) copy-start(bf16[4,128,128]{2,1,0:T(8,128)(2,1)S(1)} %shard_map.122.refs_5_.refs_3_) | copy-start | bytes 393220
  198.9 23.2 %copy-start.19 = (bf16[512,512]{1,0:T(8,128)(2,1)S(1)}, bf16[512,512]{1,0:T(8,128)(2,1)}, u32[]{:S(2)}) copy-start(bf16[512,512]{1,0:T(8,128)(2,1)} %get-tuple-element.48.refs_0_) | copy-start | bytes 1572868
  199.6 13.2 %collective-permute-start.19 = (bf16[192,384]{1,0:T(8,128)(2,1)}, bf16[192,384]{1,0:T(8,128)(2,1)S(1)}, u32[]{:S(2)}, u32[]{:S(2)}) collective-permute-start(bf16[192,384]{1,0:T(8,128)(2,1)} %get-tuple-element.79), channel_id=1, source_target_pairs={{0,192},{64,0},{128,64},{192,128},{1,193},{65,1},{129,65},{193,129... | collective-permute-start | bytes 442376 | tf_op jit(solution)/shard_map/ppermute | solution.py:329
  200.5 12.4 %collective-permute-start.18 = (bf16[192,384]{1,0:T(8,128)(2,1)}, bf16[192,384]{1,0:T(8,128)(2,1)S(1)}, u32[]{:S(2)}, u32[]{:S(2)}) collective-permute-start(bf16[192,384]{1,0:T(8,128)(2,1)} %get-tuple-element.80), channel_id=1, source_target_pairs={{0,128},{64,192},{128,0},{192,64},{1,129},{65,193},{129,1},{193,65... | collective-permute-start | bytes 442376 | tf_op jit(solution)/shard_map/ppermute | solution.py:329
  201.4 11.4 %collective-permute-start.17 = (bf16[192,384]{1,0:T(8,128)(2,1)S(1)}, bf16[192,384]{1,0:T(8,128)(2,1)S(1)}, u32[]{:S(2)}, u32[]{:S(2)}) collective-permute-start(bf16[192,384]{1,0:T(8,128)(2,1)S(1)} %get-tuple-element.78), channel_id=1, source_target_pairs={{0,64},{64,128},{128,192},{192,0},{1,65},{65,129},{129,193},{193,1... | collective-permute-start | bytes 442376 | tf_op jit(solution)/shard_map/ppermute | solution.py:329
  213.5 6.2 %collective-permute-start.20 = (bf16[48,384]{1,0:T(8,128)(2,1)S(1)}, bf16[48,384]{1,0:T(8,128)(2,1)S(1)}, u32[]{:S(2)}, u32[]{:S(2)}) collective-permute-start(bf16[48,384]{1,0:T(8,128)(2,1)S(1)} %get-tuple-element.84), channel_id=1, source_target_pairs={{0,16},{16,32},{32,48},{48,0},{1,17},{17,33},{33,49},{49,1},{2,18}... | collective-permute-start | bytes 110600 | tf_op jit(solution)/shard_map/ppermute | solution.py:329
  214.9 5.6 %collective-permute-start.21 = (bf16[48,384]{1,0:T(8,128)(2,1)S(1)}, bf16[48,384]{1,0:T(8,128)(2,1)S(1)}, u32[]{:S(2)}, u32[]{:S(2)}) collective-permute-start(bf16[48,384]{1,0:T(8,128)(2,1)S(1)} %get-tuple-element.83), channel_id=1, source_target_pairs={{0,32},{16,48},{32,0},{48,16},{1,33},{17,49},{33,1},{49,17},{2,34}... | collective-permute-start | bytes 110600 | tf_op jit(solution)/shard_map/ppermute | solution.py:329
  216.8 4.6 %collective-permute-start.22 = (bf16[48,384]{1,0:T(8,128)(2,1)S(1)}, bf16[48,384]{1,0:T(8,128)(2,1)S(1)}, u32[]{:S(2)}, u32[]{:S(2)}) collective-permute-start(bf16[48,384]{1,0:T(8,128)(2,1)S(1)} %get-tuple-element.82), channel_id=1, source_target_pairs={{0,48},{16,0},{32,16},{48,32},{1,49},{17,1},{33,17},{49,33},{2,50}... | collective-permute-start | bytes 110600 | tf_op jit(solution)/shard_map/ppermute | solution.py:329
  222.0 13.1 %copy-start.16 = (bf16[4,128,128]{2,1,0:T(8,128)(2,1)S(1)}, bf16[4,128,128]{2,1,0:T(8,128)(2,1)}, u32[]{:S(2)}) copy-start(bf16[4,128,128]{2,1,0:T(8,128)(2,1)} %copy-done.15) | copy-start | bytes 393220
  226.8 21.6 %all-to-all-start.4 = ((bf16[32,4,1536]{2,1,0:T(4,128)(2,1)}), bf16[32,4,1536]{2,1,0:T(4,128)(2,1)}, u32[]{:S(2)}, u32[]{:S(2)}) async-start(bf16[32,4,1536]{2,1,0:T(4,128)(2,1)} %get-tuple-element.66), calls=%async_computation.4 | async-start | bytes 786432 | tf_op jit(solution)/shard_map/all_to_all | solution.py:480
  235.1 29.2 %copy-start.2 = (f32[512,1536]{1,0:T(8,128)S(1)}, f32[512,1536]{1,0:T(8,128)}, u32[]{:S(2)}) copy-start(f32[512,1536]{1,0:T(8,128)} %copy-done.1) | copy-start | bytes 9437188
  240.2 24.2 %copy-start.29 = (f32[3,1536]{1,0:T(4,128)S(1)}, f32[3,1536]{1,0:T(4,128)}, u32[]{:S(2)}) copy-start(f32[3,1536]{1,0:T(4,128)} %refs_2_.1) | copy-start | bytes 55300
  240.2 6.2 %collective-permute-start.23 = (bf16[256,128]{1,0:T(8,128)(2,1)}, bf16[256,128]{1,0:T(8,128)(2,1)S(1)}, u32[]{:S(2)}, u32[]{:S(2)}) collective-permute-start(bf16[256,128]{1,0:T(8,128)(2,1)} %get-tuple-element.69), channel_id=1, source_target_pairs={{0,1},{1,2},{2,3},{3,0},{4,5},{5,6},{6,7},{7,4},{8,9},{9,10},{10,1... | collective-permute-start | bytes 196616 | tf_op jit(solution)/shard_map/ppermute | solution.py:329
  240.6 7.0 %collective-permute-start.24 = (bf16[256,128]{1,0:T(8,128)(2,1)}, bf16[256,128]{1,0:T(8,128)(2,1)S(1)}, u32[]{:S(2)}, u32[]{:S(2)}) collective-permute-start(bf16[256,128]{1,0:T(8,128)(2,1)} %get-tuple-element.70), channel_id=1, source_target_pairs={{0,2},{1,3},{2,0},{3,1},{4,6},{5,7},{6,4},{7,5},{8,10},{9,11},{10,... | collective-permute-start | bytes 196616 | tf_op jit(solution)/shard_map/ppermute | solution.py:329
  243.9 4.5 %collective-permute-start.25 = (bf16[256,128]{1,0:T(8,128)(2,1)}, bf16[256,128]{1,0:T(8,128)(2,1)S(1)}, u32[]{:S(2)}, u32[]{:S(2)}) collective-permute-start(bf16[256,128]{1,0:T(8,128)(2,1)} %get-tuple-element.71), channel_id=1, source_target_pairs={{0,3},{1,0},{2,1},{3,2},{4,7},{5,4},{6,5},{7,6},{8,11},{9,8},{10,9... | collective-permute-start | bytes 196616 | tf_op jit(solution)/shard_map/ppermute | solution.py:329
  250.4 8.9 %collective-permute-start.26 = (bf16[496,128]{1,0:T(8,128)(2,1)S(1)}, bf16[496,128]{1,0:T(8,128)(2,1)S(1)}, u32[]{:S(2)}, u32[]{:S(2)}) collective-permute-start(bf16[496,128]{1,0:T(8,128)(2,1)S(1)} %shard_map.126.refs_0_), channel_id=1, source_target_pairs={{0,4},{4,0},{1,5},{5,1},{2,6},{6,2},{3,7},{7,3},{8,12},{12,8},{9,1... | collective-permute-start | bytes 380936 | tf_op jit(solution)/shard_map/ppermute | solution.py:337
  260.2 12.2 %all-to-all-start.5 = ((bf16[4,496,128]{2,1,0:T(8,128)(2,1)}), bf16[4,496,128]{2,1,0:T(8,128)(2,1)}, u32[]{:S(2)}, u32[]{:S(2)}) async-start(bf16[4,496,128]{2,1,0:T(8,128)(2,1)} %shard_map.127), calls=%async_computation.5 | async-start | bytes 1015808 | tf_op jit(solution)/shard_map/all_to_all | solution.py:509
  (27 other events, 37.8 us)

commit v4 on v3

--- a/solution.py
+++ b/solution.py
@@ -207,7 +207,9 @@
     )(mine, other)
 
 
-def backward_kernel(mix_ref, delta_ref, tok_ref, before_ref, after_ref, out_ref, spread_ref):
+def backward_kernel(
+    mix_ref, delta_ref, tok_ref, before_ref, after_ref, order_ref, conv_ref, second_ref, out_ref, spread_ref, *refs
+):
     d_conv = matmul(mix_ref[...], delta_ref[...]).astype(BF16)
     out_ref[...] = d_conv
     d_wide = d_conv.astype(F32)
@@ -222,6 +224,7 @@
     edge = jnp.where(target == here - 1, d_wide[:1][None], edge)
     sums = jnp.concatenate([*sums, jnp.zeros((1, step), F32)], axis=0)
     spread_ref[...] = jnp.where(line == lines - 1, edge, sums[None]).astype(BF16)
+    first_kernel(order_ref, delta_ref, conv_ref, second_ref, *refs)
 
 
 def tokens_kernel(d_conv_ref, spread_ref, taps_ref, gate_ref, out_ref):
@@ -469,25 +472,17 @@
     pieces = send_pieces(cut(add_up(arrived), "x", 0), "x")
     pieces = send_pieces(cut(add_up(pieces), "z_lo", 0), "z_lo")
 
-    d_conv, spread = on_device(
+    d_conv, spread, *factors = on_device(
         backward_kernel,
-        [lead_back, d_first, features, tok_before, tok_after],
-        [wide, like((owners, conv_weight.shape[0] + 1, width))],
-        needs=[grad_second, *pieces[1:]],
-        kept=[0, 1],
+        [lead_back, d_first, features, tok_before, tok_after, to_position, conv_in, grad_second],
+        [wide, like((owners, conv_weight.shape[0] + 1, width))] + [like((2 * size, size))] * y_count,
+        scratch=[pltpu.VMEM((blocks, size, size), F32)],
+        needs=pieces[1:],
+        kept=range(2 + y_count),
+        stay=[0, 1, 2, 5, 6, 7],
         step=512,
     )
     spread = lax.all_to_all(spread, SEQ, split_axis=0, concat_axis=0, tiled=True)
-    *factors, = on_device(
-        first_kernel,
-        [to_position, d_first, conv_in, grad_second],
-        [like((2 * size, size))] * y_count,
-        scratch=[pltpu.VMEM((blocks, size, size), F32)],
-        needs=[d_conv],
-        kept=range(y_count),
-        stay=[0, 1, 2],
-        step=512,
-    )
     parts = [
         *pieces,
         *send_pieces(factors, "y"),

time: 279 us -> 280 us (level)
  waiting for transfers between devices: 90.7 us -> 99 us
  local copies, waits for them, and re-layouts: 21.4 us -> 18.2 us
    ppermute x4, waiting for transfers between devices: 13.6 us -> 17.1 us  [swap(): return lax.ppermute(values, axis, [(0, 1), (1, 0)])]
    all_to_all x1, waiting for transfers between devices: 0.01 us -> 3.45 us  [shards(): lax.all_to_all(spread, SEQ, split_axis=0, concat_axis=0, tiled=True)]
    unnamed x84 -> x74, local copies, waits for them, and re-layouts: 18.5 us -> 16.1 us
    pallas_call x18 -> x17, Pallas kernels: 57 us -> 54.6 us  [on_device(): pl.pallas_call(body, grid=(width // step if step else 1,), in_specs=[spec...]
  transfers between devices with their start and end apart: 33 -> 33, of which waited for: 20 -> 22; matrix products, arithmetic and copies ran while one was open for 2% -> 1% of each run, Pallas kernels for 16% -> 14%
where the time goes in v4:
time: 280 us; the launch traced here: 277 us
  waiting for transfers between devices  99 us (35%)
  starting transfers between devices  95.2 us (34%)
  Pallas kernels  62.2 us (22%)
  local copies, waits for them, and re-layouts  18.2 us (6%)
    ppermute x21, waiting for transfers between devices, shift(): lax.ppermute(values, axis, [(i, (i + step) % count) for i in range(count)])  73.5 us
    pallas_call x17, Pallas kernels, on_device(): pl.pallas_call(body, grid=(width // step if step else 1,), in_specs=[spec...  54.6 us
    ppermute x21, starting transfers between devices, shift(): lax.ppermute(values, axis, [(i, (i + step) % count) for i in range(count)])  34.8 us
    all_to_all x4, starting transfers between devices, exchange(): lax.all_to_all(cut, SEQ, split_axis=0, concat_axis=0, tiled=True)  32.6 us
    ppermute x4, waiting for transfers between devices, swap(): return lax.ppermute(values, axis, [(0, 1), (1, 0)])  17.1 us
    unnamed x74, local copies, waits for them, and re-layouts  16.1 us
    all_to_all x1, starting transfers between devices, shards(): lax.all_to_all(spread, SEQ, split_axis=0, concat_axis=0, tiled=True)  9.3 us
    ppermute x1, starting transfers between devices, halo_rows(): after = lax.ppermute(first, SEQ, down)  6.34 us
  transfers between devices with their start and end apart: 33, of which 22 were waited for; matrix products, arithmetic and copies ran while one was open for 1% of the time, Pallas kernels for 14%

profile of v4, /device:TPU:6, one launch (start us, length us, event | category | flops | bytes accessed | tf_op | source)
XLA Modules:
  0.0 277.2 jit_solution(4910047825170808033)
XLA Ops:
  1.6 1.9 collective-permute-start.2
  3.5 3.3 %collective-permute-start.3 = (bf16[48,384]{1,0:T(8,128)(2,1)S(1)}, bf16[48,384]{1,0:T(8,128)(2,1)S(1)}, u32[]{:S(2)}, u32[]{:S(2)}) collective-permute-start(bf16[48,384]{1,0:T(8,128)(2,1)S(1)} %constant_dynamic-slice_fusion.refs_5_.refs_0_), channel_id=1, source_target_pairs={{0,32},{16,48},{32,0},{48,16},{1,33},{17,49},{33,1},{49,17},{2,34}... | collective-permute-start | bytes 110600 | tf_op jit(solution)/shard_map/ppermute | solution.py:332
  8.5 1.9 collective-permute-start
  10.5 6.3 %collective-permute-start.1 = (bf16[1,1536]{1,0:T(2,128)(2,1)S(1)}, bf16[1,1536]{1,0:T(2,128)(2,1)S(1)}, u32[]{:S(2)}, u32[]{:S(2)}) collective-permute-start(bf16[1,1536]{1,0:T(2,128)(2,1)S(1)} %get-tuple-element.76), channel_id=1, source_target_pairs={{8,0},{16,8},{24,16},{32,24},{40,32},{48,40},{56,48},{64,56},{72,6... | collective-permute-start | bytes 9224 | tf_op jit(solution)/shard_map/ppermute | solution.py:348
  18.9 4.4 %shard_map.110 = (bf16[512,1536]{1,0:T(8,128)(2,1)}, bf16[512,1536]{1,0:T(8,128)(2,1)}) custom-call(bf16[512,1536]{1,0:T(8,128)(2,1)} %bitcast.20, bf16[1,1536]{1,0:T(2,128)(2,1)S(1)} %collective-permute-done.refs_1_.refs_3_, bf16[1,1536]{1,0:T(2,128)(2,1)S(1)} %collective-permute-done.1.refs_2_.refs_4_, f32[3,1536]{1,0:T(4,128)} %refs_2_.1, ...), custom_call_target="tpu_custom_call" | custom-call | flops 1000 | bytes 1000 | tf_op jit(solution)/shard_map/pallas_call | solution.py:54
  23.4 8.6 %all-to-all-start = ((bf16[32,16,1536]{2,1,0:T(8,128)(2,1)}), bf16[32,16,1536]{2,1,0:T(8,128)(2,1)S(1)}, u32[]{:S(2)}, u32[]{:S(2)}) async-start(bf16[32,16,1536]{2,1,0:T(8,128)(2,1)} %bitcast.34), calls=%async_computation | async-start | bytes 3145728 | tf_op jit(solution)/shard_map/all_to_all | solution.py:24
  32.3 2.7 collective-permute-start.6
  35.0 13.6 %collective-permute-done.5.refs_1_ = bf16[4,48,384]{2,1,0:T(8,128)(2,1)S(1)} collective-permute-done((bf16[4,48,384]{2,1,0:T(8,128)(2,1)S(1)}, bf16[4,48,384]{2,1,0:T(8,128)(2,1)S(1)}, u32[]{:S(2)}, u32[]{:S(2)}) %collective-permute-start.5) | collective-permute-done | bytes 147488 | tf_op jit(solution)/shard_map/ppermute | solution.py:332
  49.7 2.4 collective-permute-done.7.refs_3_
  52.1 1.6 collective-permute-start.8
  53.8 1.7 collective-permute-start.10
  55.4 3.5 %shard_map.111 = (bf16[512,512]{1,0:T(8,128)(2,1)}, bf16[512,512]{1,0:T(8,128)(2,1)}, bf16[512,512]{1,0:T(8,128)(2,1)}, bf16[512,512]{1,0:T(8,128)(2,1)}, bf16[512,512]{1,0:T(8,128)(2,1)}) custom-call(bf16[4,128,128]{2,1,0:T(8,128)(2,1)} %refs_0_.3, bf16[4,128,128]{2,1,0:T(8,128)(2,1)} %refs_1_.1, bf16[512,1536]{1,0:T(8,128)(2,1)} %get-tuple-element.41.refs_2_), custom_call_target="tpu_custom_call" | custom-call | flops 1000 | bytes 1000 | tf_op jit(solution)/shard_map/pallas_call | solution.py:54
  58.9 9.9 %collective-permute-done.8.refs_1_.refs_2_ = bf16[16,48,384]{2,1,0:T(8,128)(2,1)S(1)} collective-permute-done((bf16[16,48,384]{2,1,0:T(8,128)(2,1)S(1)}, bf16[16,48,384]{2,1,0:T(8,128)(2,1)S(1)}, u32[]{:S(2)}, u32[]{:S(2)}) %collective-permute-start.8) | collective-permute-done | bytes 589856 | tf_op jit(solution)/shard_map/ppermute | solution.py:332
  69.9 3.6 %shard_map.115.refs_5_ = bf16[512,1536]{1,0:T(8,128)(2,1)} custom-call(bf16[512,512]{1,0:T(8,128)(2,1)} %get-tuple-element.43.refs_0_, bf16[512,1536]{1,0:T(8,128)(2,1)S(1)} %bitcast.24, bf16[16,48,384]{2,1,0:T(8,128)(2,1)} %copy-done.8, bf16[16,48,384]{2,1,0:T(8,128)(2,1)} %copy-done.10), custom_call_target="tpu_custom_call" | custom-call | flops 1000 | bytes 1000 | tf_op jit(solution)/shard_map/pallas_call | solution.py:54
  73.4 9.3 %all-to-all-start.1 = ((bf16[32,16,1536]{2,1,0:T(8,128)(2,1)}), bf16[32,16,1536]{2,1,0:T(8,128)(2,1)}, u32[]{:S(2)}, u32[]{:S(2)}) async-start(bf16[32,16,1536]{2,1,0:T(8,128)(2,1)} %bitcast.32), calls=%async_computation.1 | async-start | bytes 3145728 | tf_op jit(solution)/shard_map/all_to_all | solution.py:24
  82.8 2.8 %collective-permute-start.9 = (bf16[16,48,384]{2,1,0:T(8,128)(2,1)}, bf16[16,48,384]{2,1,0:T(8,128)(2,1)S(1)}, u32[]{:S(2)}, u32[]{:S(2)}) collective-permute-start(bf16[16,48,384]{2,1,0:T(8,128)(2,1)} %bitcast.30), channel_id=1, source_target_pairs={{0,2},{1,3},{2,0},{3,1},{4,6},{5,7},{6,4},{7,5},{8,10},{9,11},{10,... | collective-permute-start | bytes 1769480 | tf_op jit(solution)/shard_map/ppermute | solution.py:332
  85.5 14.4 %collective-permute-done.9.refs_2_ = bf16[16,48,384]{2,1,0:T(8,128)(2,1)S(1)} collective-permute-done((bf16[16,48,384]{2,1,0:T(8,128)(2,1)}, bf16[16,48,384]{2,1,0:T(8,128)(2,1)S(1)}, u32[]{:S(2)}, u32[]{:S(2)}) %collective-permute-start.9) | collective-permute-done | bytes 589856 | tf_op jit(solution)/shard_map/ppermute | solution.py:332
  103.6 4.5 %collective-permute-done.11.refs_2_ = bf16[4,16,48,384]{3,2,1,0:T(8,128)(2,1)S(1)} collective-permute-done((bf16[4,16,48,384]{3,2,1,0:T(8,128)(2,1)S(1)}, bf16[4,16,48,384]{3,2,1,0:T(8,128)(2,1)S(1)}, u32[]{:S(2)}, u32[]{:S(2)}) %collective-permute-start.11) | collective-permute-done | bytes 2359328 | tf_op jit(solution)/shard_map/ppermute | solution.py:340
  109.6 8.2 %shard_map.116 = (bf16[16,2,48,1536]{3,2,1,0:T(8,128)(2,1)}, f32[512,1536]{1,0:T(8,128)}, bf16[512,1536]{1,0:T(8,128)(2,1)}) custom-call(bf16[512,1536]{1,0:T(8,128)(2,1)S(1)} %bitcast.22, bf16[4,16,48,384]{3,2,1,0:T(8,128)(2,1)S(1)} %shard_map.114.refs_1_, bf16[4,16,48,384]{3,2,1,0:T(8,128)(2,1)} %copy-done.26, bf16[512,1536]{1,0:T(8,128)(2,1)S(1)} %bitcast.26, ...), custom_call_target="tpu_custom_call" | custom-call | flops 1000 | bytes 1000 | tf_op jit(solution)/shard_map/pallas_call | solution.py:54
  117.7 2.0 all-to-all-done.1
  119.7 6.9 %all-to-all-start.2 = ((bf16[32,16,1536]{2,1,0:T(8,128)(2,1)}), bf16[32,16,1536]{2,1,0:T(8,128)(2,1)}, u32[]{:S(2)}, u32[]{:S(2)}) async-start(bf16[32,16,1536]{2,1,0:T(8,128)(2,1)} %bitcast.36), calls=%async_computation.2 | async-start | bytes 3145728 | tf_op jit(solution)/shard_map/all_to_all | solution.py:24
  131.5 4.9 %shard_map.117 = (bf16[512,1536]{1,0:T(8,128)(2,1)}, bf16[512,1536]{1,0:T(8,128)(2,1)S(1)}) custom-call(bf16[512,512]{1,0:T(8,128)(2,1)S(1)} %copy-done.7, bf16[512,1536]{1,0:T(8,128)(2,1)} %bitcast.8.refs_1_, f32[512,1536]{1,0:T(8,128)} %get-tuple-element.46.refs_2_, bf16[512,1536]{1,0:T(8,128)(2,1)S(1)} %bitcast.27, bf16[16,128]{1,0:T(8,128)(2,1)} %copy-done.36), custom_call_target="tpu_custom_call" | custom-call | flops 1000 | bytes 1000 | tf_op jit(solution)/shard_map/pallas_call | solution.py:54
  136.4 4.6 %shard_map.119 = (bf16[768,1536]{1,0:T(8,128)(2,1)S(1)}, bf16[768,1536]{1,0:T(8,128)(2,1)}) custom-call(bf16[512,1536]{1,0:T(8,128)(2,1)S(1)} %bitcast.23, bf16[512,1536]{1,0:T(8,128)(2,1)S(1)} %get-tuple-element.51.left_ref.refs_1_), custom_call_target="tpu_custom_call" | custom-call | flops 1000 | bytes 1000 | tf_op jit(solution)/shard_map/pallas_call | solution.py:54
  141.1 4.6 %collective-permute-done.13.other_ref = bf16[768,1536]{1,0:T(8,128)(2,1)S(1)} collective-permute-done((bf16[768,1536]{1,0:T(8,128)(2,1)}, bf16[768,1536]{1,0:T(8,128)(2,1)S(1)}, u32[]{:S(2)}, u32[]{:S(2)}) %collective-permute-start.13) | collective-permute-done | bytes 2359328 | tf_op jit(solution)/shard_map/ppermute | solution.py:340
  147.1 2.7 shard_map.120
  151.3 1.9 collective-permute-start.15
  153.1 5.0 %shard_map.118.refs_2_.refs_3_ = f32[512,1536]{1,0:T(8,128)S(1)} custom-call(bf16[512,1536]{1,0:T(8,128)(2,1)S(1)} %get-tuple-element.51.left_ref.refs_1_, bf16[1536,1536]{1,0:T(8,128)(2,1)} %bitcast.35), custom_call_target="tpu_custom_call" | custom-call | flops 1000 | bytes 1000 | tf_op jit(solution)/shard_map/pallas_call | solution.py:154
  158.1 1.6 copy-done.1
  159.7 6.8 %collective-permute-done.14.refs_3_ = bf16[768,384]{1,0:T(8,128)(2,1)S(1)} collective-permute-done((bf16[768,384]{1,0:T(8,128)(2,1)S(1)}, bf16[768,384]{1,0:T(8,128)(2,1)S(1)}, u32[]{:S(2)}, u32[]{:S(2)}) %collective-permute-start.14) | collective-permute-done | bytes 589856 | tf_op jit(solution)/shard_map/ppermute | solution.py:332
  167.3 4.2 %shard_map.121.refs_3_ = bf16[512,1536]{1,0:T(8,128)(2,1)} custom-call(bf16[512,512]{1,0:T(8,128)(2,1)} %get-tuple-element.49.refs_0_, bf16[512,1536]{1,0:T(8,128)(2,1)} %bitcast.11.refs_1_, f32[512,1536]{1,0:T(8,128)} %copy-done.1, bf16[768,384]{1,0:T(8,128)(2,1)} %copy-done.28, bf16[768,384]{1,0:T(8,128)(2,1)} %collective-permute-done.15.refs_4_), custom_call_target="tpu_custom_call" | custom-call | flops 1000 | bytes 1000 | tf_op jit(solution)/shard_map/pallas_call | solution.py:54
  171.5 7.9 %all-to-all-start.3 = ((bf16[32,16,1536]{2,1,0:T(8,128)(2,1)}), bf16[32,16,1536]{2,1,0:T(8,128)(2,1)}, u32[]{:S(2)}, u32[]{:S(2)}) async-start(bf16[32,16,1536]{2,1,0:T(8,128)(2,1)} %bitcast.33), calls=%async_computation.3 | async-start | bytes 3145728 | tf_op jit(solution)/shard_map/all_to_all | solution.py:24
  179.4 2.2 collective-permute-start.16
  181.6 4.2 %shard_map.122.refs_7_ = bf16[4,128,128]{2,1,0:T(8,128)(2,1)S(1)} custom-call(bf16[512,512]{1,0:T(8,128)(2,1)S(1)} %copy-done.15, bf16[512,1536]{1,0:T(8,128)(2,1)} %bitcast.11.refs_1_, bf16[512,1536]{1,0:T(8,128)(2,1)S(1)} %bitcast.25, bf16[512,1536]{1,0:T(8,128)(2,1)} %shard_map.121.refs_3_), custom_call_target="tpu_custom_call" | custom-call | flops 1000 | bytes 1000 | tf_op jit(solution)/shard_map/pallas_call | solution.py:54
  185.8 10.6 %collective-permute-done.16 = bf16[768,384]{1,0:T(8,128)(2,1)} collective-permute-done((bf16[768,384]{1,0:T(8,128)(2,1)S(1)}, bf16[768,384]{1,0:T(8,128)(2,1)}, u32[]{:S(2)}, u32[]{:S(2)}) %collective-permute-start.16) | collective-permute-done | bytes 589856 | tf_op jit(solution)/shard_map/ppermute | solution.py:332
  200.0 2.3 collective-permute-start.17
  202.2 9.4 %collective-permute-done.19 = bf16[192,384]{1,0:T(8,128)(2,1)S(1)} collective-permute-done((bf16[192,384]{1,0:T(8,128)(2,1)S(1)}, bf16[192,384]{1,0:T(8,128)(2,1)S(1)}, u32[]{:S(2)}, u32[]{:S(2)}) %collective-permute-start.19) | collective-permute-done | bytes 147488 | tf_op jit(solution)/shard_map/ppermute | solution.py:332
  212.4 1.7 collective-permute-start.20
  215.3 2.3 collective-permute-start.22
  219.9 7.3 %shard_map.123 = (bf16[512,1536]{1,0:T(8,128)(2,1)}, bf16[32,4,1536]{2,1,0:T(4,128)(2,1)}, bf16[256,128]{1,0:T(8,128)(2,1)}, bf16[256,128]{1,0:T(8,128)(2,1)}, b...) custom-call(bf16[512,512]{1,0:T(8,128)(2,1)} %get-tuple-element.48.refs_0_, bf16[512,1536]{1,0:T(8,128)(2,1)} %bitcast.14.refs_1_, ...), custom_call_target="tpu_custom_call" | custom-call | flops 1000 | bytes 1000 | tf_op jit(solution)/shard_map/pallas_call | solution.py:54
  227.3 9.3 %all-to-all-start.4 = ((bf16[32,4,1536]{2,1,0:T(4,128)(2,1)}), bf16[32,4,1536]{2,1,0:T(4,128)(2,1)}, u32[]{:S(2)}, u32[]{:S(2)}) async-start(bf16[32,4,1536]{2,1,0:T(4,128)(2,1)} %get-tuple-element.67), calls=%async_computation.4 | async-start | bytes 786432 | tf_op jit(solution)/shard_map/all_to_all | solution.py:485
  237.1 3.3 %collective-permute-start.24 = (bf16[256,128]{1,0:T(8,128)(2,1)}, bf16[256,128]{1,0:T(8,128)(2,1)S(1)}, u32[]{:S(2)}, u32[]{:S(2)}) collective-permute-start(bf16[256,128]{1,0:T(8,128)(2,1)} %get-tuple-element.70), channel_id=1, source_target_pairs={{0,2},{1,3},{2,0},{3,1},{4,6},{5,7},{6,4},{7,5},{8,10},{9,11},{10,... | collective-permute-start | bytes 196616 | tf_op jit(solution)/shard_map/ppermute | solution.py:332
  244.9 3.4 %all-to-all-done.4.refs_1_.refs_8_ = bf16[32,4,1536]{2,1,0:T(4,128)(2,1)} async-done(((bf16[32,4,1536]{2,1,0:T(4,128)(2,1)}), bf16[32,4,1536]{2,1,0:T(4,128)(2,1)}, u32[]{:S(2)}, u32[]{:S(2)}) %all-to-all-start.4) | async-done | bytes 393248 | tf_op jit(solution)/shard_map/all_to_all | solution.py:485
  249.8 5.5 %collective-permute-start.26 = (bf16[496,128]{1,0:T(8,128)(2,1)S(1)}, bf16[496,128]{1,0:T(8,128)(2,1)S(1)}, u32[]{:S(2)}, u32[]{:S(2)}) collective-permute-start(bf16[496,128]{1,0:T(8,128)(2,1)S(1)} %shard_map.125.refs_0_), channel_id=1, source_target_pairs={{0,4},{4,0},{1,5},{5,1},{2,6},{6,2},{3,7},{7,3},{8,12},{12,8},{9,1... | collective-permute-start | bytes 380936 | tf_op jit(solution)/shard_map/ppermute | solution.py:340
  255.2 7.0 %collective-permute-done.26.refs_1_ = bf16[496,128]{1,0:T(8,128)(2,1)S(1)} collective-permute-done((bf16[496,128]{1,0:T(8,128)(2,1)S(1)}, bf16[496,128]{1,0:T(8,128)(2,1)S(1)}, u32[]{:S(2)}, u32[]{:S(2)}) %collective-permute-start.26) | collective-permute-done | bytes 127008 | tf_op jit(solution)/shard_map/ppermute | solution.py:340
  263.1 4.2 %all-to-all-start.5 = ((bf16[4,496,128]{2,1,0:T(8,128)(2,1)}), bf16[4,496,128]{2,1,0:T(8,128)(2,1)}, u32[]{:S(2)}, u32[]{:S(2)}) async-start(bf16[4,496,128]{2,1,0:T(8,128)(2,1)} %shard_map.126), calls=%async_computation.5 | async-start | bytes 1015808 | tf_op jit(solution)/shard_map/all_to_all | solution.py:504
  268.6 3.8 %shard_map.124 = bf16[512,1536]{1,0:T(8,128)(2,1)} custom-call(bf16[512,1536]{1,0:T(8,128)(2,1)S(1)} %copy-done.14, bf16[32,4,1536]{2,1,0:T(4,128)(2,1)} %all-to-all-done.4.refs_1_.refs_8_, f32[3,1536]{1,0:T(4,128)S(1)} %copy-done.25, f32[512,1536]{1,0:T(8,128)S(1)} %copy-done.2), custom_call_target="tpu_custom_call" | custom-call | flops 1000 | bytes 1000 | tf_op jit(solution)/shard_map/pallas_call | solution.py:54
  272.4 2.9 %all-to-all-done.5.refs_0_ = bf16[4,496,128]{2,1,0:T(8,128)(2,1)} async-done(((bf16[4,496,128]{2,1,0:T(8,128)(2,1)}), bf16[4,496,128]{2,1,0:T(8,128)(2,1)}, u32[]{:S(2)}, u32[]{:S(2)}) %all-to-all-start.5) | async-done | bytes 507936 | tf_op jit(solution)/shard_map/all_to_all | solution.py:504
  275.3 1.9 shard_map.127
  (118 shorter events, 37.6 us)
Async XLA Ops:
  1.6 16.7 %copy-start.17 = (bf16[48,384]{1,0:T(8,128)(2,1)}, bf16[48,384]{1,0:T(8,128)(2,1)S(1)}, u32[]{:S(2)}) copy-start(bf16[48,384]{1,0:T(8,128)(2,1)S(1)} %constant_dynamic-slice_fusion.refs_5_.refs_0_) | copy-start | bytes 110596
  1.6 16.7 %collective-permute-start.2 = (bf16[48,384]{1,0:T(8,128)(2,1)S(1)}, bf16[48,384]{1,0:T(8,128)(2,1)S(1)}, u32[]{:S(2)}, u32[]{:S(2)}) collective-permute-start(bf16[48,384]{1,0:T(8,128)(2,1)S(1)} %constant_dynamic-slice_fusion.refs_5_.refs_0_), channel_id=1, source_target_pairs={{0,16},{16,32},{32,48},{48,0},{1,17},{17,33},{33,49},{49,1},{2,18}... | collective-permute-start | bytes 110600 | tf_op jit(solution)/shard_map/ppermute | solution.py:332
  3.5 14.8 %collective-permute-start.3 = (bf16[48,384]{1,0:T(8,128)(2,1)S(1)}, bf16[48,384]{1,0:T(8,128)(2,1)S(1)}, u32[]{:S(2)}, u32[]{:S(2)}) collective-permute-start(bf16[48,384]{1,0:T(8,128)(2,1)S(1)} %constant_dynamic-slice_fusion.refs_5_.refs_0_), channel_id=1, source_target_pairs={{0,32},{16,48},{32,0},{48,16},{1,33},{17,49},{33,1},{49,17},{2,34}... | collective-permute-start | bytes 110600 | tf_op jit(solution)/shard_map/ppermute | solution.py:332
  6.7 11.5 %collective-permute-start.4 = (bf16[48,384]{1,0:T(8,128)(2,1)S(1)}, bf16[48,384]{1,0:T(8,128)(2,1)S(1)}, u32[]{:S(2)}, u32[]{:S(2)}) collective-permute-start(bf16[48,384]{1,0:T(8,128)(2,1)S(1)} %constant_dynamic-slice_fusion.refs_5_.refs_0_), channel_id=1, source_target_pairs={{0,48},{16,0},{32,16},{48,32},{1,49},{17,1},{33,17},{49,33},{2,50}... | collective-permute-start | bytes 110600 | tf_op jit(solution)/shard_map/ppermute | solution.py:332
  8.5 9.7 %collective-permute-start = (bf16[1,1536]{1,0:T(2,128)(2,1)S(1)}, bf16[1,1536]{1,0:T(2,128)(2,1)S(1)}, u32[]{:S(2)}, u32[]{:S(2)}) collective-permute-start(bf16[1,1536]{1,0:T(2,128)(2,1)S(1)} %get-tuple-element.77), channel_id=1, source_target_pairs={{0,8},{8,16},{16,24},{24,32},{32,40},{40,48},{48,56},{56,64},{64,7... | collective-permute-start | bytes 9224 | tf_op jit(solution)/shard_map/ppermute | solution.py:347
  10.5 7.8 %collective-permute-start.1 = (bf16[1,1536]{1,0:T(2,128)(2,1)S(1)}, bf16[1,1536]{1,0:T(2,128)(2,1)S(1)}, u32[]{:S(2)}, u32[]{:S(2)}) collective-permute-start(bf16[1,1536]{1,0:T(2,128)(2,1)S(1)} %get-tuple-element.76), channel_id=1, source_target_pairs={{8,0},{16,8},{24,16},{32,24},{40,32},{48,40},{56,48},{64,56},{72,6... | collective-permute-start | bytes 9224 | tf_op jit(solution)/shard_map/ppermute | solution.py:348
  23.3 8.6 %copy-start.18 = (bf16[48,384]{1,0:T(8,128)(2,1)S(1)}, bf16[48,384]{1,0:T(8,128)(2,1)}, u32[]{:S(2)}) copy-start(bf16[48,384]{1,0:T(8,128)(2,1)} %copy-done.17) | copy-start | bytes 110596
  23.3 8.6 %copy-start.20 = (bf16[48,384]{1,0:T(8,128)(2,1)S(1)}, bf16[48,384]{1,0:T(8,128)(2,1)}, u32[]{:S(2)}) copy-start(bf16[48,384]{1,0:T(8,128)(2,1)} %copy-done.19) | copy-start | bytes 110596
  23.3 8.6 %copy-start.22 = (bf16[48,384]{1,0:T(8,128)(2,1)S(1)}, bf16[48,384]{1,0:T(8,128)(2,1)}, u32[]{:S(2)}) copy-start(bf16[48,384]{1,0:T(8,128)(2,1)} %copy-done.21) | copy-start | bytes 110596
  23.4 8.6 %copy-start.24 = (bf16[48,384]{1,0:T(8,128)(2,1)S(1)}, bf16[48,384]{1,0:T(8,128)(2,1)}, u32[]{:S(2)}) copy-start(bf16[48,384]{1,0:T(8,128)(2,1)} %copy-done.23) | copy-start | bytes 110596
  23.4 45.5 %all-to-all-start = ((bf16[32,16,1536]{2,1,0:T(8,128)(2,1)}), bf16[32,16,1536]{2,1,0:T(8,128)(2,1)S(1)}, u32[]{:S(2)}, u32[]{:S(2)}) async-start(bf16[32,16,1536]{2,1,0:T(8,128)(2,1)} %bitcast.34), calls=%async_computation | async-start | bytes 3145728 | tf_op jit(solution)/shard_map/all_to_all | solution.py:24
  32.0 16.5 %collective-permute-start.5 = (bf16[4,48,384]{2,1,0:T(8,128)(2,1)S(1)}, bf16[4,48,384]{2,1,0:T(8,128)(2,1)S(1)}, u32[]{:S(2)}, u32[]{:S(2)}) collective-permute-start(bf16[4,48,384]{2,1,0:T(8,128)(2,1)S(1)} %shard_map.112.refs_0_), channel_id=1, source_target_pairs={{0,64},{64,128},{128,192},{192,0},{1,65},{65,129},{129,193},{193,1... | collective-permute-start | bytes 442376 | tf_op jit(solution)/shard_map/ppermute | solution.py:332
  32.3 17.4 %collective-permute-start.6 = (bf16[4,48,384]{2,1,0:T(8,128)(2,1)S(1)}, bf16[4,48,384]{2,1,0:T(8,128)(2,1)S(1)}, u32[]{:S(2)}, u32[]{:S(2)}) collective-permute-start(bf16[4,48,384]{2,1,0:T(8,128)(2,1)S(1)} %shard_map.112.refs_0_), channel_id=1, source_target_pairs={{0,128},{64,192},{128,0},{192,64},{1,129},{65,193},{129,1},{193,65... | collective-permute-start | bytes 442376 | tf_op jit(solution)/shard_map/ppermute | solution.py:332
  35.0 17.1 %collective-permute-start.7 = (bf16[4,48,384]{2,1,0:T(8,128)(2,1)S(1)}, bf16[4,48,384]{2,1,0:T(8,128)(2,1)S(1)}, u32[]{:S(2)}, u32[]{:S(2)}) collective-permute-start(bf16[4,48,384]{2,1,0:T(8,128)(2,1)S(1)} %shard_map.112.refs_0_), channel_id=1, source_target_pairs={{0,192},{64,0},{128,64},{192,128},{1,193},{65,1},{129,65},{193,129... | collective-permute-start | bytes 442376 | tf_op jit(solution)/shard_map/ppermute | solution.py:332
  52.1 16.7 %copy-start.12 = (bf16[4,4,48,384]{3,2,1,0:T(8,128)(2,1)}, bf16[4,4,48,384]{3,2,1,0:T(8,128)(2,1)S(1)}, u32[]{:S(2)}) copy-start(bf16[4,4,48,384]{3,2,1,0:T(8,128)(2,1)S(1)} %shard_map.113) | copy-start | bytes 1769476
  52.1 16.7 %collective-permute-start.8 = (bf16[16,48,384]{2,1,0:T(8,128)(2,1)S(1)}, bf16[16,48,384]{2,1,0:T(8,128)(2,1)S(1)}, u32[]{:S(2)}, u32[]{:S(2)}) collective-permute-start(bf16[16,48,384]{2,1,0:T(8,128)(2,1)S(1)} %bitcast.28), channel_id=1, source_target_pairs={{0,1},{1,2},{2,3},{3,0},{4,5},{5,6},{6,7},{7,4},{8,9},{9,10},{10,1... | collective-permute-start | bytes 1769480 | tf_op jit(solution)/shard_map/ppermute | solution.py:332
  53.8 15.1 %collective-permute-start.10 = (bf16[16,48,384]{2,1,0:T(8,128)(2,1)S(1)}, bf16[16,48,384]{2,1,0:T(8,128)(2,1)S(1)}, u32[]{:S(2)}, u32[]{:S(2)}) collective-permute-start(bf16[16,48,384]{2,1,0:T(8,128)(2,1)S(1)} %bitcast.29), channel_id=1, source_target_pairs={{0,3},{1,0},{2,1},{3,2},{4,7},{5,4},{6,5},{7,6},{8,11},{9,8},{10,9... | collective-permute-start | bytes 1769480 | tf_op jit(solution)/shard_map/ppermute | solution.py:332
  73.4 46.3 %all-to-all-start.1 = ((bf16[32,16,1536]{2,1,0:T(8,128)(2,1)}), bf16[32,16,1536]{2,1,0:T(8,128)(2,1)}, u32[]{:S(2)}, u32[]{:S(2)}) async-start(bf16[32,16,1536]{2,1,0:T(8,128)(2,1)} %bitcast.32), calls=%async_computation.1 | async-start | bytes 3145728 | tf_op jit(solution)/shard_map/all_to_all | solution.py:24
  82.7 26.8 %copy-start.3 = (bf16[1,512,1536]{2,1,0:T(8,128)(2,1)S(1)}, bf16[1,512,1536]{2,1,0:T(8,128)(2,1)}, u32[]{:S(2)}) copy-start(bf16[1,512,1536]{2,1,0:T(8,128)(2,1)} %param.6) | copy-start | bytes 4718596
  82.7 26.8 %copy-start.4 = (bf16[1,512,1536]{2,1,0:T(8,128)(2,1)S(1)}, bf16[1,512,1536]{2,1,0:T(8,128)(2,1)}, u32[]{:S(2)}) copy-start(bf16[1,512,1536]{2,1,0:T(8,128)(2,1)} %param.7) | copy-start | bytes 4718596
  82.7 26.8 %copy-start.6 = (bf16[512,512]{1,0:T(8,128)(2,1)S(1)}, bf16[512,512]{1,0:T(8,128)(2,1)}, u32[]{:S(2)}) copy-start(bf16[512,512]{1,0:T(8,128)(2,1)} %get-tuple-element.42.refs_4_.refs_0_.refs_5_) | copy-start | bytes 1572868
  82.8 17.2 %collective-permute-start.9 = (bf16[16,48,384]{2,1,0:T(8,128)(2,1)}, bf16[16,48,384]{2,1,0:T(8,128)(2,1)S(1)}, u32[]{:S(2)}, u32[]{:S(2)}) collective-permute-start(bf16[16,48,384]{2,1,0:T(8,128)(2,1)} %bitcast.30), channel_id=1, source_target_pairs={{0,2},{1,3},{2,0},{3,1},{4,6},{5,7},{6,4},{7,5},{8,10},{9,11},{10,... | collective-permute-start | bytes 1769480 | tf_op jit(solution)/shard_map/ppermute | solution.py:332
  103.3 4.8 %collective-permute-start.11 = (bf16[4,16,48,384]{3,2,1,0:T(8,128)(2,1)S(1)}, bf16[4,16,48,384]{3,2,1,0:T(8,128)(2,1)S(1)}, u32[]{:S(2)}, u32[]{:S(2)}) collective-permute-start(bf16[4,16,48,384]{3,2,1,0:T(8,128)(2,1)S(1)} %shard_map.114.refs_1_), channel_id=1, source_target_pairs={{0,8},{8,0},{1,9},{9,1},{2,10},{10,2},{3,11},{11,3},{4,12},{12,4},... | collective-permute-start | bytes 7077896 | tf_op jit(solution)/shard_map/ppermute | solution.py:340
  119.7 46.8 %all-to-all-start.2 = ((bf16[32,16,1536]{2,1,0:T(8,128)(2,1)}), bf16[32,16,1536]{2,1,0:T(8,128)(2,1)}, u32[]{:S(2)}, u32[]{:S(2)}) async-start(bf16[32,16,1536]{2,1,0:T(8,128)(2,1)} %bitcast.36), calls=%async_computation.2 | async-start | bytes 3145728 | tf_op jit(solution)/shard_map/all_to_all | solution.py:24
  127.3 1.2 collective-permute-start.12
  141.0 4.7 %collective-permute-start.13 = (bf16[768,1536]{1,0:T(8,128)(2,1)}, bf16[768,1536]{1,0:T(8,128)(2,1)S(1)}, u32[]{:S(2)}, u32[]{:S(2)}) collective-permute-start(bf16[768,1536]{1,0:T(8,128)(2,1)} %get-tuple-element.54), channel_id=1, source_target_pairs={{0,8},{8,0},{1,9},{9,1},{2,10},{10,2},{3,11},{11,3},{4,12},{12,4},... | collective-permute-start | bytes 7077896 | tf_op jit(solution)/shard_map/ppermute | solution.py:340
  149.8 16.7 %collective-permute-start.14 = (bf16[768,384]{1,0:T(8,128)(2,1)S(1)}, bf16[768,384]{1,0:T(8,128)(2,1)S(1)}, u32[]{:S(2)}, u32[]{:S(2)}) collective-permute-start(bf16[768,384]{1,0:T(8,128)(2,1)S(1)} %get-tuple-element.55), channel_id=1, source_target_pairs={{0,1},{1,2},{2,3},{3,0},{4,5},{5,6},{6,7},{7,4},{8,9},{9,10},{10,1... | collective-permute-start | bytes 1769480 | tf_op jit(solution)/shard_map/ppermute | solution.py:332
  151.3 15.2 %collective-permute-start.15 = (bf16[768,384]{1,0:T(8,128)(2,1)S(1)}, bf16[768,384]{1,0:T(8,128)(2,1)}, u32[]{:S(2)}, u32[]{:S(2)}) collective-permute-start(bf16[768,384]{1,0:T(8,128)(2,1)S(1)} %get-tuple-element.56), channel_id=1, source_target_pairs={{0,3},{1,0},{2,1},{3,2},{4,7},{5,4},{6,5},{7,6},{8,11},{9,8},{10,9... | collective-permute-start | bytes 1769480 | tf_op jit(solution)/shard_map/ppermute | solution.py:332
  171.5 10.0 %copy-start.15 = (bf16[512,512]{1,0:T(8,128)(2,1)S(1)}, bf16[512,512]{1,0:T(8,128)(2,1)}, u32[]{:S(2)}) copy-start(bf16[512,512]{1,0:T(8,128)(2,1)} %get-tuple-element.58.refs_0_) | copy-start | bytes 1572868
  171.5 47.8 %all-to-all-start.3 = ((bf16[32,16,1536]{2,1,0:T(8,128)(2,1)}), bf16[32,16,1536]{2,1,0:T(8,128)(2,1)}, u32[]{:S(2)}, u32[]{:S(2)}) async-start(bf16[32,16,1536]{2,1,0:T(8,128)(2,1)} %bitcast.33), calls=%async_computation.3 | async-start | bytes 3145728 | tf_op jit(solution)/shard_map/all_to_all | solution.py:24
  179.4 17.1 %collective-permute-start.16 = (bf16[768,384]{1,0:T(8,128)(2,1)S(1)}, bf16[768,384]{1,0:T(8,128)(2,1)}, u32[]{:S(2)}, u32[]{:S(2)}) collective-permute-start(bf16[768,384]{1,0:T(8,128)(2,1)S(1)} %get-tuple-element.60), channel_id=1, source_target_pairs={{0,2},{1,3},{2,0},{3,1},{4,6},{5,7},{6,4},{7,5},{8,10},{9,11},{10,... | collective-permute-start | bytes 1769480 | tf_op jit(solution)/shard_map/ppermute | solution.py:332
  181.6 14.9 %copy-start.29 = (bf16[768,384]{1,0:T(8,128)(2,1)S(1)}, bf16[768,384]{1,0:T(8,128)(2,1)}, u32[]{:S(2)}) copy-start(bf16[768,384]{1,0:T(8,128)(2,1)} %copy-done.28) | copy-start | bytes 1769476
  185.8 12.3 %copy-start.16 = (bf16[4,128,128]{2,1,0:T(8,128)(2,1)}, bf16[4,128,128]{2,1,0:T(8,128)(2,1)S(1)}, u32[]{:S(2)}) copy-start(bf16[4,128,128]{2,1,0:T(8,128)(2,1)S(1)} %shard_map.122.refs_7_) | copy-start | bytes 393220
  198.1 13.6 %collective-permute-start.19 = (bf16[192,384]{1,0:T(8,128)(2,1)S(1)}, bf16[192,384]{1,0:T(8,128)(2,1)S(1)}, u32[]{:S(2)}, u32[]{:S(2)}) collective-permute-start(bf16[192,384]{1,0:T(8,128)(2,1)S(1)} %get-tuple-element.79), channel_id=1, source_target_pairs={{0,192},{64,0},{128,64},{192,128},{1,193},{65,1},{129,65},{193,129... | collective-permute-start | bytes 442376 | tf_op jit(solution)/shard_map/ppermute | solution.py:332
  199.0 12.7 %collective-permute-start.18 = (bf16[192,384]{1,0:T(8,128)(2,1)S(1)}, bf16[192,384]{1,0:T(8,128)(2,1)S(1)}, u32[]{:S(2)}, u32[]{:S(2)}) collective-permute-start(bf16[192,384]{1,0:T(8,128)(2,1)S(1)} %get-tuple-element.80), channel_id=1, source_target_pairs={{0,128},{64,192},{128,0},{192,64},{1,129},{65,193},{129,1},{193,65... | collective-permute-start | bytes 442376 | tf_op jit(solution)/shard_map/ppermute | solution.py:332
  200.0 11.7 %collective-permute-start.17 = (bf16[192,384]{1,0:T(8,128)(2,1)S(1)}, bf16[192,384]{1,0:T(8,128)(2,1)S(1)}, u32[]{:S(2)}, u32[]{:S(2)}) collective-permute-start(bf16[192,384]{1,0:T(8,128)(2,1)S(1)} %get-tuple-element.78), channel_id=1, source_target_pairs={{0,64},{64,128},{128,192},{192,0},{1,65},{65,129},{129,193},{193,1... | collective-permute-start | bytes 442376 | tf_op jit(solution)/shard_map/ppermute | solution.py:332
  212.4 6.1 %collective-permute-start.20 = (bf16[48,384]{1,0:T(8,128)(2,1)S(1)}, bf16[48,384]{1,0:T(8,128)(2,1)S(1)}, u32[]{:S(2)}, u32[]{:S(2)}) collective-permute-start(bf16[48,384]{1,0:T(8,128)(2,1)S(1)} %get-tuple-element.84), channel_id=1, source_target_pairs={{0,16},{16,32},{32,48},{48,0},{1,17},{17,33},{33,49},{49,1},{2,18}... | collective-permute-start | bytes 110600 | tf_op jit(solution)/shard_map/ppermute | solution.py:332
  214.0 4.9 %collective-permute-start.21 = (bf16[48,384]{1,0:T(8,128)(2,1)S(1)}, bf16[48,384]{1,0:T(8,128)(2,1)S(1)}, u32[]{:S(2)}, u32[]{:S(2)}) collective-permute-start(bf16[48,384]{1,0:T(8,128)(2,1)S(1)} %get-tuple-element.83), channel_id=1, source_target_pairs={{0,32},{16,48},{32,0},{48,16},{1,33},{17,49},{33,1},{49,17},{2,34}... | collective-permute-start | bytes 110600 | tf_op jit(solution)/shard_map/ppermute | solution.py:332
  215.3 4.0 %collective-permute-start.22 = (bf16[48,384]{1,0:T(8,128)(2,1)S(1)}, bf16[48,384]{1,0:T(8,128)(2,1)S(1)}, u32[]{:S(2)}, u32[]{:S(2)}) collective-permute-start(bf16[48,384]{1,0:T(8,128)(2,1)S(1)} %get-tuple-element.82), channel_id=1, source_target_pairs={{0,48},{16,0},{32,16},{48,32},{1,49},{17,1},{33,17},{49,33},{2,50}... | collective-permute-start | bytes 110600 | tf_op jit(solution)/shard_map/ppermute | solution.py:332
  227.3 40.0 %copy-start.2 = (f32[512,1536]{1,0:T(8,128)S(1)}, f32[512,1536]{1,0:T(8,128)}, u32[]{:S(2)}) copy-start(f32[512,1536]{1,0:T(8,128)} %copy-done.1) | copy-start | bytes 9437188
  227.3 40.0 %copy-start.25 = (f32[3,1536]{1,0:T(4,128)S(1)}, f32[3,1536]{1,0:T(4,128)}, u32[]{:S(2)}) copy-start(f32[3,1536]{1,0:T(4,128)} %refs_2_.1) | copy-start | bytes 55300
  227.3 21.0 %all-to-all-start.4 = ((bf16[32,4,1536]{2,1,0:T(4,128)(2,1)}), bf16[32,4,1536]{2,1,0:T(4,128)(2,1)}, u32[]{:S(2)}, u32[]{:S(2)}) async-start(bf16[32,4,1536]{2,1,0:T(4,128)(2,1)} %get-tuple-element.67), calls=%async_computation.4 | async-start | bytes 786432 | tf_op jit(solution)/shard_map/all_to_all | solution.py:485
  236.6 6.2 %collective-permute-start.23 = (bf16[256,128]{1,0:T(8,128)(2,1)}, bf16[256,128]{1,0:T(8,128)(2,1)S(1)}, u32[]{:S(2)}, u32[]{:S(2)}) collective-permute-start(bf16[256,128]{1,0:T(8,128)(2,1)} %get-tuple-element.69), channel_id=1, source_target_pairs={{0,1},{1,2},{2,3},{3,0},{4,5},{5,6},{6,7},{7,4},{8,9},{9,10},{10,1... | collective-permute-start | bytes 196616 | tf_op jit(solution)/shard_map/ppermute | solution.py:332
  237.1 7.0 %collective-permute-start.24 = (bf16[256,128]{1,0:T(8,128)(2,1)}, bf16[256,128]{1,0:T(8,128)(2,1)S(1)}, u32[]{:S(2)}, u32[]{:S(2)}) collective-permute-start(bf16[256,128]{1,0:T(8,128)(2,1)} %get-tuple-element.70), channel_id=1, source_target_pairs={{0,2},{1,3},{2,0},{3,1},{4,6},{5,7},{6,4},{7,5},{8,10},{9,11},{10,... | collective-permute-start | bytes 196616 | tf_op jit(solution)/shard_map/ppermute | solution.py:332
  240.4 4.5 %collective-permute-start.25 = (bf16[256,128]{1,0:T(8,128)(2,1)}, bf16[256,128]{1,0:T(8,128)(2,1)S(1)}, u32[]{:S(2)}, u32[]{:S(2)}) collective-permute-start(bf16[256,128]{1,0:T(8,128)(2,1)} %get-tuple-element.71), channel_id=1, source_target_pairs={{0,3},{1,0},{2,1},{3,2},{4,7},{5,4},{6,5},{7,6},{8,11},{9,8},{10,9... | collective-permute-start | bytes 196616 | tf_op jit(solution)/shard_map/ppermute | solution.py:332
  242.8 5.5 %copy-start.33 = (bf16[256,128]{1,0:T(8,128)(2,1)}, bf16[256,128]{1,0:T(8,128)(2,1)S(1)}, u32[]{:S(2)}) copy-start(bf16[256,128]{1,0:T(8,128)(2,1)S(1)} %collective-permute-done.23.refs_5_) | copy-start | bytes 196612
  249.8 12.5 %collective-permute-start.26 = (bf16[496,128]{1,0:T(8,128)(2,1)S(1)}, bf16[496,128]{1,0:T(8,128)(2,1)S(1)}, u32[]{:S(2)}, u32[]{:S(2)}) collective-permute-start(bf16[496,128]{1,0:T(8,128)(2,1)S(1)} %shard_map.125.refs_0_), channel_id=1, source_target_pairs={{0,4},{4,0},{1,5},{5,1},{2,6},{6,2},{3,7},{7,3},{8,12},{12,8},{9,1... | collective-permute-start | bytes 380936 | tf_op jit(solution)/shard_map/ppermute | solution.py:340
  263.1 12.2 %all-to-all-start.5 = ((bf16[4,496,128]{2,1,0:T(8,128)(2,1)}), bf16[4,496,128]{2,1,0:T(8,128)(2,1)}, u32[]{:S(2)}, u32[]{:S(2)}) async-start(bf16[4,496,128]{2,1,0:T(8,128)(2,1)} %shard_map.126), calls=%async_computation.5 | async-start | bytes 1015808 | tf_op jit(solution)/shard_map/all_to_all | solution.py:504
  (22 other events, 27.2 us)
